TPU v7x, 32 devices: a whole 2x2x4 slice. The times are simulated.
32 devices in a mesh: lat: 8 (over y, x, core), lon: 4 (over z).
Axes of the slice: x: 2, y: 2, z: 4, core: 2. Of those that a mesh axis runs over, the one named last changes fastest.
Arguments:
- obs_frac: float32 [8, 4, 2, 1024], P('lat', 'lon'), may hold values from 0 to 1
- obs_field: float32 [8, 4, 3, 1024], P('lat', 'lon'), may hold values from -6 to 6
- dipole_frac: float32 [8, 4, 2, 256], P('lat', 'lon'), may hold values from 0 to 1
- dipole_moment: float32 [8, 4, 256], P('lat', 'lon'), may hold values from -6 to 6
- obs_count: int32 [8, 4], P('lat', 'lon'), may hold values from 256 to 1024, as said below
Outputs:
- gram: float32 [8, 4, 13, 256, 256], P('lat', 'lon')
- rhs: float32 [8, 4, 256], P('lat', 'lon')
Inputs may be any that keep to these rules, and one draw needn't show every extreme that they name: `obs_count`: tiles of the first and of the last latitude row hold exactly 1024 observations; every other tile holds between 256 and 512.
All inputs are finite; a program needn't handle non-finite values.
Results may differ from a plain program's by a relative error of at most 0.0003.
Values sent between devices are 32-bit elements; how exact they have to be, the bound alone decides.
No kernel may reach another device: no remote copies, remote signals or barrier semaphores. Data moves between devices by JAX's collectives and lax.ppermute only.
A program may use at most 128 MiB of HBM per device.

v0:
```python
import math

import jax
import jax.numpy as jnp
from jax import lax
from jax.sharding import PartitionSpec as P

CROSS = ((0, 0), (-1, 0), (1, 0), (0, -1), (0, 1))
OFFSETS = (
    (0, 0),
    (-1, 0),
    (1, 0),
    (0, -1),
    (0, 1),
    (-2, 0),
    (2, 0),
    (0, -2),
    (0, 2),
    (-1, -1),
    (-1, 1),
    (1, -1),
    (1, 1),
)
OBS_RADIUS = 1.06
SOURCE_RADIUS = 0.99
KERNEL_SCALE = 0.0001
HUBER_EDGE = 0.8
DEGREE = math.pi / 180.0


def extended(cells, sides, width, closed):
    for axis, dim in sides:
        count = lax.axis_size(axis)
        ends = count if closed else count - 1
        head = lax.slice_in_dim(cells, 0, width, axis=dim)
        tail = lax.slice_in_dim(cells, cells.shape[dim] - width, cells.shape[dim], axis=dim)
        cells = jnp.concatenate(
            [
                lax.ppermute(tail, axis, [(i, (i + 1) % count) for i in range(ends)]),
                cells,
                lax.ppermute(head, axis, [((i + 1) % count, i) for i in range(ends)]),
            ],
            axis=dim,
        )
    return cells


def shifted(block, axis, distance):
    devices = range(lax.axis_size(axis))
    route = [(i - distance, i) for i in devices if i - distance in devices]
    return lax.ppermute(block, axis, route)


def passed_along(value, axis, steps):
    count = lax.axis_size(axis)
    pairs = [(source, (source + steps) % count) for source in range(count)]
    return lax.ppermute(value, axis, pairs)


def place(fraction, lat_index, lon_index, lat_tiles, lon_tiles, radius):
    lat_span = 160.0 * DEGREE / lat_tiles
    latitude = -80.0 * DEGREE + (lat_index + fraction[0]) * lat_span
    longitude = (lon_index + fraction[1]) * (2.0 * math.pi / lon_tiles)
    return radius * jnp.stack(
        [
            jnp.cos(latitude) * jnp.cos(longitude),
            jnp.cos(latitude) * jnp.sin(longitude),
            jnp.sin(latitude),
        ]
    )


def kernel(points, sources):
    separation = points[:, :, None] - sources[:, None, :]
    squared = jnp.sum(separation * separation, axis=0)
    aligned = jnp.sum(sources[:, None, :] * separation, axis=0)
    inverse_cube = squared ** (-1.5)
    return (
        KERNEL_SCALE * (3.0 * aligned / squared * separation - sources[:, None, :]) * inverse_cube
    )


def residual_terms(points, crossed, field, present):
    sources = jnp.concatenate([member[:3] for member in crossed], 1)
    moments = jnp.concatenate([member[3] for member in crossed], 0)
    coupling = kernel(points, sources)
    predicted = jnp.einsum("coj,j->co", coupling, moments, precision=lax.Precision.HIGHEST)
    residual = field - predicted
    weight = present * HUBER_EDGE / jnp.maximum(jnp.abs(residual), HUBER_EDGE)
    return (coupling, weight, weight * residual)


def shards(obs_frac, obs_field, dipole_frac, dipole_moment, obs_count):
    lat_tiles = lax.axis_size("lat")
    lon_tiles = lax.axis_size("lon")
    lat_index = lax.axis_index("lat")
    lon_index = lax.axis_index("lon")
    block_size = dipole_frac.shape[3]
    obs_slots = obs_frac.shape[3]
    source = place(dipole_frac[0, 0], lat_index, lon_index, lat_tiles, lon_tiles, SOURCE_RADIUS)
    packed = jnp.concatenate([source, dipole_moment[0, 0][None]], 0)[None, None]
    points = place(obs_frac[0, 0], lat_index, lon_index, lat_tiles, lon_tiles, OBS_RADIUS)
    present = (jnp.arange(obs_slots, dtype=jnp.int32) < obs_count[0, 0]).astype(jnp.float32)
    field = obs_field[0, 0]
    blocks = [jnp.zeros((block_size, block_size), jnp.float32) for offset in OFFSETS]
    rhs_total = jnp.zeros((block_size,), jnp.float32)
    lat_cycle = extended(packed, (("lat", 0),), 1, False)
    lon_cycle = extended(packed, (("lon", 1),), 1, True)
    crossed = [packed[0, 0], lat_cycle[0, 0], lat_cycle[2, 0], lon_cycle[0, 0], lon_cycle[0, 2]]
    coupling, weight, weighted_resid = residual_terms(points, crossed, field, present)
    coupling_low = coupling.astype(jnp.bfloat16)
    weighted_low = (weight[:, :, None] * coupling).astype(jnp.bfloat16)
    partial_value = jnp.einsum(
        "coi,coj->ij", weighted_low, coupling_low, preferred_element_type=jnp.float32
    )
    right_side = jnp.einsum("coi,co->i", coupling, weighted_resid, precision=lax.Precision.HIGHEST)
    row_blocks = [
        partial_value[first * block_size : (first + 1) * block_size] for first in range(5)
    ]
    right_parts = [right_side[first * block_size : (first + 1) * block_size] for first in range(5)]
    arrived = [
        (row_blocks[0], right_parts[0]),
        shifted((row_blocks[1], right_parts[1]), "lat", -1),
        shifted((row_blocks[2], right_parts[2]), "lat", 1),
        passed_along((row_blocks[3], right_parts[3]), "lon", -1),
        passed_along((row_blocks[4], right_parts[4]), "lon", 1),
    ]
    for first, (lat_step, lon_step) in enumerate(CROSS):
        member_rows, member_right = arrived[first]
        rhs_total = rhs_total + member_right
        for second, (lat_other, lon_other) in enumerate(CROSS):
            target = OFFSETS.index((lat_other - lat_step, lon_other - lon_step))
            blocks[target] = (
                blocks[target] + member_rows[:, second * block_size : (second + 1) * block_size]
            )
    gram = jnp.stack(blocks, 0)[None, None]
    return (gram, rhs_total[None, None])


def solution(mesh):
    in_specs = (
        P("lat", "lon", None, None),
        P("lat", "lon", None, None),
        P("lat", "lon", None, None),
        P("lat", "lon", None),
        P("lat", "lon"),
    )
    out_specs = (P("lat", "lon", None, None, None), P("lat", "lon", None))
    return jax.shard_map(shards, mesh=mesh, in_specs=in_specs, out_specs=out_specs, check_vma=False)
```

profile of v0, /device:TPU:4, one launch (start us, length us, event | category | flops | bytes accessed | tf_op | source)
XLA Modules:
  0.0 155.0 jit_solution(18207065878663406943)
XLA Ops:
  2.8 3.6 %collective-permute-start.3 = (f32[1,1,4,256]{3,2,1,0:T(4,128)S(1)}, f32[1,1,4,256]{3,2,1,0:T(4,128)S(1)}, u32[]{:S(2)}, u32[]{:S(2)}) collective-permute-start(f32[1,1,4,256]{3,2,1,0:T(4,128)S(1)} %maximum_bitcast_fusion), channel_id=1, source_target_pairs={{1,0},{2,1},{3,2},{0,3},{5,4},{6,5},{7,6},{4,7},{9,8},{10,9},{11,1... | collective-permute-start | bytes 12296 | tf_op jit(solution)/shard_map/ppermute | solution.py:41
  6.4 2.5 %collective-permute-start.1 = (f32[1,1,4,256]{3,2,1,0:T(4,128)S(1)}, f32[1,1,4,256]{3,2,1,0:T(4,128)S(1)}, u32[]{:S(2)}, u32[]{:S(2)}) collective-permute-start(f32[1,1,4,256]{3,2,1,0:T(4,128)S(1)} %maximum_bitcast_fusion), channel_id=1, source_target_pairs={{4,0},{8,4},{12,8},{16,12},{20,16},{24,20},{28,24},{5,1},{9,5},{13... | collective-permute-start | bytes 12296 | tf_op jit(solution)/shard_map/ppermute | solution.py:41
  8.9 1.9 %collective-permute-start = (f32[1,1,4,256]{3,2,1,0:T(4,128)S(1)}, f32[1,1,4,256]{3,2,1,0:T(4,128)S(1)}, u32[]{:S(2)}, u32[]{:S(2)}) collective-permute-start(f32[1,1,4,256]{3,2,1,0:T(4,128)S(1)} %maximum_bitcast_fusion), channel_id=1, source_target_pairs={{0,4},{4,8},{8,12},{12,16},{16,20},{20,24},{24,28},{1,5},{5,9},{9,... | collective-permute-start | bytes 12296 | tf_op jit(solution)/shard_map/ppermute | solution.py:39
  13.3 1.5 collective-permute-done
  15.0 7.8 %fusion = (f32[1024,1280]{0,1:T(8,128)}, f32[1024,1280]{0,1:T(8,128)}) fusion(f32[3,1024]{1,0:T(4,128)S(1)} %maximum_multiply_fusion, f32[3,1280]{1,0:T(4,128)S(1)} %constant_dynamic-update-slice_fusion), kind=kLoop, calls=%fused_computation.3 | loop fusion | flops 17039360 | bytes 10513408 | tf_op jit(solution)/shard_map/reduce_sum | solution.py:76
  22.7 6.3 %multiply_divide_fusion = (f32[1024,1280]{0,1:T(8,128)S(1)}, f32[1024,1280]{0,1:T(8,128)S(1)}) fusion(f32[1024,1280]{0,1:T(8,128)} %get-tuple-element.3, f32[1024,1280]{0,1:T(8,128)} %get-tuple-element.2), kind=kLoop, calls=%fused_computation.27 | loop fusion | flops 3932160 | bytes 20971520 | tf_op jit(solution)/shard_map/div | solution.py:79
  29.0 5.9 %fusion.67 = bf16[3,1024,1280]{1,2,0:T(8,128)(2,1)} fusion(f32[1024,1280]{0,1:T(8,128)S(1)} %get-tuple-element.11, f32[1024,1280]{0,1:T(8,128)S(1)} %get-tuple-element.10, f32[3,1024]{1,0:T(4,128)S(1)} %maximum_multiply_fusion, f32[3,1280]{1,0:T(4,128)S(1)} %constant_dynamic-update-slice_fusion), kind=kLoop, calls=%fused_computation.8.clone.clone.2 | loop fusion | flops 19660800 | bytes 18377728 | tf_op jit(solution)/shard_map/coi,coj->ij/dot_general | solution.py:113
  35.3 10.2 %fusion.8 = f32[1,3,1024]{2,0,1:T(1,128)S(1)} fusion(f32[1280,1,1]{0,1,2:T(1,128)S(1)} %reshape.216, f32[1024,1280]{0,1:T(8,128)S(1)} %get-tuple-element.11, f32[1024,1280]{0,1:T(8,128)S(1)} %get-tuple-element.10, f32[3,1024]{1,0:T(4,128)S(1)} %maximum_multiply_fusion, f32[3,1280]{1,0:T(4,128)S(1)} %constant_dynamic-update-slice_fusion), kind=kOutput, calls=%fused_computation.10 | convolution fusion | flops 62914560 | bytes 10530816 | tf_op jit(solution)/shard_map/coj,j->co/dot_general | solution.py:87
  45.6 18.7 %convolution_bitcast_fusion = f32[1280,1280]{1,0:T(8,128)} fusion(f32[3,1024]{1,0:T(4,128)S(1)} %get-tuple-element.13, f32[1024,1280]{0,1:T(8,128)} %copy-done.2, f32[1024,1280]{0,1:T(8,128)} %copy-done, f32[3,1024]{1,0:T(4,128)S(1)} %maximum_multiply_fusion, f32[3,1280]{1,0:T(4,128)S(1)} %constant_dynamic-update-slice_fusion, ...), kind=kOutput, calls=%fused_computation.12 | convolution fusion | flops 10089922560 | bytes 24943616 | tf_op jit(solution)/shard_map/coi,coj->ij/dot_general | solution.py:113
  64.3 3.1 %fusion.58 = (f32[256,1280]{1,0:T(8,128)S(1)}, f32[256,1280]{1,0:T(8,128)S(1)}, f32[256,1280]{1,0:T(8,128)S(1)}, f32[256,1280]{1,0:T(8,128)S(1)}) fusion(f32[1280,1280]{1,0:T(8,128)} %convolution_bitcast_fusion), kind=kLoop, calls=%fused_computation.106 | loop fusion | bytes 10485760 | tf_op jit(solution)/shard_map/slice | solution.py:118
  67.3 3.3 %collective-permute-start.4 = (f32[256,1280]{1,0:T(8,128)S(1)}, f32[256,1280]{1,0:T(8,128)S(1)}, u32[]{:S(2)}, u32[]{:S(2)}) collective-permute-start(f32[256,1280]{1,0:T(8,128)S(1)} %get-tuple-element.6), channel_id=1, source_target_pairs={{4,0},{8,4},{12,8},{16,12},{20,16},{24,20},{28,24},{5,1},{9,5},{13... | collective-permute-start | bytes 3932168 | tf_op jit(solution)/shard_map/ppermute | solution.py:51
  70.7 3.8 %collective-permute-start.6 = (f32[256,1280]{1,0:T(8,128)S(1)}, f32[256,1280]{1,0:T(8,128)}, u32[]{:S(2)}, u32[]{:S(2)}) collective-permute-start(f32[256,1280]{1,0:T(8,128)S(1)} %get-tuple-element.8), channel_id=1, source_target_pairs={{0,3},{1,0},{2,1},{3,2},{4,7},{5,4},{6,5},{7,6},{8,11},{9,8},{10,9... | collective-permute-start | bytes 3932168 | tf_op jit(solution)/shard_map/ppermute | solution.py:57
  74.6 1.9 %collective-permute-start.5 = (f32[256,1280]{1,0:T(8,128)S(1)}, f32[256,1280]{1,0:T(8,128)}, u32[]{:S(2)}, u32[]{:S(2)}) collective-permute-start(f32[256,1280]{1,0:T(8,128)S(1)} %get-tuple-element.9), channel_id=1, source_target_pairs={{0,4},{4,8},{8,12},{12,16},{16,20},{20,24},{24,28},{1,5},{5,9},{9,... | collective-permute-start | bytes 3932168 | tf_op jit(solution)/shard_map/ppermute | solution.py:51
  76.5 15.2 %fusion.26 = f32[1280]{0:T(1024)S(1)} fusion(f32[1024,1280]{0,1:T(8,128)S(1)} %copy-done.3, f32[1024,1280]{0,1:T(8,128)S(1)} %copy-done.1, f32[3,1024]{1,0:T(4,128)S(1)} %maximum_multiply_fusion, f32[3,1280]{1,0:T(4,128)S(1)} %constant_dynamic-update-slice_fusion, f32[3,1024,1]{1,0,2:T(4,128)S(1)} %get-tuple-element.12), kind=kOutput, calls=%fused_computation.28 | convolution fusion | flops 62914560 | bytes 10530816 | tf_op jit(solution)/shard_map/coi,co->i/dot_general | solution.py:116
  91.7 4.5 %collective-permute-start.8 = (f32[256]{0:T(256)S(1)}, f32[256]{0:T(256)S(1)}, u32[]{:S(2)}, u32[]{:S(2)}) collective-permute-start(f32[256]{0:T(256)S(1)} %get-tuple-element.14), channel_id=1, source_target_pairs={{4,0},{8,4},{12,8},{16,12},{20,16},{24,20},{28,24},{5,1},{9,5},{13... | collective-permute-start | bytes 3080 | tf_op jit(solution)/shard_map/ppermute | solution.py:51
  96.3 1.3 collective-permute-done.8
  97.5 33.2 %collective-permute-done.11 = f32[256]{0:T(256)S(1)} collective-permute-done((f32[256]{0:T(256)S(1)}, f32[256]{0:T(256)S(1)}, u32[]{:S(2)}, u32[]{:S(2)}) %collective-permute-start.11) | collective-permute-done | bytes 1056 | tf_op jit(solution)/shard_map/ppermute | solution.py:57
  130.7 1.8 %collective-permute-start.10 = (f32[256]{0:T(256)S(1)}, f32[256]{0:T(256)S(1)}, u32[]{:S(2)}, u32[]{:S(2)}) collective-permute-start(f32[256]{0:T(256)S(1)} %get-tuple-element.16), channel_id=1, source_target_pairs={{0,3},{1,0},{2,1},{3,2},{4,7},{5,4},{6,5},{7,6},{8,11},{9,8},{10,9... | collective-permute-start | bytes 3080 | tf_op jit(solution)/shard_map/ppermute | solution.py:57
  132.5 1.8 %collective-permute-done.10 = f32[256]{0:T(256)S(1)} collective-permute-done((f32[256]{0:T(256)S(1)}, f32[256]{0:T(256)S(1)}, u32[]{:S(2)}, u32[]{:S(2)}) %collective-permute-start.10) | collective-permute-done | bytes 1056 | tf_op jit(solution)/shard_map/ppermute | solution.py:57
  134.3 1.9 %collective-permute-start.9 = (f32[256]{0:T(256)S(1)}, f32[256]{0:T(256)S(1)}, u32[]{:S(2)}, u32[]{:S(2)}) collective-permute-start(f32[256]{0:T(256)S(1)} %get-tuple-element.17), channel_id=1, source_target_pairs={{0,4},{4,8},{8,12},{12,16},{16,20},{20,24},{24,28},{1,5},{5,9},{9,... | collective-permute-start | bytes 3080 | tf_op jit(solution)/shard_map/ppermute | solution.py:51
  136.2 3.9 %collective-permute-done.9 = f32[256]{0:T(256)S(1)} collective-permute-done((f32[256]{0:T(256)S(1)}, f32[256]{0:T(256)S(1)}, u32[]{:S(2)}, u32[]{:S(2)}) %collective-permute-start.9) | collective-permute-done | bytes 1056 | tf_op jit(solution)/shard_map/ppermute | solution.py:51
  140.7 1.3 fusion.50
  149.1 1.1 fusion.36
  153.3 1.7 %copy-done.4 = f32[13,256,256]{2,1,0:T(8,128)} copy-done((f32[13,256,256]{2,1,0:T(8,128)}, f32[13,256,256]{2,1,0:T(8,128)S(1)}, u32[]{:S(2)}) %copy-start.4) | copy-done | bytes 3407896
  (57 shorter events, 15.3 us)
Async XLA Ops:
  2.8 12.0 %collective-permute-start.3 = (f32[1,1,4,256]{3,2,1,0:T(4,128)S(1)}, f32[1,1,4,256]{3,2,1,0:T(4,128)S(1)}, u32[]{:S(2)}, u32[]{:S(2)}) collective-permute-start(f32[1,1,4,256]{3,2,1,0:T(4,128)S(1)} %maximum_bitcast_fusion), channel_id=1, source_target_pairs={{1,0},{2,1},{3,2},{0,3},{5,4},{6,5},{7,6},{4,7},{9,8},{10,9},{11,1... | collective-permute-start | bytes 12296 | tf_op jit(solution)/shard_map/ppermute | solution.py:41
  6.4 8.4 %collective-permute-start.2 = (f32[1,1,4,256]{3,2,1,0:T(4,128)S(1)}, f32[1,1,4,256]{3,2,1,0:T(4,128)S(1)}, u32[]{:S(2)}, u32[]{:S(2)}) collective-permute-start(f32[1,1,4,256]{3,2,1,0:T(4,128)S(1)} %maximum_bitcast_fusion), channel_id=1, source_target_pairs={{0,1},{1,2},{2,3},{3,0},{4,5},{5,6},{6,7},{7,4},{8,9},{9,10},{10,1... | collective-permute-start | bytes 12296 | tf_op jit(solution)/shard_map/ppermute | solution.py:39
  6.4 8.3 %collective-permute-start.1 = (f32[1,1,4,256]{3,2,1,0:T(4,128)S(1)}, f32[1,1,4,256]{3,2,1,0:T(4,128)S(1)}, u32[]{:S(2)}, u32[]{:S(2)}) collective-permute-start(f32[1,1,4,256]{3,2,1,0:T(4,128)S(1)} %maximum_bitcast_fusion), channel_id=1, source_target_pairs={{4,0},{8,4},{12,8},{16,12},{20,16},{24,20},{28,24},{5,1},{9,5},{13... | collective-permute-start | bytes 12296 | tf_op jit(solution)/shard_map/ppermute | solution.py:41
  8.9 5.8 %collective-permute-start = (f32[1,1,4,256]{3,2,1,0:T(4,128)S(1)}, f32[1,1,4,256]{3,2,1,0:T(4,128)S(1)}, u32[]{:S(2)}, u32[]{:S(2)}) collective-permute-start(f32[1,1,4,256]{3,2,1,0:T(4,128)S(1)} %maximum_bitcast_fusion), channel_id=1, source_target_pairs={{0,4},{4,8},{8,12},{12,16},{16,20},{20,24},{24,28},{1,5},{5,9},{9,... | collective-permute-start | bytes 12296 | tf_op jit(solution)/shard_map/ppermute | solution.py:39
  29.0 5.9 %copy-start = (f32[1024,1280]{0,1:T(8,128)}, f32[1024,1280]{0,1:T(8,128)S(1)}, u32[]{:S(2)}) copy-start(f32[1024,1280]{0,1:T(8,128)S(1)} %get-tuple-element.10) | copy-start | bytes 15728644
  29.0 6.3 %copy-start.2 = (f32[1024,1280]{0,1:T(8,128)}, f32[1024,1280]{0,1:T(8,128)S(1)}, u32[]{:S(2)}) copy-start(f32[1024,1280]{0,1:T(8,128)S(1)} %get-tuple-element.11) | copy-start | bytes 15728644
  35.3 10.2 %copy-start.5 = (f32[1,1,3,1024]{3,1,2,0:T(1,128)S(1)}, f32[1,1,3,1024]{3,1,2,0:T(1,128)}, u32[]{:S(2)}) copy-start(f32[1,1,3,1024]{3,1,2,0:T(1,128)} %param.6) | copy-start | bytes 36868
  64.3 12.2 %copy-start.1 = (f32[1024,1280]{0,1:T(8,128)S(1)}, f32[1024,1280]{0,1:T(8,128)}, u32[]{:S(2)}) copy-start(f32[1024,1280]{0,1:T(8,128)} %copy-done) | copy-start | bytes 15728644
  64.3 12.2 %copy-start.3 = (f32[1024,1280]{0,1:T(8,128)S(1)}, f32[1024,1280]{0,1:T(8,128)}, u32[]{:S(2)}) copy-start(f32[1024,1280]{0,1:T(8,128)} %copy-done.2) | copy-start | bytes 15728644
  67.3 73.3 %collective-permute-start.4 = (f32[256,1280]{1,0:T(8,128)S(1)}, f32[256,1280]{1,0:T(8,128)S(1)}, u32[]{:S(2)}, u32[]{:S(2)}) collective-permute-start(f32[256,1280]{1,0:T(8,128)S(1)} %get-tuple-element.6), channel_id=1, source_target_pairs={{4,0},{8,4},{12,8},{16,12},{20,16},{24,20},{28,24},{5,1},{9,5},{13... | collective-permute-start | bytes 3932168 | tf_op jit(solution)/shard_map/ppermute | solution.py:51
  70.7 70.0 %collective-permute-start.7 = (f32[256,1280]{1,0:T(8,128)S(1)}, f32[256,1280]{1,0:T(8,128)}, u32[]{:S(2)}, u32[]{:S(2)}) collective-permute-start(f32[256,1280]{1,0:T(8,128)S(1)} %get-tuple-element.7), channel_id=1, source_target_pairs={{0,1},{1,2},{2,3},{3,0},{4,5},{5,6},{6,7},{7,4},{8,9},{9,10},{10,1... | collective-permute-start | bytes 3932168 | tf_op jit(solution)/shard_map/ppermute | solution.py:57
  70.7 69.9 %collective-permute-start.6 = (f32[256,1280]{1,0:T(8,128)S(1)}, f32[256,1280]{1,0:T(8,128)}, u32[]{:S(2)}, u32[]{:S(2)}) collective-permute-start(f32[256,1280]{1,0:T(8,128)S(1)} %get-tuple-element.8), channel_id=1, source_target_pairs={{0,3},{1,0},{2,1},{3,2},{4,7},{5,4},{6,5},{7,6},{8,11},{9,8},{10,9... | collective-permute-start | bytes 3932168 | tf_op jit(solution)/shard_map/ppermute | solution.py:57
  74.6 66.1 %collective-permute-start.5 = (f32[256,1280]{1,0:T(8,128)S(1)}, f32[256,1280]{1,0:T(8,128)}, u32[]{:S(2)}, u32[]{:S(2)}) collective-permute-start(f32[256,1280]{1,0:T(8,128)S(1)} %get-tuple-element.9), channel_id=1, source_target_pairs={{0,4},{4,8},{8,12},{12,16},{16,20},{20,24},{24,28},{1,5},{5,9},{9,... | collective-permute-start | bytes 3932168 | tf_op jit(solution)/shard_map/ppermute | solution.py:51
  91.7 5.8 %collective-permute-start.8 = (f32[256]{0:T(256)S(1)}, f32[256]{0:T(256)S(1)}, u32[]{:S(2)}, u32[]{:S(2)}) collective-permute-start(f32[256]{0:T(256)S(1)} %get-tuple-element.14), channel_id=1, source_target_pairs={{4,0},{8,4},{12,8},{16,12},{20,16},{24,20},{28,24},{5,1},{9,5},{13... | collective-permute-start | bytes 3080 | tf_op jit(solution)/shard_map/ppermute | solution.py:51
  97.5 33.2 %collective-permute-start.11 = (f32[256]{0:T(256)S(1)}, f32[256]{0:T(256)S(1)}, u32[]{:S(2)}, u32[]{:S(2)}) collective-permute-start(f32[256]{0:T(256)S(1)} %get-tuple-element.15), channel_id=1, source_target_pairs={{0,1},{1,2},{2,3},{3,0},{4,5},{5,6},{6,7},{7,4},{8,9},{9,10},{10,1... | collective-permute-start | bytes 3080 | tf_op jit(solution)/shard_map/ppermute | solution.py:57
  130.7 3.6 %collective-permute-start.10 = (f32[256]{0:T(256)S(1)}, f32[256]{0:T(256)S(1)}, u32[]{:S(2)}, u32[]{:S(2)}) collective-permute-start(f32[256]{0:T(256)S(1)} %get-tuple-element.16), channel_id=1, source_target_pairs={{0,3},{1,0},{2,1},{3,2},{4,7},{5,4},{6,5},{7,6},{8,11},{9,8},{10,9... | collective-permute-start | bytes 3080 | tf_op jit(solution)/shard_map/ppermute | solution.py:57
  134.3 5.8 %collective-permute-start.9 = (f32[256]{0:T(256)S(1)}, f32[256]{0:T(256)S(1)}, u32[]{:S(2)}, u32[]{:S(2)}) collective-permute-start(f32[256]{0:T(256)S(1)} %get-tuple-element.17), channel_id=1, source_target_pairs={{0,4},{4,8},{8,12},{12,16},{16,20},{20,24},{24,28},{1,5},{5,9},{9,... | collective-permute-start | bytes 3080 | tf_op jit(solution)/shard_map/ppermute | solution.py:51
  153.2 1.8 %copy-start.4 = (f32[13,256,256]{2,1,0:T(8,128)}, f32[13,256,256]{2,1,0:T(8,128)S(1)}, u32[]{:S(2)}) copy-start(f32[13,256,256]{2,1,0:T(8,128)S(1)} %fusion.30) | copy-start | bytes 10223620
where the time goes:
time: 156 us; the launch traced here: 155 us
  matrix products  44.1 us (28%)
  waiting for transfers between devices  41.6 us (27%)
  other arithmetic  33.4 us (21%)
  starting transfers between devices  25.4 us (16%)
  local copies, waits for them, and re-layouts  8.93 us (6%)
  between operations  1.6 us (1%)
    ppermute x4, waiting for transfers between devices, passed_along(): return lax.ppermute(value, axis, pairs)  35 us
    dot_general x1, matrix products, shards(): jnp.einsum('coi,coj->ij', weighted_low, coupling_low, preferred_element_t...  18.7 us
    dot_general x1, matrix products, shards(): jnp.einsum('coi,co->i', coupling, weighted_resid, precision=lax.Precision...  15.2 us
    ppermute x4, starting transfers between devices, shifted(): return lax.ppermute(block, axis, route)  11.7 us
    dot_general x1, matrix products, residual_terms(): jnp.einsum('coj,j->co', coupling, moments, precision=lax.Precision.HIGHEST)  10.2 us
    unnamed x10, other arithmetic  8.61 us
    reduce_sum x1, other arithmetic, kernel(): aligned = jnp.sum(sources[:, None, :] * separation, axis=0)  7.79 us
    div x1, other arithmetic, kernel(): 3.0 * aligned / squared * separation - sources[:, None, :]  6.25 us
  transfers between devices with their start and end apart: 12, of which 5 were waited for; matrix products, arithmetic and copies ran while one was open for 11% of the time, Pallas kernels for 0%

commit v1 on v0

v1 whole, which is shorter than its diff:
```python
import functools
import math

import jax
import jax.numpy as jnp
from jax import lax
from jax.experimental import pallas as pl
from jax.experimental.pallas import tpu as pltpu
from jax.sharding import PartitionSpec as P

CROSS = ((0, 0), (-1, 0), (1, 0), (0, -1), (0, 1))
OFFSETS = (
    (0, 0),
    (-1, 0),
    (1, 0),
    (0, -1),
    (0, 1),
    (-2, 0),
    (2, 0),
    (0, -2),
    (0, 2),
    (-1, -1),
    (-1, 1),
    (1, -1),
    (1, 1),
)
OBS_RADIUS = 1.06
SOURCE_RADIUS = 0.99
KERNEL_SCALE = 0.0001
HUBER_EDGE = 0.8
DEGREE = math.pi / 180.0
CHUNK = 256
ROWS = 16
LANES = 128


def cycled(value, axis, steps):
    count = lax.axis_size(axis)
    return lax.ppermute(value, axis, [(i, (i + steps) % count) for i in range(count)])


def place(fraction, lat_index, lon_index, lat_tiles, lon_tiles, radius):
    lat_span = 160.0 * DEGREE / lat_tiles
    latitude = -80.0 * DEGREE + (lat_index + fraction[0]) * lat_span
    longitude = (lon_index + fraction[1]) * (2.0 * math.pi / lon_tiles)
    return radius * jnp.stack(
        [
            jnp.cos(latitude) * jnp.cos(longitude),
            jnp.cos(latitude) * jnp.sin(longitude),
            jnp.sin(latitude),
        ]
    )


def row_kernel(
    own_ref,
    north_ref,
    south_ref,
    west_ref,
    east_ref,
    far_north_ref,
    far_south_ref,
    far_west_ref,
    far_east_ref,
    gram_ref,
    rhs_ref,
    obs,
    column,
    held_even,
    held_odd,
    weighted_even,
    weighted_odd,
    kept,
    predicted,
    right,
    table,
    items,
    members,
    *,
    lat_tiles,
):
    size = rhs_ref.shape[1]
    chunks = obs.shape[0] // len(CROSS)
    slots = chunks * CHUNK
    lat = lax.axis_index("lat")

    for tile, ref in enumerate((own_ref, north_ref, south_ref, west_ref, east_ref)):
        for chunk in range(chunks):
            obs[tile * chunks + chunk] = ref[:, chunk * CHUNK : (chunk + 1) * CHUNK]
    sources = {(0, 0): own_ref, (-1, 0): north_ref, (1, 0): south_ref, (0, -1): west_ref, (0, 1): east_ref}
    sources = {offset: (ref, slots) for offset, ref in sources.items()}
    for at, offset in enumerate(((-2, 0), (-1, -1), (-1, 1))):
        sources[offset] = (far_north_ref, at * size)
    for at, offset in enumerate(((2, 0), (1, -1), (1, 1))):
        sources[offset] = (far_south_ref, at * size)
    sources[(0, -2)] = (far_west_ref, 0)
    sources[(0, 2)] = (far_east_ref, 0)

    def inside(step):
        return (lat + step >= 0) & (lat + step < lat_tiles)

    for target, offset in enumerate(OFFSETS):
        ref, start = sources[offset]
        upright = ref[:, start : start + size].T
        for part in range(4):
            values = jnp.broadcast_to(upright[:, part : part + 1], (size, LANES))
            if part == 3 and offset[0] != 0:
                values = values * inside(offset[0]).astype(jnp.float32)
            column[target, part] = values

    total = jnp.int32(0)
    for tile in (0, 3, 4, 1, 2):
        step = CROSS[tile]
        row = lat + step[0]
        first_row, last_row = row == 0, row == lat_tiles - 1
        own = (-step[0], -step[1])
        rest = [b for b in CROSS if b != own and b[0] == 0]
        ends = [b for b in CROSS if b != own and b[0] != 0]
        order = [OFFSETS.index((b[0] + step[0], b[1] + step[1])) for b in [own] + rest + ends]
        for at, target in enumerate(order):
            table[tile, at] = target
        if len(ends) == 2:
            table[tile, 3] = jnp.where(first_row, order[4], order[3])
            table[tile, 4] = jnp.where(first_row, order[3], order[4])
        members[tile] = 5 - first_row.astype(jnp.int32) - last_row.astype(jnp.int32)
        count = jnp.where(first_row | last_row, chunks, chunks // 2)
        count = jnp.where(inside(step[0]), count, 0)

        def note(chunk, at, tile=tile):
            items[0, at] = tile
            items[1, at] = tile * chunks + chunk
            return at + 1

        total = lax.fori_loop(0, count, note, total)

    gram_ref[...] = jnp.zeros_like(gram_ref)
    held_odd[...] = jnp.zeros_like(held_odd)
    weighted_odd[...] = jnp.zeros_like(weighted_odd)
    right[...] = jnp.zeros_like(right)

    def evaluate(tile, chunk, at, held):
        target = table[tile, at]
        spare = (at != 0).astype(jnp.int32)
        point = [jnp.broadcast_to(obs[chunk, c : c + 1, :], (ROWS, CHUNK)) for c in range(3)]
        sums = [predicted[c] for c in range(3)]
        near = 3.0 * (OBS_RADIUS * OBS_RADIUS - SOURCE_RADIUS * SOURCE_RADIUS) * 0.5 * KERNEL_SCALE
        for start in range(0, size, ROWS):
            span = slice(start, start + ROWS)
            wide = [jnp.concatenate([column[target, part, span, :]] * (CHUNK // LANES), axis=1) for part in range(4)]
            apart = [point[c] - wide[c] for c in range(3)]
            squared = apart[0] * apart[0] + apart[1] * apart[1] + apart[2] * apart[2]
            inverse = lax.rsqrt(squared)
            inverse_square = inverse * inverse
            cube = inverse_square * inverse
            along = cube * (near * inverse_square - 1.5 * KERNEL_SCALE)
            across = cube * KERNEL_SCALE
            for c in range(3):
                value = along * apart[c] - across * wide[c]
                held[at, span, c * CHUNK : (c + 1) * CHUNK] = value.astype(jnp.bfloat16)
                kept[spare, c, span, :] = value
                part = value * wide[3]
                for sub in range(0, ROWS, 8):
                    sums[c] = sums[c] + part[sub : sub + 8]
        for c in range(3):
            predicted[c] = sums[c]

    def multiply(tile, at, held, weighted):
        target = table[tile, at]
        gram_ref[target] += lax.dot_general(
            weighted[...], held[at], (((1,), (1,)), ((), ())), preferred_element_type=jnp.float32
        )

    def finish(chunk, weighted):
        present = obs[chunk, 6:7, :]
        scale, force = [], []
        for c in range(3):
            residual = obs[chunk, 3 + c : 4 + c, :] - jnp.sum(predicted[c], axis=0, keepdims=True)
            weight = present * HUBER_EDGE / jnp.maximum(jnp.abs(residual), HUBER_EDGE)
            scale.append(jnp.broadcast_to(weight, (ROWS, CHUNK)))
            force.append(jnp.broadcast_to(weight * residual, (ROWS, CHUNK)))
        for start in range(0, size, ROWS):
            span = slice(start, start + ROWS)
            pull = None
            for c in range(3):
                value = kept[0, c, span, :]
                weighted[span, c * CHUNK : (c + 1) * CHUNK] = (scale[c] * value).astype(jnp.bfloat16)
                part = force[c] * value
                pull = part if pull is None else pull + part
            for lane in range(0, CHUNK, LANES):
                right[span, :] += pull[:, lane : lane + LANES]

    def advance(item, held, weighted, held_before, weighted_before):
        tile, chunk = items[0, item], items[1, item]
        before = items[0, jnp.maximum(item - 1, 0)]
        predicted[...] = jnp.zeros_like(predicted)

        def block(at, carry):
            multiply(before, at, held_before, weighted_before)
            evaluate(tile, chunk, at, held)
            return carry

        lax.fori_loop(0, jnp.maximum(members[tile], members[before]), block, 0)
        finish(chunk, weighted)

    def pair(at, carry):
        advance(2 * at, held_even, weighted_even, held_odd, weighted_odd)
        advance(2 * at + 1, held_odd, weighted_odd, held_even, weighted_even)
        return carry

    lax.fori_loop(0, total // 2, pair, 0)
    last = items[0, total - 1]

    def drain(at, carry):
        multiply(last, at, held_odd, weighted_odd)
        return carry

    lax.fori_loop(0, members[last], drain, 0)

    for target, offset in enumerate(OFFSETS):
        if offset[0] != 0:

            @pl.when(jnp.logical_not(inside(offset[0])))
            def _():
                gram_ref[target] = jnp.zeros_like(gram_ref[target])

    rhs_ref[...] = jnp.sum(right[...].T, axis=0, keepdims=True)


def shards(obs_frac, obs_field, dipole_frac, dipole_moment, obs_count):
    lat_tiles = lax.axis_size("lat")
    lon_tiles = lax.axis_size("lon")
    lat_index = lax.axis_index("lat")
    lon_index = lax.axis_index("lon")
    size = dipole_frac.shape[3]
    slots = obs_frac.shape[3]
    source = place(dipole_frac[0, 0], lat_index, lon_index, lat_tiles, lon_tiles, SOURCE_RADIUS)
    points = place(obs_frac[0, 0], lat_index, lon_index, lat_tiles, lon_tiles, OBS_RADIUS)
    present = (jnp.arange(slots, dtype=jnp.int32) < obs_count[0, 0]).astype(jnp.float32)
    observed = jnp.concatenate([points, obs_field[0, 0], present[None], jnp.zeros((1, slots), jnp.float32)], 0)
    dipoles = jnp.concatenate([source, dipole_moment[0, 0][None], jnp.zeros((4, size), jnp.float32)], 0)
    package = jnp.concatenate([observed, dipoles], 1)
    north = cycled(package, "lat", 1)
    south = cycled(package, "lat", -1)
    west = cycled(package, "lon", 1)
    east = cycled(package, "lon", -1)
    far_north = cycled(jnp.concatenate([north[:, slots:], west[:, slots:], east[:, slots:]], 1), "lat", 1)
    far_south = cycled(jnp.concatenate([south[:, slots:], west[:, slots:], east[:, slots:]], 1), "lat", -1)
    far_west = cycled(west[:, slots:], "lon", 1)
    far_east = cycled(east[:, slots:], "lon", -1)
    chunks = slots // CHUNK
    gram, rhs = pl.pallas_call(
        functools.partial(row_kernel, lat_tiles=lat_tiles),
        out_shape=(
            jax.ShapeDtypeStruct((len(OFFSETS), size, size), jnp.float32),
            jax.ShapeDtypeStruct((1, size), jnp.float32),
        ),
        in_specs=[pl.BlockSpec(memory_space=pltpu.VMEM)] * 9,
        out_specs=(pl.BlockSpec(memory_space=pltpu.VMEM), pl.BlockSpec(memory_space=pltpu.VMEM)),
        scratch_shapes=[
            pltpu.VMEM((5 * chunks, 8, CHUNK), jnp.float32),
            pltpu.VMEM((len(OFFSETS), 4, size, LANES), jnp.float32),
            pltpu.VMEM((5, size, 3 * CHUNK), jnp.bfloat16),
            pltpu.VMEM((5, size, 3 * CHUNK), jnp.bfloat16),
            pltpu.VMEM((size, 3 * CHUNK), jnp.bfloat16),
            pltpu.VMEM((size, 3 * CHUNK), jnp.bfloat16),
            pltpu.VMEM((2, 3, size, CHUNK), jnp.float32),
            pltpu.VMEM((3, 8, CHUNK), jnp.float32),
            pltpu.VMEM((size, LANES), jnp.float32),
            pltpu.SMEM((5, 5), jnp.int32),
            pltpu.SMEM((2, 5 * chunks), jnp.int32),
            pltpu.SMEM((5,), jnp.int32),
        ],
        compiler_params=pltpu.CompilerParams(vmem_limit_bytes=60 * 1024 * 1024),
        name="row_blocks",
    )(package, north, south, west, east, far_north, far_south, far_west, far_east)
    return (gram[None, None], rhs[None])


def solution(mesh):
    in_specs = (
        P("lat", "lon", None, None),
        P("lat", "lon", None, None),
        P("lat", "lon", None, None),
        P("lat", "lon", None),
        P("lat", "lon"),
    )
    out_specs = (P("lat", "lon", None, None, None), P("lat", "lon", None))
    return jax.shard_map(shards, mesh=mesh, in_specs=in_specs, out_specs=out_specs, check_vma=False)
```

time: 156 us -> 57.7 us (0.37)
  the two profiles are of different devices: /device:TPU:4 before, /device:TPU:0 now
where the time goes in v1:
time: 57.7 us; the launch traced here: 57.3 us
  Pallas kernels  30.1 us (52%)
  starting transfers between devices  10.8 us (19%)
  waiting for transfers between devices  9.75 us (17%)
  other arithmetic  3.27 us (6%)
  local copies, waits for them, and re-layouts  1.88 us (3%)
  between operations  1.41 us (2%)
    pallas_call x1, Pallas kernels, shards(): pl.pallas_call(functools.partial(row_kernel, lat_tiles=lat_tiles), out_sh...  30.1 us
    ppermute x8, starting transfers between devices, cycled(): lax.ppermute(value, axis, [(i, (i + steps) % count) for i in range(count)])  10.8 us
    ppermute x8, waiting for transfers between devices, cycled(): lax.ppermute(value, axis, [(i, (i + steps) % count) for i in range(count)])  9.75 us
    unnamed x19, local copies, waits for them, and re-layouts  1.86 us
    mul x2, other arithmetic, place(): jnp.cos(latitude) * jnp.cos(longitude)  1.79 us
  transfers between devices with their start and end apart: 8, of which 5 were waited for; matrix products, arithmetic and copies ran while one was open for 0% of the time, Pallas kernels for 0%

profile of v1, /device:TPU:0, one launch (start us, length us, event | category | flops | bytes accessed | tf_op | source)
XLA Modules:
  0.0 57.3 jit_solution(10406752076258092993)
XLA Ops:
  1.3 0.7 %copy.9 = f32[1,1,3,1024]{3,2,1,0:T(4,128)S(1)} copy(f32[1,1,3,1024]{3,1,2,0:T(1,128)} %param.6) | data formatting | bytes 24576
  2.0 0.7 %fusion.1 = (f32[1,1,1,256]{3,2,1,0:T(1,128)S(1)}, f32[1,1,1,256]{3,2,1,0:T(1,128)S(1)}) fusion(f32[1,1,2,256]{3,2,1,0:T(2,128)} %param.7, f32[]{:T(128)S(6)} %convert_element_type.18), kind=kLoop, calls=%fused_computation.20 | loop fusion | flops 768 | bytes 3076 | tf_op jit(solution)/shard_map/cos | solution.py:48
  2.7 1.0 %multiply_bitcast_fusion.1 = (f32[1,1024]{1,0:T(1,128)S(1)}, f32[1,1024]{1,0:T(1,128)S(1)}, f32[1,1024]{1,0:T(1,128)S(1)}) fusion(f32[1,1,2,1024]{3,2,1,0:T(2,128)} %param.5, f32[]{:T(128)S(6)} %convert_element_type.19, f32[]{:T(128)S(6)} %convert_element_type.18), kind=kLoop, calls=%fused_computation.10 | loop fusion | flops 7168 | bytes 20488 | tf_op jit(solution)/shard_map/mul | solution.py:48
  3.8 0.8 %multiply_bitcast_fusion.3 = (f32[1,256]{1,0:T(1,128)S(1)}, f32[1,256]{1,0:T(1,128)S(1)}, f32[1,256]{1,0:T(1,128)S(1)}) fusion(f32[1,1,1,256]{3,2,1,0:T(1,128)S(1)} %get-tuple-element.6, f32[1,1,2,256]{3,2,1,0:T(2,128)} %param.7, f32[]{:T(128)S(6)} %convert_element_type.19, f32[1,1,1,256]{3,2,1,0:T(1,128)S(1)} %get-tuple-element.7), kind=kLoop, calls=%fused_computation.15 | loop fusion | flops 1024 | bytes 6148 | tf_op jit(solution)/shard_map/mul | solution.py:48
  4.6 0.7 %maximum_maximum_fusion.own_ref = f32[8,1280]{1,0:T(8,128)S(1)} fusion(f32[4,256]{1,0:T(4,128)S(1)} %broadcast_in_dim.14, f32[1,256]{1,0:T(1,128)} %bitcast.21, f32[3,256]{1,0:T(4,128)S(1)} %maximum_multiply_fusion.1, f32[1,1024]{1,0:T(1,128)S(1)} %broadcast_in_dim.13, f32[1,1024]{1,0:T(1,128)S(1)} %compare_convert_fusion, f32[3,1024]{1,0:T(4,128)S(1)} %bitcast.20, ...), kind=kLoop, calls=%fused_computation | loop fusion | flops 61440 | bytes 81920 | tf_op jit(solution)/shard_map/concatenate | solution.py:241
  5.3 5.1 %collective-permute-start.3 = (f32[8,1280]{1,0:T(8,128)S(1)}, f32[8,1280]{1,0:T(8,128)S(1)}, u32[]{:S(2)}, u32[]{:S(2)}) collective-permute-start(f32[8,1280]{1,0:T(8,128)S(1)} %maximum_maximum_fusion.own_ref), channel_id=1, source_target_pairs={{0,3},{1,0},{2,1},{3,2},{4,7},{5,4},{6,5},{7,6},{8,11},{9,8},{10,9... | collective-permute-start | bytes 122888 | tf_op jit(solution)/shard_map/ppermute | solution.py:39
  10.5 0.0 collective-permute-start.2
  10.5 1.6 %collective-permute-start.1 = (f32[8,1280]{1,0:T(8,128)S(1)}, f32[8,1280]{1,0:T(8,128)S(1)}, u32[]{:S(2)}, u32[]{:S(2)}) collective-permute-start(f32[8,1280]{1,0:T(8,128)S(1)} %maximum_maximum_fusion.own_ref), channel_id=1, source_target_pairs={{0,28},{4,0},{8,4},{12,8},{16,12},{20,16},{24,20},{28,24},{1,29},{... | collective-permute-start | bytes 122888 | tf_op jit(solution)/shard_map/ppermute | solution.py:39
  12.1 0.0 collective-permute-start
  12.1 0.1 collective-permute-done.3.east_ref
  12.1 4.1 %collective-permute-done.2.west_ref = f32[8,1280]{1,0:T(8,128)S(1)} collective-permute-done((f32[8,1280]{1,0:T(8,128)S(1)}, f32[8,1280]{1,0:T(8,128)S(1)}, u32[]{:S(2)}, u32[]{:S(2)}) %collective-permute-start.2) | collective-permute-done | bytes 40992 | tf_op jit(solution)/shard_map/ppermute | solution.py:39
  16.3 0.1 collective-permute-done.north_ref
  16.4 0.4 collective-permute-start.5
  16.8 0.1 collective-permute-start.4
  17.0 3.5 %collective-permute-start.7 = (f32[8,256]{1,0:T(8,128)S(1)}, f32[8,256]{1,0:T(8,128)S(1)}, u32[]{:S(2)}, u32[]{:S(2)}) collective-permute-start(f32[8,256]{1,0:T(8,128)S(1)} %slice.42), channel_id=1, source_target_pairs={{0,3},{1,0},{2,1},{3,2},{4,7},{5,4},{6,5},{7,6},{8,11},{9,8},{10,9... | collective-permute-start | bytes 24584 | tf_op jit(solution)/shard_map/ppermute | solution.py:39
  20.5 0.0 collective-permute-start.6
  20.5 1.4 %collective-permute-done.7.far_east_ref = f32[8,256]{1,0:T(8,128)S(1)} collective-permute-done((f32[8,256]{1,0:T(8,128)S(1)}, f32[8,256]{1,0:T(8,128)S(1)}, u32[]{:S(2)}, u32[]{:S(2)}) %collective-permute-start.7) | collective-permute-done | bytes 8224 | tf_op jit(solution)/shard_map/ppermute | solution.py:39
  21.9 4.1 %collective-permute-done.6.far_west_ref = f32[8,256]{1,0:T(8,128)S(1)} collective-permute-done((f32[8,256]{1,0:T(8,128)S(1)}, f32[8,256]{1,0:T(8,128)S(1)}, u32[]{:S(2)}, u32[]{:S(2)}) %collective-permute-start.6) | collective-permute-done | bytes 8224 | tf_op jit(solution)/shard_map/ppermute | solution.py:39
  26.0 0.0 collective-permute-done.5.far_south_ref
  26.0 0.0 collective-permute-done.4.far_north_ref
  26.0 0.5 copy-done.8
  26.6 0.0 copy-done.5
  26.6 0.6 %copy-done.6 = f32[8,768]{1,0:T(8,128)} copy-done((f32[8,768]{1,0:T(8,128)}, f32[8,768]{1,0:T(8,128)S(1)}, u32[]{:S(2)}) %copy-start.6) | copy-done | bytes 24600
  27.2 30.1 %row_blocks.1 = (f32[13,256,256]{2,1,0:T(8,128)}, f32[1,256]{1,0:T(1,128)}) custom-call(f32[8,1280]{1,0:T(8,128)} %copy-done, f32[8,1280]{1,0:T(8,128)} %copy-done.4, f32[8,1280]{1,0:T(8,128)} %copy-done.3, f32[8,1280]{1,0:T(8,128)} %copy-done.2, f32[8,1280]{1,0:T(8,128)} %copy-done.1, f32[8,768]{1,0:T(8,128)} %copy-done.6, f32[8,768]{1,0:T(8,128)} %copy-done.5, ...), custom_call_target="tpu_custom_call" | custom-call | tf_op jit(solution)/shard_map/row_blocks/pallas_call | solution.py:251
  (26 shorter events, 0.1 us)
Async XLA Ops:
  5.3 20.7 %copy-start = (f32[8,1280]{1,0:T(8,128)}, f32[8,1280]{1,0:T(8,128)S(1)}, u32[]{:S(2)}) copy-start(f32[8,1280]{1,0:T(8,128)S(1)} %maximum_maximum_fusion.own_ref) | copy-start | bytes 122884
  5.3 6.8 %collective-permute-start.3 = (f32[8,1280]{1,0:T(8,128)S(1)}, f32[8,1280]{1,0:T(8,128)S(1)}, u32[]{:S(2)}, u32[]{:S(2)}) collective-permute-start(f32[8,1280]{1,0:T(8,128)S(1)} %maximum_maximum_fusion.own_ref), channel_id=1, source_target_pairs={{0,3},{1,0},{2,1},{3,2},{4,7},{5,4},{6,5},{7,6},{8,11},{9,8},{10,9... | collective-permute-start | bytes 122888 | tf_op jit(solution)/shard_map/ppermute | solution.py:39
  10.5 5.8 %collective-permute-start.2 = (f32[8,1280]{1,0:T(8,128)S(1)}, f32[8,1280]{1,0:T(8,128)S(1)}, u32[]{:S(2)}, u32[]{:S(2)}) collective-permute-start(f32[8,1280]{1,0:T(8,128)S(1)} %maximum_maximum_fusion.own_ref), channel_id=1, source_target_pairs={{0,1},{1,2},{2,3},{3,0},{4,5},{5,6},{6,7},{7,4},{8,9},{9,10},{10,1... | collective-permute-start | bytes 122888 | tf_op jit(solution)/shard_map/ppermute | solution.py:39
  10.5 5.8 %collective-permute-start.1 = (f32[8,1280]{1,0:T(8,128)S(1)}, f32[8,1280]{1,0:T(8,128)S(1)}, u32[]{:S(2)}, u32[]{:S(2)}) collective-permute-start(f32[8,1280]{1,0:T(8,128)S(1)} %maximum_maximum_fusion.own_ref), channel_id=1, source_target_pairs={{0,28},{4,0},{8,4},{12,8},{16,12},{20,16},{24,20},{28,24},{1,29},{... | collective-permute-start | bytes 122888 | tf_op jit(solution)/shard_map/ppermute | solution.py:39
  12.1 4.3 %collective-permute-start = (f32[8,1280]{1,0:T(8,128)S(1)}, f32[8,1280]{1,0:T(8,128)S(1)}, u32[]{:S(2)}, u32[]{:S(2)}) collective-permute-start(f32[8,1280]{1,0:T(8,128)S(1)} %maximum_maximum_fusion.own_ref), channel_id=1, source_target_pairs={{0,4},{4,8},{8,12},{12,16},{16,20},{20,24},{24,28},{28,0},{1,5},{5... | collective-permute-start | bytes 122888 | tf_op jit(solution)/shard_map/ppermute | solution.py:39
  12.1 13.9 %copy-start.1 = (f32[8,1280]{1,0:T(8,128)}, f32[8,1280]{1,0:T(8,128)S(1)}, u32[]{:S(2)}) copy-start(f32[8,1280]{1,0:T(8,128)S(1)} %collective-permute-done.3.east_ref) | copy-start | bytes 122884
  16.3 9.7 %copy-start.2 = (f32[8,1280]{1,0:T(8,128)}, f32[8,1280]{1,0:T(8,128)S(1)}, u32[]{:S(2)}) copy-start(f32[8,1280]{1,0:T(8,128)S(1)} %collective-permute-done.2.west_ref) | copy-start | bytes 122884
  16.3 9.7 %copy-start.3 = (f32[8,1280]{1,0:T(8,128)}, f32[8,1280]{1,0:T(8,128)S(1)}, u32[]{:S(2)}) copy-start(f32[8,1280]{1,0:T(8,128)S(1)} %collective-permute-done.1.south_ref) | copy-start | bytes 122884
  16.4 9.6 %copy-start.4 = (f32[8,1280]{1,0:T(8,128)}, f32[8,1280]{1,0:T(8,128)S(1)}, u32[]{:S(2)}) copy-start(f32[8,1280]{1,0:T(8,128)S(1)} %collective-permute-done.north_ref) | copy-start | bytes 122884
  16.4 9.6 %collective-permute-start.5 = (f32[8,768]{1,0:T(8,128)S(1)}, f32[8,768]{1,0:T(8,128)S(1)}, u32[]{:S(2)}, u32[]{:S(2)}) collective-permute-start(f32[8,768]{1,0:T(8,128)S(1)} %get-tuple-element.8), channel_id=1, source_target_pairs={{0,28},{4,0},{8,4},{12,8},{16,12},{20,16},{24,20},{28,24},{1,29},{... | collective-permute-start | bytes 73736 | tf_op jit(solution)/shard_map/ppermute | solution.py:39
  16.8 9.1 %collective-permute-start.4 = (f32[8,768]{1,0:T(8,128)S(1)}, f32[8,768]{1,0:T(8,128)S(1)}, u32[]{:S(2)}, u32[]{:S(2)}) collective-permute-start(f32[8,768]{1,0:T(8,128)S(1)} %get-tuple-element.9), channel_id=1, source_target_pairs={{0,4},{4,8},{8,12},{12,16},{16,20},{20,24},{24,28},{28,0},{1,5},{5... | collective-permute-start | bytes 73736 | tf_op jit(solution)/shard_map/ppermute | solution.py:39
  17.0 4.9 %collective-permute-start.7 = (f32[8,256]{1,0:T(8,128)S(1)}, f32[8,256]{1,0:T(8,128)S(1)}, u32[]{:S(2)}, u32[]{:S(2)}) collective-permute-start(f32[8,256]{1,0:T(8,128)S(1)} %slice.42), channel_id=1, source_target_pairs={{0,3},{1,0},{2,1},{3,2},{4,7},{5,4},{6,5},{7,6},{8,11},{9,8},{10,9... | collective-permute-start | bytes 24584 | tf_op jit(solution)/shard_map/ppermute | solution.py:39
  20.5 5.4 %collective-permute-start.6 = (f32[8,256]{1,0:T(8,128)S(1)}, f32[8,256]{1,0:T(8,128)S(1)}, u32[]{:S(2)}, u32[]{:S(2)}) collective-permute-start(f32[8,256]{1,0:T(8,128)S(1)} %slice.41), channel_id=1, source_target_pairs={{0,1},{1,2},{2,3},{3,0},{4,5},{5,6},{6,7},{7,4},{8,9},{9,10},{10,1... | collective-permute-start | bytes 24584 | tf_op jit(solution)/shard_map/ppermute | solution.py:39
  21.9 4.1 %copy-start.7 = (f32[8,256]{1,0:T(8,128)}, f32[8,256]{1,0:T(8,128)S(1)}, u32[]{:S(2)}) copy-start(f32[8,256]{1,0:T(8,128)S(1)} %collective-permute-done.7.far_east_ref) | copy-start | bytes 24580
  26.0 0.6 %copy-start.8 = (f32[8,256]{1,0:T(8,128)}, f32[8,256]{1,0:T(8,128)S(1)}, u32[]{:S(2)}) copy-start(f32[8,256]{1,0:T(8,128)S(1)} %collective-permute-done.6.far_west_ref) | copy-start | bytes 24580
  26.0 0.6 %copy-start.5 = (f32[8,768]{1,0:T(8,128)}, f32[8,768]{1,0:T(8,128)S(1)}, u32[]{:S(2)}) copy-start(f32[8,768]{1,0:T(8,128)S(1)} %collective-permute-done.5.far_south_ref) | copy-start | bytes 73732
  26.6 0.6 %copy-start.6 = (f32[8,768]{1,0:T(8,128)}, f32[8,768]{1,0:T(8,128)S(1)}, u32[]{:S(2)}) copy-start(f32[8,768]{1,0:T(8,128)S(1)} %collective-permute-done.4.far_north_ref) | copy-start | bytes 73732

commit v2 on v1

--- a/solution.py
+++ b/solution.py
@@ -32,6 +32,8 @@
 CHUNK = 256
 ROWS = 16
 LANES = 128
+DEPTH = 64
+STRETCH = KERNEL_SCALE ** (-2.0 / 3.0)
 
 
 def cycled(value, axis, steps):
@@ -50,6 +52,13 @@
             jnp.sin(latitude),
         ]
     )
+
+
+def split(values):
+    high = values.astype(jnp.bfloat16).astype(jnp.float32)
+    rest = values - high
+    middle = rest.astype(jnp.bfloat16).astype(jnp.float32)
+    return high, middle, rest - middle
 
 
 def row_kernel(
@@ -66,16 +75,21 @@
     rhs_ref,
     obs,
     column,
+    tall,
+    flat,
     held_even,
     held_odd,
     weighted_even,
     weighted_odd,
+    apart_even,
+    apart_odd,
     kept,
     predicted,
     right,
     table,
     items,
     members,
+    counts,
     *,
     lat_tiles,
 ):
@@ -99,17 +113,34 @@
     def inside(step):
         return (lat + step >= 0) & (lat + step < lat_tiles)
 
+    picks = lax.broadcasted_iota(jnp.int32, (DEPTH, 4 * LANES), 0)
+    parts = lax.broadcasted_iota(jnp.int32, (DEPTH, 4 * LANES), 1) // LANES
+    picks = ((picks == parts) | (picks == parts + 16) | (picks == parts + 32)).astype(jnp.bfloat16)
+    row_of = lax.broadcasted_iota(jnp.int32, (8, size), 0)
     for target, offset in enumerate(OFFSETS):
         ref, start = sources[offset]
-        upright = ref[:, start : start + size].T
+        values = ref[:, start : start + size]
+        if offset[0] != 0:
+            values = jnp.where((row_of < 3) | inside(offset[0]), values, 0.0)
+        high, middle, low = split(values)
+        ones = jnp.ones_like(values)
+        stacked = jnp.concatenate([high, high, middle, high, low, middle, ones, jnp.zeros_like(values)], 0)
+        upright = stacked.T.astype(jnp.bfloat16)
+        tall[target] = upright
+        wide = lax.dot_general(upright, picks, (((1,), (0,)), ((), ())), preferred_element_type=jnp.float32)
         for part in range(4):
-            values = jnp.broadcast_to(upright[:, part : part + 1], (size, LANES))
-            if part == 3 and offset[0] != 0:
-                values = values * inside(offset[0]).astype(jnp.float32)
-            column[target, part] = values
-
-    total = jnp.int32(0)
-    for tile in (0, 3, 4, 1, 2):
+            column[target, part] = wide[:, part * LANES : (part + 1) * LANES]
+
+    row_of = lax.broadcasted_iota(jnp.int32, (8, CHUNK), 0)
+    base = STRETCH * (OBS_RADIUS * OBS_RADIUS + SOURCE_RADIUS * SOURCE_RADIUS)
+    for at in range(obs.shape[0]):
+        high, middle, low = split(jnp.where(row_of < 3, obs[at] * (-2.0 * STRETCH), 0.0))
+        first, second, third = split(jnp.full((8, CHUNK), base, jnp.float32))
+        constant = jnp.where(row_of == 0, first, jnp.where(row_of == 1, second, jnp.where(row_of == 2, third, 0.0)))
+        stacked = jnp.concatenate([high, middle, high, low, high, middle, constant, jnp.zeros_like(high)], 0)
+        flat[at] = stacked.astype(jnp.bfloat16)
+
+    for tile in range(len(CROSS)):
         step = CROSS[tile]
         row = lat + step[0]
         first_row, last_row = row == 0, row == lat_tiles - 1
@@ -124,38 +155,44 @@
             table[tile, 4] = jnp.where(first_row, order[3], order[4])
         members[tile] = 5 - first_row.astype(jnp.int32) - last_row.astype(jnp.int32)
         count = jnp.where(first_row | last_row, chunks, chunks // 2)
-        count = jnp.where(inside(step[0]), count, 0)
-
-        def note(chunk, at, tile=tile):
-            items[0, at] = tile
-            items[1, at] = tile * chunks + chunk
-            return at + 1
-
-        total = lax.fori_loop(0, count, note, total)
+        counts[tile] = jnp.where(inside(step[0]), count, 0)
+
+    total = jnp.int32(0)
+    for full in (5, 4):
+        for tile in (0, 3, 4, 1, 2):
+
+            def note(chunk, at, tile=tile):
+                items[0, at] = tile
+                items[1, at] = tile * chunks + chunk
+                return at + 1
+
+            total = lax.fori_loop(0, jnp.where(members[tile] == full, counts[tile], 0), note, total)
 
     gram_ref[...] = jnp.zeros_like(gram_ref)
     held_odd[...] = jnp.zeros_like(held_odd)
     weighted_odd[...] = jnp.zeros_like(weighted_odd)
     right[...] = jnp.zeros_like(right)
 
-    def evaluate(tile, chunk, at, held):
+    def separate(tile, chunk, at, apart):
+        apart[at] = lax.dot_general(
+            tall[table[tile, at]], flat[chunk], (((1,), (0,)), ((), ())), preferred_element_type=jnp.float32
+        )
+
+    def evaluate(tile, chunk, at, held, apart):
         target = table[tile, at]
         spare = (at != 0).astype(jnp.int32)
         point = [jnp.broadcast_to(obs[chunk, c : c + 1, :], (ROWS, CHUNK)) for c in range(3)]
         sums = [predicted[c] for c in range(3)]
-        near = 3.0 * (OBS_RADIUS * OBS_RADIUS - SOURCE_RADIUS * SOURCE_RADIUS) * 0.5 * KERNEL_SCALE
+        near = 1.5 * (OBS_RADIUS * OBS_RADIUS - SOURCE_RADIUS * SOURCE_RADIUS) * STRETCH
         for start in range(0, size, ROWS):
             span = slice(start, start + ROWS)
             wide = [jnp.concatenate([column[target, part, span, :]] * (CHUNK // LANES), axis=1) for part in range(4)]
-            apart = [point[c] - wide[c] for c in range(3)]
-            squared = apart[0] * apart[0] + apart[1] * apart[1] + apart[2] * apart[2]
-            inverse = lax.rsqrt(squared)
+            inverse = lax.rsqrt(apart[at, span, :])
             inverse_square = inverse * inverse
             cube = inverse_square * inverse
-            along = cube * (near * inverse_square - 1.5 * KERNEL_SCALE)
-            across = cube * KERNEL_SCALE
+            along = near * inverse_square - 1.5
             for c in range(3):
-                value = along * apart[c] - across * wide[c]
+                value = cube * (along * (point[c] - wide[c]) - wide[c])
                 held[at, span, c * CHUNK : (c + 1) * CHUNK] = value.astype(jnp.bfloat16)
                 kept[spare, c, span, :] = value
                 part = value * wide[3]
@@ -166,9 +203,10 @@
 
     def multiply(tile, at, held, weighted):
         target = table[tile, at]
-        gram_ref[target] += lax.dot_general(
-            weighted[...], held[at], (((1,), (1,)), ((), ())), preferred_element_type=jnp.float32
-        )
+        for half in (slice(0, size // 2), slice(size // 2, size)):
+            gram_ref[target, half] += lax.dot_general(
+                weighted[half], held[at], (((1,), (1,)), ((), ())), preferred_element_type=jnp.float32
+            )
 
     def finish(chunk, weighted):
         present = obs[chunk, 6:7, :]
@@ -189,24 +227,32 @@
             for lane in range(0, CHUNK, LANES):
                 right[span, :] += pull[:, lane : lane + LANES]
 
-    def advance(item, held, weighted, held_before, weighted_before):
+    def advance(item, held, weighted, apart, held_before, weighted_before, apart_later):
         tile, chunk = items[0, item], items[1, item]
         before = items[0, jnp.maximum(item - 1, 0)]
+        after = jnp.minimum(item + 1, total - 1)
+        later, later_chunk = items[0, after], items[1, after]
         predicted[...] = jnp.zeros_like(predicted)
 
         def block(at, carry):
+            separate(later, later_chunk, at, apart_later)
             multiply(before, at, held_before, weighted_before)
-            evaluate(tile, chunk, at, held)
+            evaluate(tile, chunk, at, held, apart)
             return carry
 
-        lax.fori_loop(0, jnp.maximum(members[tile], members[before]), block, 0)
+        lax.fori_loop(0, members[before], block, 0)
         finish(chunk, weighted)
 
     def pair(at, carry):
-        advance(2 * at, held_even, weighted_even, held_odd, weighted_odd)
-        advance(2 * at + 1, held_odd, weighted_odd, held_even, weighted_even)
+        advance(2 * at, held_even, weighted_even, apart_even, held_odd, weighted_odd, apart_odd)
+        advance(2 * at + 1, held_odd, weighted_odd, apart_odd, held_even, weighted_even, apart_even)
         return carry
 
+    def open_item(at, carry):
+        separate(items[0, 0], items[1, 0], at, apart_even)
+        return carry
+
+    lax.fori_loop(0, members[items[0, 0]], open_item, 0)
     lax.fori_loop(0, total // 2, pair, 0)
     last = items[0, total - 1]
 
@@ -259,15 +305,20 @@
         scratch_shapes=[
             pltpu.VMEM((5 * chunks, 8, CHUNK), jnp.float32),
             pltpu.VMEM((len(OFFSETS), 4, size, LANES), jnp.float32),
+            pltpu.VMEM((len(OFFSETS), size, DEPTH), jnp.bfloat16),
+            pltpu.VMEM((5 * chunks, DEPTH, CHUNK), jnp.bfloat16),
             pltpu.VMEM((5, size, 3 * CHUNK), jnp.bfloat16),
             pltpu.VMEM((5, size, 3 * CHUNK), jnp.bfloat16),
             pltpu.VMEM((size, 3 * CHUNK), jnp.bfloat16),
             pltpu.VMEM((size, 3 * CHUNK), jnp.bfloat16),
+            pltpu.VMEM((5, size, CHUNK), jnp.float32),
+            pltpu.VMEM((5, size, CHUNK), jnp.float32),
             pltpu.VMEM((2, 3, size, CHUNK), jnp.float32),
             pltpu.VMEM((3, 8, CHUNK), jnp.float32),
             pltpu.VMEM((size, LANES), jnp.float32),
             pltpu.SMEM((5, 5), jnp.int32),
             pltpu.SMEM((2, 5 * chunks), jnp.int32),
+            pltpu.SMEM((5,), jnp.int32),
             pltpu.SMEM((5,), jnp.int32),
         ],
         compiler_params=pltpu.CompilerParams(vmem_limit_bytes=60 * 1024 * 1024),

time: 57.7 us -> 60.9 us (1.055)
  Pallas kernels: 30.1 us -> 33.3 us
    pallas_call x1, Pallas kernels: 30.1 us -> 33.3 us  [shards(): pl.pallas_call(functools.partial(row_kernel, lat_tiles=lat_tiles), out_sh...]
where the time goes in v2:
time: 60.9 us; the launch traced here: 60.4 us
  Pallas kernels  33.3 us (55%)
  starting transfers between devices  10.8 us (18%)
  waiting for transfers between devices  9.75 us (16%)
  other arithmetic  3.27 us (5%)
  local copies, waits for them, and re-layouts  1.88 us (3%)
  between operations  1.41 us (2%)
    pallas_call x1, Pallas kernels, shards(): pl.pallas_call(functools.partial(row_kernel, lat_tiles=lat_tiles), out_sh...  33.3 us
    ppermute x8, starting transfers between devices, cycled(): lax.ppermute(value, axis, [(i, (i + steps) % count) for i in range(count)])  10.8 us
    ppermute x8, waiting for transfers between devices, cycled(): lax.ppermute(value, axis, [(i, (i + steps) % count) for i in range(count)])  9.75 us
    unnamed x19, local copies, waits for them, and re-layouts  1.86 us
    mul x2, other arithmetic, place(): jnp.cos(latitude) * jnp.cos(longitude)  1.79 us
  transfers between devices with their start and end apart: 8, of which 5 were waited for; matrix products, arithmetic and copies ran while one was open for 0% of the time, Pallas kernels for 0%

profile of v2, /device:TPU:0, one launch (start us, length us, event | category | flops | bytes accessed | tf_op | source)
XLA Modules:
  0.0 60.4 jit_solution(7762821974512586676)
XLA Ops:
  1.3 0.7 %copy.9 = f32[1,1,3,1024]{3,2,1,0:T(4,128)S(1)} copy(f32[1,1,3,1024]{3,1,2,0:T(1,128)} %param.6) | data formatting | bytes 24576
  2.0 0.7 %fusion.1 = (f32[1,1,1,256]{3,2,1,0:T(1,128)S(1)}, f32[1,1,1,256]{3,2,1,0:T(1,128)S(1)}) fusion(f32[1,1,2,256]{3,2,1,0:T(2,128)} %param.7, f32[]{:T(128)S(6)} %convert_element_type.18), kind=kLoop, calls=%fused_computation.20 | loop fusion | flops 768 | bytes 3076 | tf_op jit(solution)/shard_map/cos | solution.py:50
  2.7 1.0 %multiply_bitcast_fusion.1 = (f32[1,1024]{1,0:T(1,128)S(1)}, f32[1,1024]{1,0:T(1,128)S(1)}, f32[1,1024]{1,0:T(1,128)S(1)}) fusion(f32[1,1,2,1024]{3,2,1,0:T(2,128)} %param.5, f32[]{:T(128)S(6)} %convert_element_type.19, f32[]{:T(128)S(6)} %convert_element_type.18), kind=kLoop, calls=%fused_computation.10 | loop fusion | flops 7168 | bytes 20488 | tf_op jit(solution)/shard_map/mul | solution.py:50
  3.8 0.8 %multiply_bitcast_fusion.3 = (f32[1,256]{1,0:T(1,128)S(1)}, f32[1,256]{1,0:T(1,128)S(1)}, f32[1,256]{1,0:T(1,128)S(1)}) fusion(f32[1,1,1,256]{3,2,1,0:T(1,128)S(1)} %get-tuple-element.6, f32[1,1,2,256]{3,2,1,0:T(2,128)} %param.7, f32[]{:T(128)S(6)} %convert_element_type.19, f32[1,1,1,256]{3,2,1,0:T(1,128)S(1)} %get-tuple-element.7), kind=kLoop, calls=%fused_computation.15 | loop fusion | flops 1024 | bytes 6148 | tf_op jit(solution)/shard_map/mul | solution.py:50
  4.6 0.7 %maximum_maximum_fusion.own_ref = f32[8,1280]{1,0:T(8,128)S(1)} fusion(f32[4,256]{1,0:T(4,128)S(1)} %broadcast_in_dim.14, f32[1,256]{1,0:T(1,128)} %bitcast.21, f32[3,256]{1,0:T(4,128)S(1)} %maximum_multiply_fusion.1, f32[1,1024]{1,0:T(1,128)S(1)} %broadcast_in_dim.13, f32[1,1024]{1,0:T(1,128)S(1)} %compare_convert_fusion, f32[3,1024]{1,0:T(4,128)S(1)} %bitcast.20, ...), kind=kLoop, calls=%fused_computation | loop fusion | flops 61440 | bytes 81920 | tf_op jit(solution)/shard_map/concatenate | solution.py:287
  5.3 5.1 %collective-permute-start.3 = (f32[8,1280]{1,0:T(8,128)S(1)}, f32[8,1280]{1,0:T(8,128)S(1)}, u32[]{:S(2)}, u32[]{:S(2)}) collective-permute-start(f32[8,1280]{1,0:T(8,128)S(1)} %maximum_maximum_fusion.own_ref), channel_id=1, source_target_pairs={{0,3},{1,0},{2,1},{3,2},{4,7},{5,4},{6,5},{7,6},{8,11},{9,8},{10,9... | collective-permute-start | bytes 122888 | tf_op jit(solution)/shard_map/ppermute | solution.py:41
  10.5 0.0 collective-permute-start.2
  10.5 1.6 %collective-permute-start.1 = (f32[8,1280]{1,0:T(8,128)S(1)}, f32[8,1280]{1,0:T(8,128)S(1)}, u32[]{:S(2)}, u32[]{:S(2)}) collective-permute-start(f32[8,1280]{1,0:T(8,128)S(1)} %maximum_maximum_fusion.own_ref), channel_id=1, source_target_pairs={{0,28},{4,0},{8,4},{12,8},{16,12},{20,16},{24,20},{28,24},{1,29},{... | collective-permute-start | bytes 122888 | tf_op jit(solution)/shard_map/ppermute | solution.py:41
  12.1 0.0 collective-permute-start
  12.1 0.1 collective-permute-done.3.east_ref
  12.1 4.1 %collective-permute-done.2.west_ref = f32[8,1280]{1,0:T(8,128)S(1)} collective-permute-done((f32[8,1280]{1,0:T(8,128)S(1)}, f32[8,1280]{1,0:T(8,128)S(1)}, u32[]{:S(2)}, u32[]{:S(2)}) %collective-permute-start.2) | collective-permute-done | bytes 40992 | tf_op jit(solution)/shard_map/ppermute | solution.py:41
  16.3 0.1 collective-permute-done.north_ref
  16.4 0.4 collective-permute-start.5
  16.8 0.1 collective-permute-start.4
  17.0 3.5 %collective-permute-start.7 = (f32[8,256]{1,0:T(8,128)S(1)}, f32[8,256]{1,0:T(8,128)S(1)}, u32[]{:S(2)}, u32[]{:S(2)}) collective-permute-start(f32[8,256]{1,0:T(8,128)S(1)} %slice.42), channel_id=1, source_target_pairs={{0,3},{1,0},{2,1},{3,2},{4,7},{5,4},{6,5},{7,6},{8,11},{9,8},{10,9... | collective-permute-start | bytes 24584 | tf_op jit(solution)/shard_map/ppermute | solution.py:41
  20.5 0.0 collective-permute-start.6
  20.5 1.4 %collective-permute-done.7.far_east_ref = f32[8,256]{1,0:T(8,128)S(1)} collective-permute-done((f32[8,256]{1,0:T(8,128)S(1)}, f32[8,256]{1,0:T(8,128)S(1)}, u32[]{:S(2)}, u32[]{:S(2)}) %collective-permute-start.7) | collective-permute-done | bytes 8224 | tf_op jit(solution)/shard_map/ppermute | solution.py:41
  21.9 4.1 %collective-permute-done.6.far_west_ref = f32[8,256]{1,0:T(8,128)S(1)} collective-permute-done((f32[8,256]{1,0:T(8,128)S(1)}, f32[8,256]{1,0:T(8,128)S(1)}, u32[]{:S(2)}, u32[]{:S(2)}) %collective-permute-start.6) | collective-permute-done | bytes 8224 | tf_op jit(solution)/shard_map/ppermute | solution.py:41
  26.0 0.0 collective-permute-done.5.far_south_ref
  26.0 0.0 collective-permute-done.4.far_north_ref
  26.0 0.5 copy-done.8
  26.6 0.0 copy-done.5
  26.6 0.6 copy-done.6
  27.2 33.3 %row_blocks.1 = (f32[13,256,256]{2,1,0:T(8,128)}, f32[1,256]{1,0:T(1,128)}) custom-call(f32[8,1280]{1,0:T(8,128)} %copy-done, f32[8,1280]{1,0:T(8,128)} %copy-done.4, f32[8,1280]{1,0:T(8,128)} %copy-done.3, f32[8,1280]{1,0:T(8,128)} %copy-done.2, f32[8,1280]{1,0:T(8,128)} %copy-done.1, f32[8,768]{1,0:T(8,128)} %copy-done.6, f32[8,768]{1,0:T(8,128)} %copy-done.5, ...), custom_call_target="tpu_custom_call" | custom-call | tf_op jit(solution)/shard_map/row_blocks/pallas_call | solution.py:297
  (26 shorter events, 0.1 us)
Async XLA Ops:
  5.3 20.7 %copy-start = (f32[8,1280]{1,0:T(8,128)}, f32[8,1280]{1,0:T(8,128)S(1)}, u32[]{:S(2)}) copy-start(f32[8,1280]{1,0:T(8,128)S(1)} %maximum_maximum_fusion.own_ref) | copy-start | bytes 122884
  5.3 6.8 %collective-permute-start.3 = (f32[8,1280]{1,0:T(8,128)S(1)}, f32[8,1280]{1,0:T(8,128)S(1)}, u32[]{:S(2)}, u32[]{:S(2)}) collective-permute-start(f32[8,1280]{1,0:T(8,128)S(1)} %maximum_maximum_fusion.own_ref), channel_id=1, source_target_pairs={{0,3},{1,0},{2,1},{3,2},{4,7},{5,4},{6,5},{7,6},{8,11},{9,8},{10,9... | collective-permute-start | bytes 122888 | tf_op jit(solution)/shard_map/ppermute | solution.py:41
  10.5 5.8 %collective-permute-start.2 = (f32[8,1280]{1,0:T(8,128)S(1)}, f32[8,1280]{1,0:T(8,128)S(1)}, u32[]{:S(2)}, u32[]{:S(2)}) collective-permute-start(f32[8,1280]{1,0:T(8,128)S(1)} %maximum_maximum_fusion.own_ref), channel_id=1, source_target_pairs={{0,1},{1,2},{2,3},{3,0},{4,5},{5,6},{6,7},{7,4},{8,9},{9,10},{10,1... | collective-permute-start | bytes 122888 | tf_op jit(solution)/shard_map/ppermute | solution.py:41
  10.5 5.8 %collective-permute-start.1 = (f32[8,1280]{1,0:T(8,128)S(1)}, f32[8,1280]{1,0:T(8,128)S(1)}, u32[]{:S(2)}, u32[]{:S(2)}) collective-permute-start(f32[8,1280]{1,0:T(8,128)S(1)} %maximum_maximum_fusion.own_ref), channel_id=1, source_target_pairs={{0,28},{4,0},{8,4},{12,8},{16,12},{20,16},{24,20},{28,24},{1,29},{... | collective-permute-start | bytes 122888 | tf_op jit(solution)/shard_map/ppermute | solution.py:41
  12.1 4.3 %collective-permute-start = (f32[8,1280]{1,0:T(8,128)S(1)}, f32[8,1280]{1,0:T(8,128)S(1)}, u32[]{:S(2)}, u32[]{:S(2)}) collective-permute-start(f32[8,1280]{1,0:T(8,128)S(1)} %maximum_maximum_fusion.own_ref), channel_id=1, source_target_pairs={{0,4},{4,8},{8,12},{12,16},{16,20},{20,24},{24,28},{28,0},{1,5},{5... | collective-permute-start | bytes 122888 | tf_op jit(solution)/shard_map/ppermute | solution.py:41
  12.1 13.9 %copy-start.1 = (f32[8,1280]{1,0:T(8,128)}, f32[8,1280]{1,0:T(8,128)S(1)}, u32[]{:S(2)}) copy-start(f32[8,1280]{1,0:T(8,128)S(1)} %collective-permute-done.3.east_ref) | copy-start | bytes 122884
  16.3 9.7 %copy-start.2 = (f32[8,1280]{1,0:T(8,128)}, f32[8,1280]{1,0:T(8,128)S(1)}, u32[]{:S(2)}) copy-start(f32[8,1280]{1,0:T(8,128)S(1)} %collective-permute-done.2.west_ref) | copy-start | bytes 122884
  16.3 9.7 %copy-start.3 = (f32[8,1280]{1,0:T(8,128)}, f32[8,1280]{1,0:T(8,128)S(1)}, u32[]{:S(2)}) copy-start(f32[8,1280]{1,0:T(8,128)S(1)} %collective-permute-done.1.south_ref) | copy-start | bytes 122884
  16.4 9.6 %copy-start.4 = (f32[8,1280]{1,0:T(8,128)}, f32[8,1280]{1,0:T(8,128)S(1)}, u32[]{:S(2)}) copy-start(f32[8,1280]{1,0:T(8,128)S(1)} %collective-permute-done.north_ref) | copy-start | bytes 122884
  16.4 9.6 %collective-permute-start.5 = (f32[8,768]{1,0:T(8,128)S(1)}, f32[8,768]{1,0:T(8,128)S(1)}, u32[]{:S(2)}, u32[]{:S(2)}) collective-permute-start(f32[8,768]{1,0:T(8,128)S(1)} %get-tuple-element.8), channel_id=1, source_target_pairs={{0,28},{4,0},{8,4},{12,8},{16,12},{20,16},{24,20},{28,24},{1,29},{... | collective-permute-start | bytes 73736 | tf_op jit(solution)/shard_map/ppermute | solution.py:41
  16.8 9.1 %collective-permute-start.4 = (f32[8,768]{1,0:T(8,128)S(1)}, f32[8,768]{1,0:T(8,128)S(1)}, u32[]{:S(2)}, u32[]{:S(2)}) collective-permute-start(f32[8,768]{1,0:T(8,128)S(1)} %get-tuple-element.9), channel_id=1, source_target_pairs={{0,4},{4,8},{8,12},{12,16},{16,20},{20,24},{24,28},{28,0},{1,5},{5... | collective-permute-start | bytes 73736 | tf_op jit(solution)/shard_map/ppermute | solution.py:41
  17.0 4.9 %collective-permute-start.7 = (f32[8,256]{1,0:T(8,128)S(1)}, f32[8,256]{1,0:T(8,128)S(1)}, u32[]{:S(2)}, u32[]{:S(2)}) collective-permute-start(f32[8,256]{1,0:T(8,128)S(1)} %slice.42), channel_id=1, source_target_pairs={{0,3},{1,0},{2,1},{3,2},{4,7},{5,4},{6,5},{7,6},{8,11},{9,8},{10,9... | collective-permute-start | bytes 24584 | tf_op jit(solution)/shard_map/ppermute | solution.py:41
  20.5 5.4 %collective-permute-start.6 = (f32[8,256]{1,0:T(8,128)S(1)}, f32[8,256]{1,0:T(8,128)S(1)}, u32[]{:S(2)}, u32[]{:S(2)}) collective-permute-start(f32[8,256]{1,0:T(8,128)S(1)} %slice.41), channel_id=1, source_target_pairs={{0,1},{1,2},{2,3},{3,0},{4,5},{5,6},{6,7},{7,4},{8,9},{9,10},{10,1... | collective-permute-start | bytes 24584 | tf_op jit(solution)/shard_map/ppermute | solution.py:41
  21.9 4.1 %copy-start.7 = (f32[8,256]{1,0:T(8,128)}, f32[8,256]{1,0:T(8,128)S(1)}, u32[]{:S(2)}) copy-start(f32[8,256]{1,0:T(8,128)S(1)} %collective-permute-done.7.far_east_ref) | copy-start | bytes 24580
  26.0 0.6 copy-start.8
  26.0 0.6 copy-start.5
  26.6 0.6 copy-start.6

commit v3 on v2

--- a/solution.py
+++ b/solution.py
@@ -29,7 +29,7 @@
 KERNEL_SCALE = 0.0001
 HUBER_EDGE = 0.8
 DEGREE = math.pi / 180.0
-CHUNK = 256
+CHUNK = 512
 ROWS = 16
 LANES = 128
 DEPTH = 64
@@ -90,6 +90,9 @@
     items,
     members,
     counts,
+    waits,
+    gram,
+    sent,
     *,
     lat_tiles,
 ):
@@ -168,7 +171,7 @@
 
             total = lax.fori_loop(0, jnp.where(members[tile] == full, counts[tile], 0), note, total)
 
-    gram_ref[...] = jnp.zeros_like(gram_ref)
+    gram[...] = jnp.zeros_like(gram)
     held_odd[...] = jnp.zeros_like(held_odd)
     weighted_odd[...] = jnp.zeros_like(weighted_odd)
     right[...] = jnp.zeros_like(right)
@@ -204,9 +207,13 @@
     def multiply(tile, at, held, weighted):
         target = table[tile, at]
         for half in (slice(0, size // 2), slice(size // 2, size)):
-            gram_ref[target, half] += lax.dot_general(
-                weighted[half], held[at], (((1,), (1,)), ((), ())), preferred_element_type=jnp.float32
+            gram[target, half] += lax.dot_general(
+                held[at, half], weighted[...], (((1,), (0,)), ((), ())), preferred_element_type=jnp.float32
             )
+
+    def flush(target):
+        gram[target] = gram[target].T
+        pltpu.make_async_copy(gram.at[target], gram_ref.at[target], sent.at[target]).start()
 
     def finish(chunk, weighted):
         present = obs[chunk, 6:7, :]
@@ -216,16 +223,17 @@
             weight = present * HUBER_EDGE / jnp.maximum(jnp.abs(residual), HUBER_EDGE)
             scale.append(jnp.broadcast_to(weight, (ROWS, CHUNK)))
             force.append(jnp.broadcast_to(weight * residual, (ROWS, CHUNK)))
-        for start in range(0, size, ROWS):
-            span = slice(start, start + ROWS)
-            pull = None
-            for c in range(3):
-                value = kept[0, c, span, :]
-                weighted[span, c * CHUNK : (c + 1) * CHUNK] = (scale[c] * value).astype(jnp.bfloat16)
-                part = force[c] * value
-                pull = part if pull is None else pull + part
+        for start in range(0, size, LANES):
+            span = slice(start, start + LANES)
             for lane in range(0, CHUNK, LANES):
-                right[span, :] += pull[:, lane : lane + LANES]
+                over = slice(lane, lane + LANES)
+                pull = right[span, :]
+                for c in range(3):
+                    value = kept[0, c, span, over]
+                    scaled = (jnp.broadcast_to(scale[c][:1, over], (LANES, LANES)) * value).astype(jnp.bfloat16)
+                    weighted[c * CHUNK + lane : c * CHUNK + lane + LANES, span] = scaled.T
+                    pull = pull + jnp.broadcast_to(force[c][:1, over], (LANES, LANES)) * value
+                right[span, :] = pull
 
     def advance(item, held, weighted, apart, held_before, weighted_before, apart_later):
         tile, chunk = items[0, item], items[1, item]
@@ -254,22 +262,61 @@
 
     lax.fori_loop(0, members[items[0, 0]], open_item, 0)
     lax.fori_loop(0, total // 2, pair, 0)
+    odd = total % 2 == 1
     last = items[0, total - 1]
 
-    def drain(at, carry):
-        multiply(last, at, held_odd, weighted_odd)
-        return carry
-
-    lax.fori_loop(0, members[last], drain, 0)
+    @pl.when(odd)
+    def _():
+        advance(total - 1, held_even, weighted_even, apart_even, held_odd, weighted_odd, apart_odd)
+
+    for target in range(len(OFFSETS)):
+        waits[target] = 0
+
+    def mark(at, carry):
+        waits[table[last, at]] = 1
+        return carry
+
+    lax.fori_loop(0, members[last], mark, 0)
 
     for target, offset in enumerate(OFFSETS):
         if offset[0] != 0:
 
             @pl.when(jnp.logical_not(inside(offset[0])))
             def _():
-                gram_ref[target] = jnp.zeros_like(gram_ref[target])
+                gram[target] = jnp.zeros_like(gram[target])
+
+    def early(target, carry):
+        @pl.when(waits[target] == 0)
+        def _():
+            flush(target)
+
+        return carry
+
+    lax.fori_loop(0, len(OFFSETS), early, 0)
+
+    def drain(held, weighted):
+        def block(at, carry):
+            multiply(last, at, held, weighted)
+            flush(table[last, at])
+            return carry
+
+        lax.fori_loop(0, members[last], block, 0)
+
+    @pl.when(odd)
+    def _():
+        drain(held_even, weighted_even)
+
+    @pl.when(jnp.logical_not(odd))
+    def _():
+        drain(held_odd, weighted_odd)
 
     rhs_ref[...] = jnp.sum(right[...].T, axis=0, keepdims=True)
+
+    def close(target, carry):
+        pltpu.make_async_copy(gram.at[target], gram_ref.at[target], sent.at[target]).wait()
+        return carry
+
+    lax.fori_loop(0, len(OFFSETS), close, 0)
 
 
 def shards(obs_frac, obs_field, dipole_frac, dipole_moment, obs_count):
@@ -301,7 +348,7 @@
             jax.ShapeDtypeStruct((1, size), jnp.float32),
         ),
         in_specs=[pl.BlockSpec(memory_space=pltpu.VMEM)] * 9,
-        out_specs=(pl.BlockSpec(memory_space=pltpu.VMEM), pl.BlockSpec(memory_space=pltpu.VMEM)),
+        out_specs=(pl.BlockSpec(memory_space=pl.ANY), pl.BlockSpec(memory_space=pltpu.VMEM)),
         scratch_shapes=[
             pltpu.VMEM((5 * chunks, 8, CHUNK), jnp.float32),
             pltpu.VMEM((len(OFFSETS), 4, size, LANES), jnp.float32),
@@ -309,8 +356,8 @@
             pltpu.VMEM((5 * chunks, DEPTH, CHUNK), jnp.bfloat16),
             pltpu.VMEM((5, size, 3 * CHUNK), jnp.bfloat16),
             pltpu.VMEM((5, size, 3 * CHUNK), jnp.bfloat16),
-            pltpu.VMEM((size, 3 * CHUNK), jnp.bfloat16),
-            pltpu.VMEM((size, 3 * CHUNK), jnp.bfloat16),
+            pltpu.VMEM((3 * CHUNK, size), jnp.bfloat16),
+            pltpu.VMEM((3 * CHUNK, size), jnp.bfloat16),
             pltpu.VMEM((5, size, CHUNK), jnp.float32),
             pltpu.VMEM((5, size, CHUNK), jnp.float32),
             pltpu.VMEM((2, 3, size, CHUNK), jnp.float32),
@@ -320,8 +367,11 @@
             pltpu.SMEM((2, 5 * chunks), jnp.int32),
             pltpu.SMEM((5,), jnp.int32),
             pltpu.SMEM((5,), jnp.int32),
+            pltpu.SMEM((len(OFFSETS),), jnp.int32),
+            pltpu.VMEM((len(OFFSETS), size, size), jnp.float32),
+            pltpu.SemaphoreType.DMA((len(OFFSETS),)),
         ],
-        compiler_params=pltpu.CompilerParams(vmem_limit_bytes=60 * 1024 * 1024),
+        compiler_params=pltpu.CompilerParams(vmem_limit_bytes=44 * 1024 * 1024),
         name="row_blocks",
     )(package, north, south, west, east, far_north, far_south, far_west, far_east)
     return (gram[None, None], rhs[None])

time: 60.9 us -> 52.8 us (0.87)
  Pallas kernels: 33.3 us -> 26.4 us
  local copies, waits for them, and re-layouts: 1.88 us -> 0.73 us
    pallas_call x1, Pallas kernels: 33.3 us -> 26.4 us  [shards(): pl.pallas_call(functools.partial(row_kernel, lat_tiles=lat_tiles), out_sh...]
    unnamed x19 -> x1, local copies, waits for them, and re-layouts: 1.86 us -> 0.71 us
where the time goes in v3:
time: 52.8 us; the launch traced here: 52.3 us
  Pallas kernels  26.4 us (50%)
  starting transfers between devices  10.8 us (20%)
  waiting for transfers between devices  9.77 us (19%)
  other arithmetic  3.27 us (6%)
  between operations  1.34 us (3%)
  local copies, waits for them, and re-layouts  0.73 us (1%)
    pallas_call x1, Pallas kernels, shards(): pl.pallas_call(functools.partial(row_kernel, lat_tiles=lat_tiles), out_sh...  26.4 us
    ppermute x8, starting transfers between devices, cycled(): lax.ppermute(value, axis, [(i, (i + steps) % count) for i in range(count)])  10.8 us
    ppermute x8, waiting for transfers between devices, cycled(): lax.ppermute(value, axis, [(i, (i + steps) % count) for i in range(count)])  9.77 us
    mul x2, other arithmetic, place(): jnp.cos(latitude) * jnp.cos(longitude)  1.79 us
  transfers between devices with their start and end apart: 8, of which 5 were waited for; matrix products, arithmetic and copies ran while one was open for 0% of the time, Pallas kernels for 0%

profile of v3, /device:TPU:0, one launch (start us, length us, event | category | flops | bytes accessed | tf_op | source)
XLA Modules:
  0.0 52.3 jit_solution(7893905495863950855)
XLA Ops:
  1.3 0.7 %copy.9 = f32[1,1,3,1024]{3,2,1,0:T(4,128)S(1)} copy(f32[1,1,3,1024]{3,1,2,0:T(1,128)} %param.6) | data formatting | bytes 24576
  2.0 0.7 %fusion.1 = (f32[1,1,1,256]{3,2,1,0:T(1,128)S(1)}, f32[1,1,1,256]{3,2,1,0:T(1,128)S(1)}) fusion(f32[1,1,2,256]{3,2,1,0:T(2,128)} %param.7, f32[]{:T(128)S(6)} %convert_element_type.18), kind=kLoop, calls=%fused_computation.20 | loop fusion | flops 768 | bytes 3076 | tf_op jit(solution)/shard_map/cos | solution.py:50
  2.7 1.0 %multiply_bitcast_fusion.1 = (f32[1,1024]{1,0:T(1,128)S(1)}, f32[1,1024]{1,0:T(1,128)S(1)}, f32[1,1024]{1,0:T(1,128)S(1)}) fusion(f32[1,1,2,1024]{3,2,1,0:T(2,128)} %param.5, f32[]{:T(128)S(6)} %convert_element_type.19, f32[]{:T(128)S(6)} %convert_element_type.18), kind=kLoop, calls=%fused_computation.10 | loop fusion | flops 7168 | bytes 20488 | tf_op jit(solution)/shard_map/mul | solution.py:50
  3.8 0.8 %multiply_bitcast_fusion.3 = (f32[1,256]{1,0:T(1,128)S(1)}, f32[1,256]{1,0:T(1,128)S(1)}, f32[1,256]{1,0:T(1,128)S(1)}) fusion(f32[1,1,1,256]{3,2,1,0:T(1,128)S(1)} %get-tuple-element.6, f32[1,1,2,256]{3,2,1,0:T(2,128)} %param.7, f32[]{:T(128)S(6)} %convert_element_type.19, f32[1,1,1,256]{3,2,1,0:T(1,128)S(1)} %get-tuple-element.7), kind=kLoop, calls=%fused_computation.15 | loop fusion | flops 1024 | bytes 6148 | tf_op jit(solution)/shard_map/mul | solution.py:50
  4.6 0.7 %maximum_maximum_fusion.own_ref = f32[8,1280]{1,0:T(8,128)S(1)} fusion(f32[4,256]{1,0:T(4,128)S(1)} %broadcast_in_dim.14, f32[1,256]{1,0:T(1,128)} %bitcast.21, f32[3,256]{1,0:T(4,128)S(1)} %maximum_multiply_fusion.1, f32[1,1024]{1,0:T(1,128)S(1)} %broadcast_in_dim.13, f32[1,1024]{1,0:T(1,128)S(1)} %compare_convert_fusion, f32[3,1024]{1,0:T(4,128)S(1)} %bitcast.20, ...), kind=kLoop, calls=%fused_computation | loop fusion | flops 61440 | bytes 81920 | tf_op jit(solution)/shard_map/concatenate | solution.py:334
  5.3 5.1 %collective-permute-start.3 = (f32[8,1280]{1,0:T(8,128)S(1)}, f32[8,1280]{1,0:T(8,128)S(1)}, u32[]{:S(2)}, u32[]{:S(2)}) collective-permute-start(f32[8,1280]{1,0:T(8,128)S(1)} %maximum_maximum_fusion.own_ref), channel_id=1, source_target_pairs={{0,3},{1,0},{2,1},{3,2},{4,7},{5,4},{6,5},{7,6},{8,11},{9,8},{10,9... | collective-permute-start | bytes 122888 | tf_op jit(solution)/shard_map/ppermute | solution.py:41
  10.4 0.0 collective-permute-start.2
  10.4 1.6 %collective-permute-start.1 = (f32[8,1280]{1,0:T(8,128)S(1)}, f32[8,1280]{1,0:T(8,128)S(1)}, u32[]{:S(2)}, u32[]{:S(2)}) collective-permute-start(f32[8,1280]{1,0:T(8,128)S(1)} %maximum_maximum_fusion.own_ref), channel_id=1, source_target_pairs={{0,28},{4,0},{8,4},{12,8},{16,12},{20,16},{24,20},{28,24},{1,29},{... | collective-permute-start | bytes 122888 | tf_op jit(solution)/shard_map/ppermute | solution.py:41
  12.1 0.0 collective-permute-start
  12.1 0.1 collective-permute-done.3.east_ref
  12.1 4.1 %collective-permute-done.2.west_ref = f32[8,1280]{1,0:T(8,128)S(1)} collective-permute-done((f32[8,1280]{1,0:T(8,128)S(1)}, f32[8,1280]{1,0:T(8,128)S(1)}, u32[]{:S(2)}, u32[]{:S(2)}) %collective-permute-start.2) | collective-permute-done | bytes 40992 | tf_op jit(solution)/shard_map/ppermute | solution.py:41
  16.2 0.0 collective-permute-done.1.south_ref
  16.3 0.1 collective-permute-done.north_ref
  16.4 0.4 collective-permute-start.5
  16.8 0.1 collective-permute-start.4
  16.9 3.5 %collective-permute-start.7 = (f32[8,256]{1,0:T(8,128)S(1)}, f32[8,256]{1,0:T(8,128)S(1)}, u32[]{:S(2)}, u32[]{:S(2)}) collective-permute-start(f32[8,256]{1,0:T(8,128)S(1)} %slice.42), channel_id=1, source_target_pairs={{0,3},{1,0},{2,1},{3,2},{4,7},{5,4},{6,5},{7,6},{8,11},{9,8},{10,9... | collective-permute-start | bytes 24584 | tf_op jit(solution)/shard_map/ppermute | solution.py:41
  20.4 0.0 collective-permute-start.6
  20.4 1.4 %collective-permute-done.7.far_east_ref = f32[8,256]{1,0:T(8,128)S(1)} collective-permute-done((f32[8,256]{1,0:T(8,128)S(1)}, f32[8,256]{1,0:T(8,128)S(1)}, u32[]{:S(2)}, u32[]{:S(2)}) %collective-permute-start.7) | collective-permute-done | bytes 8224 | tf_op jit(solution)/shard_map/ppermute | solution.py:41
  21.8 4.1 %collective-permute-done.6.far_west_ref = f32[8,256]{1,0:T(8,128)S(1)} collective-permute-done((f32[8,256]{1,0:T(8,128)S(1)}, f32[8,256]{1,0:T(8,128)S(1)}, u32[]{:S(2)}, u32[]{:S(2)}) %collective-permute-start.6) | collective-permute-done | bytes 8224 | tf_op jit(solution)/shard_map/ppermute | solution.py:41
  25.9 0.0 collective-permute-done.5.far_south_ref
  25.9 0.0 collective-permute-done.4.far_north_ref
  25.9 26.4 %row_blocks.1 = (f32[13,256,256]{2,1,0:T(8,128)}, f32[1,256]{1,0:T(1,128)}) custom-call(f32[8,1280]{1,0:T(8,128)S(1)} %maximum_maximum_fusion.own_ref, f32[8,1280]{1,0:T(8,128)S(1)} %collective-permute-done.north_ref, f32[8,1280]{1,0:T(8,128)S(1)} %collective-permute-done.1.south_ref, f32[8,1280]{1,0:T(8,128)S(1)} %collective-permute-done.2.west_ref, ...), custom_call_target="tpu_custom_call" | custom-call | tf_op jit(solution)/shard_map/row_blocks/pallas_call | solution.py:344
  (10 shorter events, 0.1 us)
Async XLA Ops:
  5.3 6.8 %collective-permute-start.3 = (f32[8,1280]{1,0:T(8,128)S(1)}, f32[8,1280]{1,0:T(8,128)S(1)}, u32[]{:S(2)}, u32[]{:S(2)}) collective-permute-start(f32[8,1280]{1,0:T(8,128)S(1)} %maximum_maximum_fusion.own_ref), channel_id=1, source_target_pairs={{0,3},{1,0},{2,1},{3,2},{4,7},{5,4},{6,5},{7,6},{8,11},{9,8},{10,9... | collective-permute-start | bytes 122888 | tf_op jit(solution)/shard_map/ppermute | solution.py:41
  10.4 5.8 %collective-permute-start.2 = (f32[8,1280]{1,0:T(8,128)S(1)}, f32[8,1280]{1,0:T(8,128)S(1)}, u32[]{:S(2)}, u32[]{:S(2)}) collective-permute-start(f32[8,1280]{1,0:T(8,128)S(1)} %maximum_maximum_fusion.own_ref), channel_id=1, source_target_pairs={{0,1},{1,2},{2,3},{3,0},{4,5},{5,6},{6,7},{7,4},{8,9},{9,10},{10,1... | collective-permute-start | bytes 122888 | tf_op jit(solution)/shard_map/ppermute | solution.py:41
  10.4 5.8 %collective-permute-start.1 = (f32[8,1280]{1,0:T(8,128)S(1)}, f32[8,1280]{1,0:T(8,128)S(1)}, u32[]{:S(2)}, u32[]{:S(2)}) collective-permute-start(f32[8,1280]{1,0:T(8,128)S(1)} %maximum_maximum_fusion.own_ref), channel_id=1, source_target_pairs={{0,28},{4,0},{8,4},{12,8},{16,12},{20,16},{24,20},{28,24},{1,29},{... | collective-permute-start | bytes 122888 | tf_op jit(solution)/shard_map/ppermute | solution.py:41
  12.1 4.3 %collective-permute-start = (f32[8,1280]{1,0:T(8,128)S(1)}, f32[8,1280]{1,0:T(8,128)S(1)}, u32[]{:S(2)}, u32[]{:S(2)}) collective-permute-start(f32[8,1280]{1,0:T(8,128)S(1)} %maximum_maximum_fusion.own_ref), channel_id=1, source_target_pairs={{0,4},{4,8},{8,12},{12,16},{16,20},{20,24},{24,28},{28,0},{1,5},{5... | collective-permute-start | bytes 122888 | tf_op jit(solution)/shard_map/ppermute | solution.py:41
  16.4 9.5 %collective-permute-start.5 = (f32[8,768]{1,0:T(8,128)S(1)}, f32[8,768]{1,0:T(8,128)S(1)}, u32[]{:S(2)}, u32[]{:S(2)}) collective-permute-start(f32[8,768]{1,0:T(8,128)S(1)} %get-tuple-element.8), channel_id=1, source_target_pairs={{0,28},{4,0},{8,4},{12,8},{16,12},{20,16},{24,20},{28,24},{1,29},{... | collective-permute-start | bytes 73736 | tf_op jit(solution)/shard_map/ppermute | solution.py:41
  16.8 9.1 %collective-permute-start.4 = (f32[8,768]{1,0:T(8,128)S(1)}, f32[8,768]{1,0:T(8,128)S(1)}, u32[]{:S(2)}, u32[]{:S(2)}) collective-permute-start(f32[8,768]{1,0:T(8,128)S(1)} %get-tuple-element.9), channel_id=1, source_target_pairs={{0,4},{4,8},{8,12},{12,16},{16,20},{20,24},{24,28},{28,0},{1,5},{5... | collective-permute-start | bytes 73736 | tf_op jit(solution)/shard_map/ppermute | solution.py:41
  16.9 4.9 %collective-permute-start.7 = (f32[8,256]{1,0:T(8,128)S(1)}, f32[8,256]{1,0:T(8,128)S(1)}, u32[]{:S(2)}, u32[]{:S(2)}) collective-permute-start(f32[8,256]{1,0:T(8,128)S(1)} %slice.42), channel_id=1, source_target_pairs={{0,3},{1,0},{2,1},{3,2},{4,7},{5,4},{6,5},{7,6},{8,11},{9,8},{10,9... | collective-permute-start | bytes 24584 | tf_op jit(solution)/shard_map/ppermute | solution.py:41
  20.4 5.4 %collective-permute-start.6 = (f32[8,256]{1,0:T(8,128)S(1)}, f32[8,256]{1,0:T(8,128)S(1)}, u32[]{:S(2)}, u32[]{:S(2)}) collective-permute-start(f32[8,256]{1,0:T(8,128)S(1)} %slice.41), channel_id=1, source_target_pairs={{0,1},{1,2},{2,3},{3,0},{4,5},{5,6},{6,7},{7,4},{8,9},{9,10},{10,1... | collective-permute-start | bytes 24584 | tf_op jit(solution)/shard_map/ppermute | solution.py:41

commit v4 on v3

--- a/solution.py
+++ b/solution.py
@@ -193,9 +193,10 @@
             inverse = lax.rsqrt(apart[at, span, :])
             inverse_square = inverse * inverse
             cube = inverse_square * inverse
-            along = near * inverse_square - 1.5
+            along = cube * (near * inverse_square - 1.5)
+            across = along + cube
             for c in range(3):
-                value = cube * (along * (point[c] - wide[c]) - wide[c])
+                value = along * point[c] - across * wide[c]
                 held[at, span, c * CHUNK : (c + 1) * CHUNK] = value.astype(jnp.bfloat16)
                 kept[spare, c, span, :] = value
                 part = value * wide[3]
@@ -338,8 +339,8 @@
     east = cycled(package, "lon", -1)
     far_north = cycled(jnp.concatenate([north[:, slots:], west[:, slots:], east[:, slots:]], 1), "lat", 1)
     far_south = cycled(jnp.concatenate([south[:, slots:], west[:, slots:], east[:, slots:]], 1), "lat", -1)
-    far_west = cycled(west[:, slots:], "lon", 1)
-    far_east = cycled(east[:, slots:], "lon", -1)
+    far_west = cycled(dipoles, "lon", 2)
+    far_east = far_west if lon_tiles == 4 else cycled(dipoles, "lon", -2)
     chunks = slots // CHUNK
     gram, rhs = pl.pallas_call(
         functools.partial(row_kernel, lat_tiles=lat_tiles),

time: 52.8 us -> 47.9 us (0.907)
  starting transfers between devices: 10.8 us -> 7.98 us
  waiting for transfers between devices: 9.77 us -> 8.16 us
  Pallas kernels: 26.4 us -> 25.3 us
  other arithmetic: 3.27 us -> 3.96 us
    ppermute x8 -> x7, starting transfers between devices: 10.8 us -> 7.98 us  [cycled(): lax.ppermute(value, axis, [(i, (i + steps) % count) for i in range(count)])]
    ppermute x8 -> x7, waiting for transfers between devices: 9.77 us -> 8.16 us  [cycled(): lax.ppermute(value, axis, [(i, (i + steps) % count) for i in range(count)])]
    pallas_call x1, Pallas kernels: 26.4 us -> 25.3 us  [shards(): pl.pallas_call(functools.partial(row_kernel, lat_tiles=lat_tiles), out_sh...]
    concatenate x0 -> x1, other arithmetic: none -> 0.69 us  [shards(): jnp.concatenate([source, dipole_moment[0, 0][None], jnp.zeros((4, size),...]
  transfers between devices with their start and end apart: 8 -> 7, of which waited for: 5 -> 4; matrix products, arithmetic and copies ran while one was open for 0% -> 1% of each run, Pallas kernels for 0% -> 0%
where the time goes in v4:
time: 47.9 us; the launch traced here: 47.4 us
  Pallas kernels  25.3 us (53%)
  waiting for transfers between devices  8.16 us (17%)
  starting transfers between devices  7.98 us (17%)
  other arithmetic  3.96 us (8%)
  between operations  1.34 us (3%)
  local copies, waits for them, and re-layouts  0.73 us (2%)
    pallas_call x1, Pallas kernels, shards(): pl.pallas_call(functools.partial(row_kernel, lat_tiles=lat_tiles), out_sh...  25.3 us
    ppermute x7, waiting for transfers between devices, cycled(): lax.ppermute(value, axis, [(i, (i + steps) % count) for i in range(count)])  8.16 us
    ppermute x7, starting transfers between devices, cycled(): lax.ppermute(value, axis, [(i, (i + steps) % count) for i in range(count)])  7.98 us
    mul x2, other arithmetic, place(): jnp.cos(latitude) * jnp.cos(longitude)  1.79 us
  transfers between devices with their start and end apart: 7, of which 4 were waited for; matrix products, arithmetic and copies ran while one was open for 1% of the time, Pallas kernels for 0%

profile of v4, /device:TPU:0, one launch (start us, length us, event | category | flops | bytes accessed | tf_op | source)
XLA Modules:
  0.0 47.4 jit_solution(4863448447909837393)
XLA Ops:
  1.3 0.7 %copy.9 = f32[1,1,3,1024]{3,2,1,0:T(4,128)S(1)} copy(f32[1,1,3,1024]{3,1,2,0:T(1,128)} %param.6) | data formatting | bytes 24576
  2.0 0.7 %fusion.1 = (f32[1,1,1,256]{3,2,1,0:T(1,128)S(1)}, f32[1,1,1,256]{3,2,1,0:T(1,128)S(1)}) fusion(f32[1,1,2,256]{3,2,1,0:T(2,128)} %param.7, f32[]{:T(128)S(6)} %convert_element_type.18), kind=kLoop, calls=%fused_computation.21 | loop fusion | flops 768 | bytes 3076 | tf_op jit(solution)/shard_map/cos | solution.py:50
  2.7 1.0 %multiply_bitcast_fusion.1 = (f32[1,1024]{1,0:T(1,128)S(1)}, f32[1,1024]{1,0:T(1,128)S(1)}, f32[1,1024]{1,0:T(1,128)S(1)}) fusion(f32[1,1,2,1024]{3,2,1,0:T(2,128)} %param.5, f32[]{:T(128)S(6)} %convert_element_type.19, f32[]{:T(128)S(6)} %convert_element_type.18), kind=kLoop, calls=%fused_computation.11 | loop fusion | flops 7168 | bytes 20488 | tf_op jit(solution)/shard_map/mul | solution.py:50
  3.8 0.8 %multiply_bitcast_fusion.3 = (f32[1,256]{1,0:T(1,128)S(1)}, f32[1,256]{1,0:T(1,128)S(1)}, f32[1,256]{1,0:T(1,128)S(1)}) fusion(f32[1,1,1,256]{3,2,1,0:T(1,128)S(1)} %get-tuple-element.6, f32[1,1,2,256]{3,2,1,0:T(2,128)} %param.7, f32[]{:T(128)S(6)} %convert_element_type.19, f32[1,1,1,256]{3,2,1,0:T(1,128)S(1)} %get-tuple-element.7), kind=kLoop, calls=%fused_computation.16 | loop fusion | flops 1024 | bytes 6148 | tf_op jit(solution)/shard_map/mul | solution.py:50
  4.6 0.7 %maximum_maximum_fusion.own_ref = f32[8,1280]{1,0:T(8,128)S(1)} fusion(f32[4,256]{1,0:T(4,128)S(1)} %broadcast_in_dim.14, f32[1,256]{1,0:T(1,128)} %bitcast.21, f32[3,256]{1,0:T(4,128)S(1)} %maximum_multiply_fusion.1, f32[1,1024]{1,0:T(1,128)S(1)} %broadcast_in_dim.13, f32[1,1024]{1,0:T(1,128)S(1)} %compare_convert_fusion, f32[3,1024]{1,0:T(4,128)S(1)} %bitcast.20, ...), kind=kLoop, calls=%fused_computation | loop fusion | flops 61440 | bytes 81920 | tf_op jit(solution)/shard_map/concatenate | solution.py:335
  5.3 5.1 %collective-permute-start.3 = (f32[8,1280]{1,0:T(8,128)S(1)}, f32[8,1280]{1,0:T(8,128)S(1)}, u32[]{:S(2)}, u32[]{:S(2)}) collective-permute-start(f32[8,1280]{1,0:T(8,128)S(1)} %maximum_maximum_fusion.own_ref), channel_id=1, source_target_pairs={{0,3},{1,0},{2,1},{3,2},{4,7},{5,4},{6,5},{7,6},{8,11},{9,8},{10,9... | collective-permute-start | bytes 122888 | tf_op jit(solution)/shard_map/ppermute | solution.py:41
  10.4 0.0 collective-permute-start.2
  10.4 1.6 %collective-permute-start.1 = (f32[8,1280]{1,0:T(8,128)S(1)}, f32[8,1280]{1,0:T(8,128)S(1)}, u32[]{:S(2)}, u32[]{:S(2)}) collective-permute-start(f32[8,1280]{1,0:T(8,128)S(1)} %maximum_maximum_fusion.own_ref), channel_id=1, source_target_pairs={{0,28},{4,0},{8,4},{12,8},{16,12},{20,16},{24,20},{28,24},{1,29},{... | collective-permute-start | bytes 122888 | tf_op jit(solution)/shard_map/ppermute | solution.py:41
  12.1 0.0 collective-permute-start
  12.1 0.1 collective-permute-done.3.east_ref
  12.1 4.1 %collective-permute-done.2.west_ref = f32[8,1280]{1,0:T(8,128)S(1)} collective-permute-done((f32[8,1280]{1,0:T(8,128)S(1)}, f32[8,1280]{1,0:T(8,128)S(1)}, u32[]{:S(2)}, u32[]{:S(2)}) %collective-permute-start.2) | collective-permute-done | bytes 40992 | tf_op jit(solution)/shard_map/ppermute | solution.py:41
  16.2 0.0 collective-permute-done.1.south_ref
  16.3 0.1 collective-permute-done.north_ref
  16.4 0.4 collective-permute-start.5
  16.8 0.1 collective-permute-start.4
  16.9 0.7 %pad_maximum_fusion.4 = f32[8,256]{1,0:T(8,128)S(1)} fusion(f32[4,256]{1,0:T(4,128)S(1)} %broadcast_in_dim.14, f32[1,256]{1,0:T(1,128)} %bitcast.22, f32[3,256]{1,0:T(4,128)S(1)} %maximum_multiply_fusion.1), kind=kLoop, calls=%fused_computation.8 | loop fusion | flops 4096 | bytes 16384 | tf_op jit(solution)/shard_map/concatenate | solution.py:334
  17.6 0.7 %collective-permute-start.6 = (f32[8,256]{1,0:T(8,128)S(1)}, f32[8,256]{1,0:T(8,128)S(1)}, u32[]{:S(2)}, u32[]{:S(2)}) collective-permute-start(f32[8,256]{1,0:T(8,128)S(1)} %pad_maximum_fusion.4), channel_id=1, source_target_pairs={{0,2},{1,3},{2,0},{3,1},{4,6},{5,7},{6,4},{7,5},{8,10},{9,11},{10,... | collective-permute-start | bytes 24584 | tf_op jit(solution)/shard_map/ppermute | solution.py:41
  18.3 3.8 %collective-permute-done.6.far_west_ref.far_east_ref = f32[8,256]{1,0:T(8,128)S(1)} collective-permute-done((f32[8,256]{1,0:T(8,128)S(1)}, f32[8,256]{1,0:T(8,128)S(1)}, u32[]{:S(2)}, u32[]{:S(2)}) %collective-permute-start.6) | collective-permute-done | bytes 8224 | tf_op jit(solution)/shard_map/ppermute | solution.py:41
  22.2 0.0 collective-permute-done.5.far_south_ref
  22.2 0.0 collective-permute-done.4.far_north_ref
  22.2 25.3 %row_blocks.1 = (f32[13,256,256]{2,1,0:T(8,128)}, f32[1,256]{1,0:T(1,128)}) custom-call(f32[8,1280]{1,0:T(8,128)S(1)} %maximum_maximum_fusion.own_ref, f32[8,1280]{1,0:T(8,128)S(1)} %collective-permute-done.north_ref, f32[8,1280]{1,0:T(8,128)S(1)} %collective-permute-done.1.south_ref, f32[8,1280]{1,0:T(8,128)S(1)} %collective-permute-done.2.west_ref, ...), custom_call_target="tpu_custom_call" | custom-call | tf_op jit(solution)/shard_map/row_blocks/pallas_call | solution.py:345
  (10 shorter events, 0.1 us)
Async XLA Ops:
  5.3 6.8 %collective-permute-start.3 = (f32[8,1280]{1,0:T(8,128)S(1)}, f32[8,1280]{1,0:T(8,128)S(1)}, u32[]{:S(2)}, u32[]{:S(2)}) collective-permute-start(f32[8,1280]{1,0:T(8,128)S(1)} %maximum_maximum_fusion.own_ref), channel_id=1, source_target_pairs={{0,3},{1,0},{2,1},{3,2},{4,7},{5,4},{6,5},{7,6},{8,11},{9,8},{10,9... | collective-permute-start | bytes 122888 | tf_op jit(solution)/shard_map/ppermute | solution.py:41
  10.4 5.8 %collective-permute-start.2 = (f32[8,1280]{1,0:T(8,128)S(1)}, f32[8,1280]{1,0:T(8,128)S(1)}, u32[]{:S(2)}, u32[]{:S(2)}) collective-permute-start(f32[8,1280]{1,0:T(8,128)S(1)} %maximum_maximum_fusion.own_ref), channel_id=1, source_target_pairs={{0,1},{1,2},{2,3},{3,0},{4,5},{5,6},{6,7},{7,4},{8,9},{9,10},{10,1... | collective-permute-start | bytes 122888 | tf_op jit(solution)/shard_map/ppermute | solution.py:41
  10.4 5.8 %collective-permute-start.1 = (f32[8,1280]{1,0:T(8,128)S(1)}, f32[8,1280]{1,0:T(8,128)S(1)}, u32[]{:S(2)}, u32[]{:S(2)}) collective-permute-start(f32[8,1280]{1,0:T(8,128)S(1)} %maximum_maximum_fusion.own_ref), channel_id=1, source_target_pairs={{0,28},{4,0},{8,4},{12,8},{16,12},{20,16},{24,20},{28,24},{1,29},{... | collective-permute-start | bytes 122888 | tf_op jit(solution)/shard_map/ppermute | solution.py:41
  12.1 4.3 %collective-permute-start = (f32[8,1280]{1,0:T(8,128)S(1)}, f32[8,1280]{1,0:T(8,128)S(1)}, u32[]{:S(2)}, u32[]{:S(2)}) collective-permute-start(f32[8,1280]{1,0:T(8,128)S(1)} %maximum_maximum_fusion.own_ref), channel_id=1, source_target_pairs={{0,4},{4,8},{8,12},{12,16},{16,20},{20,24},{24,28},{28,0},{1,5},{5... | collective-permute-start | bytes 122888 | tf_op jit(solution)/shard_map/ppermute | solution.py:41
  16.4 5.8 %collective-permute-start.5 = (f32[8,768]{1,0:T(8,128)S(1)}, f32[8,768]{1,0:T(8,128)S(1)}, u32[]{:S(2)}, u32[]{:S(2)}) collective-permute-start(f32[8,768]{1,0:T(8,128)S(1)} %get-tuple-element.8), channel_id=1, source_target_pairs={{0,28},{4,0},{8,4},{12,8},{16,12},{20,16},{24,20},{28,24},{1,29},{... | collective-permute-start | bytes 73736 | tf_op jit(solution)/shard_map/ppermute | solution.py:41
  16.8 5.4 %collective-permute-start.4 = (f32[8,768]{1,0:T(8,128)S(1)}, f32[8,768]{1,0:T(8,128)S(1)}, u32[]{:S(2)}, u32[]{:S(2)}) collective-permute-start(f32[8,768]{1,0:T(8,128)S(1)} %get-tuple-element.9), channel_id=1, source_target_pairs={{0,4},{4,8},{8,12},{12,16},{16,20},{20,24},{24,28},{28,0},{1,5},{5... | collective-permute-start | bytes 73736 | tf_op jit(solution)/shard_map/ppermute | solution.py:41
  17.6 4.6 %collective-permute-start.6 = (f32[8,256]{1,0:T(8,128)S(1)}, f32[8,256]{1,0:T(8,128)S(1)}, u32[]{:S(2)}, u32[]{:S(2)}) collective-permute-start(f32[8,256]{1,0:T(8,128)S(1)} %pad_maximum_fusion.4), channel_id=1, source_target_pairs={{0,2},{1,3},{2,0},{3,1},{4,6},{5,7},{6,4},{7,5},{8,10},{9,11},{10,... | collective-permute-start | bytes 24584 | tf_op jit(solution)/shard_map/ppermute | solution.py:41

commit v5 on v4

--- a/solution.py
+++ b/solution.py
@@ -41,17 +41,46 @@
     return lax.ppermute(value, axis, [(i, (i + steps) % count) for i in range(count)])
 
 
-def place(fraction, lat_index, lon_index, lat_tiles, lon_tiles, radius):
+def pack_kernel(
+    obs_frac_ref, obs_field_ref, dipole_frac_ref, moment_ref, obs_count, package, dipoles,
+    obs_frac, obs_field, dipole_frac, moment, landed, *, lat_tiles, lon_tiles,
+):
+    loads = [
+        pltpu.make_async_copy(source, target, landed.at[at])
+        for at, (source, target) in enumerate(
+            ((obs_frac_ref, obs_frac), (obs_field_ref, obs_field), (dipole_frac_ref, dipole_frac), (moment_ref, moment))
+        )
+    ]
+    for load in loads:
+        load.start()
+    for load in loads:
+        load.wait()
+    lat_index = lax.axis_index("lat").astype(jnp.float32)
+    lon_index = lax.axis_index("lon").astype(jnp.float32)
     lat_span = 160.0 * DEGREE / lat_tiles
-    latitude = -80.0 * DEGREE + (lat_index + fraction[0]) * lat_span
-    longitude = (lon_index + fraction[1]) * (2.0 * math.pi / lon_tiles)
-    return radius * jnp.stack(
-        [
-            jnp.cos(latitude) * jnp.cos(longitude),
-            jnp.cos(latitude) * jnp.sin(longitude),
-            jnp.sin(latitude),
+    lon_span = 2.0 * math.pi / lon_tiles
+
+    def place(fraction, radius):
+        row = lax.broadcasted_iota(jnp.int32, fraction.shape, 0)
+        angle = jnp.where(row == 0, -80.0 * DEGREE + (lat_index + fraction) * lat_span, (lon_index + fraction) * lon_span)
+        cosine, sine = jnp.cos(angle), jnp.sin(angle)
+        return [
+            radius * (cosine[0:1] * cosine[1:2]),
+            radius * (cosine[0:1] * sine[1:2]),
+            radius * sine[0:1],
         ]
-    )
+
+    slots, size = obs_frac.shape[1], dipole_frac.shape[1]
+    for row, value in enumerate(place(obs_frac[...], OBS_RADIUS)):
+        package[row : row + 1, :slots] = value
+    package[3:6, :slots] = obs_field[...]
+    index = lax.broadcasted_iota(jnp.int32, (1, slots), 1)
+    package[6:7, :slots] = (index < obs_count[0, 0]).astype(jnp.float32)
+    package[7:8, :slots] = jnp.zeros((1, slots), jnp.float32)
+    rows = place(dipole_frac[...], SOURCE_RADIUS) + [moment[...], jnp.zeros((4, size), jnp.float32)]
+    filled = jnp.concatenate(rows, 0)
+    package[:, slots:] = filled
+    dipoles[...] = filled
 
 
 def split(values):
@@ -120,6 +149,7 @@
     parts = lax.broadcasted_iota(jnp.int32, (DEPTH, 4 * LANES), 1) // LANES
     picks = ((picks == parts) | (picks == parts + 16) | (picks == parts + 32)).astype(jnp.bfloat16)
     row_of = lax.broadcasted_iota(jnp.int32, (8, size), 0)
+    right[...] = jnp.zeros_like(right)
     for target, offset in enumerate(OFFSETS):
         ref, start = sources[offset]
         values = ref[:, start : start + size]
@@ -129,6 +159,7 @@
         ones = jnp.ones_like(values)
         stacked = jnp.concatenate([high, high, middle, high, low, middle, ones, jnp.zeros_like(values)], 0)
         upright = stacked.T.astype(jnp.bfloat16)
+        gram[target] = jnp.zeros((size, size), jnp.float32)
         tall[target] = upright
         wide = lax.dot_general(upright, picks, (((1,), (0,)), ((), ())), preferred_element_type=jnp.float32)
         for part in range(4):
@@ -171,10 +202,6 @@
 
             total = lax.fori_loop(0, jnp.where(members[tile] == full, counts[tile], 0), note, total)
 
-    gram[...] = jnp.zeros_like(gram)
-    held_odd[...] = jnp.zeros_like(held_odd)
-    weighted_odd[...] = jnp.zeros_like(weighted_odd)
-    right[...] = jnp.zeros_like(right)
 
     def separate(tile, chunk, at, apart):
         apart[at] = lax.dot_general(
@@ -205,8 +232,7 @@
         for c in range(3):
             predicted[c] = sums[c]
 
-    def multiply(tile, at, held, weighted):
-        target = table[tile, at]
+    def multiply(target, at, held, weighted):
         for half in (slice(0, size // 2), slice(size // 2, size)):
             gram[target, half] += lax.dot_general(
                 held[at, half], weighted[...], (((1,), (0,)), ((), ())), preferred_element_type=jnp.float32
@@ -236,6 +262,28 @@
                     pull = pull + jnp.broadcast_to(force[c][:1, over], (LANES, LANES)) * value
                 right[span, :] = pull
 
+    last = items[0, total - 1]
+    twice = items[0, jnp.maximum(total - 2, 0)] == last
+
+    def clear(target, carry):
+        waits[target] = 0
+        return carry
+
+    lax.fori_loop(0, len(OFFSETS), clear, 0)
+
+    def mark(at, carry):
+        waits[table[last, at]] = 1
+        return carry
+
+    lax.fori_loop(0, members[last], mark, 0)
+
+    def early(target, carry):
+        @pl.when(waits[target] == 0)
+        def _():
+            flush(target)
+
+        return carry
+
     def advance(item, held, weighted, apart, held_before, weighted_before, apart_later):
         tile, chunk = items[0, item], items[1, item]
         before = items[0, jnp.maximum(item - 1, 0)]
@@ -243,9 +291,14 @@
         later, later_chunk = items[0, after], items[1, after]
         predicted[...] = jnp.zeros_like(predicted)
 
+        @pl.when((item == total - 1) & twice)
+        def _():
+            lax.fori_loop(0, len(OFFSETS), early, 0)
+
         def block(at, carry):
             separate(later, later_chunk, at, apart_later)
-            multiply(before, at, held_before, weighted_before)
+            target = jnp.where(item == 0, len(OFFSETS), table[before, at])
+            multiply(target, at, held_before, weighted_before)
             evaluate(tile, chunk, at, held, apart)
             return carry
 
@@ -264,40 +317,18 @@
     lax.fori_loop(0, members[items[0, 0]], open_item, 0)
     lax.fori_loop(0, total // 2, pair, 0)
     odd = total % 2 == 1
-    last = items[0, total - 1]
 
     @pl.when(odd)
     def _():
         advance(total - 1, held_even, weighted_even, apart_even, held_odd, weighted_odd, apart_odd)
 
-    for target in range(len(OFFSETS)):
-        waits[target] = 0
-
-    def mark(at, carry):
-        waits[table[last, at]] = 1
-        return carry
-
-    lax.fori_loop(0, members[last], mark, 0)
-
-    for target, offset in enumerate(OFFSETS):
-        if offset[0] != 0:
-
-            @pl.when(jnp.logical_not(inside(offset[0])))
-            def _():
-                gram[target] = jnp.zeros_like(gram[target])
-
-    def early(target, carry):
-        @pl.when(waits[target] == 0)
-        def _():
-            flush(target)
-
-        return carry
-
-    lax.fori_loop(0, len(OFFSETS), early, 0)
+    @pl.when(jnp.logical_not(twice))
+    def _():
+        lax.fori_loop(0, len(OFFSETS), early, 0)
 
     def drain(held, weighted):
         def block(at, carry):
-            multiply(last, at, held, weighted)
+            multiply(table[last, at], at, held, weighted)
             flush(table[last, at])
             return carry
 
@@ -323,24 +354,35 @@
 def shards(obs_frac, obs_field, dipole_frac, dipole_moment, obs_count):
     lat_tiles = lax.axis_size("lat")
     lon_tiles = lax.axis_size("lon")
-    lat_index = lax.axis_index("lat")
-    lon_index = lax.axis_index("lon")
     size = dipole_frac.shape[3]
     slots = obs_frac.shape[3]
-    source = place(dipole_frac[0, 0], lat_index, lon_index, lat_tiles, lon_tiles, SOURCE_RADIUS)
-    points = place(obs_frac[0, 0], lat_index, lon_index, lat_tiles, lon_tiles, OBS_RADIUS)
-    present = (jnp.arange(slots, dtype=jnp.int32) < obs_count[0, 0]).astype(jnp.float32)
-    observed = jnp.concatenate([points, obs_field[0, 0], present[None], jnp.zeros((1, slots), jnp.float32)], 0)
-    dipoles = jnp.concatenate([source, dipole_moment[0, 0][None], jnp.zeros((4, size), jnp.float32)], 0)
-    package = jnp.concatenate([observed, dipoles], 1)
+    package, dipoles = pl.pallas_call(
+        functools.partial(pack_kernel, lat_tiles=lat_tiles, lon_tiles=lon_tiles),
+        out_shape=(
+            jax.ShapeDtypeStruct((8, slots + size), jnp.float32),
+            jax.ShapeDtypeStruct((8, size), jnp.float32),
+        ),
+        in_specs=[pl.BlockSpec(memory_space=pltpu.HBM)] * 4 + [pl.BlockSpec(memory_space=pltpu.SMEM)],
+        out_specs=(pl.BlockSpec(memory_space=pltpu.VMEM), pl.BlockSpec(memory_space=pltpu.VMEM)),
+        scratch_shapes=[
+            pltpu.VMEM((2, slots), jnp.float32),
+            pltpu.VMEM((3, slots), jnp.float32),
+            pltpu.VMEM((2, size), jnp.float32),
+            pltpu.VMEM((1, size), jnp.float32),
+            pltpu.SemaphoreType.DMA((4,)),
+        ],
+        compiler_params=pltpu.CompilerParams(vmem_limit_bytes=4 * 1024 * 1024),
+        name="pack_tile",
+    )(obs_frac[0, 0], obs_field[0, 0], dipole_frac[0, 0], dipole_moment[0], obs_count)
     north = cycled(package, "lat", 1)
     south = cycled(package, "lat", -1)
+    far_west = cycled(dipoles, "lon", 2)
+    far_east = far_west if lon_tiles == 4 else cycled(dipoles, "lon", -2)
     west = cycled(package, "lon", 1)
     east = cycled(package, "lon", -1)
+    north, south, far_west, far_east, west, east = lax.optimization_barrier((north, south, far_west, far_east, west, east))
     far_north = cycled(jnp.concatenate([north[:, slots:], west[:, slots:], east[:, slots:]], 1), "lat", 1)
     far_south = cycled(jnp.concatenate([south[:, slots:], west[:, slots:], east[:, slots:]], 1), "lat", -1)
-    far_west = cycled(dipoles, "lon", 2)
-    far_east = far_west if lon_tiles == 4 else cycled(dipoles, "lon", -2)
     chunks = slots // CHUNK
     gram, rhs = pl.pallas_call(
         functools.partial(row_kernel, lat_tiles=lat_tiles),
@@ -369,7 +411,7 @@
             pltpu.SMEM((5,), jnp.int32),
             pltpu.SMEM((5,), jnp.int32),
             pltpu.SMEM((len(OFFSETS),), jnp.int32),
-            pltpu.VMEM((len(OFFSETS), size, size), jnp.float32),
+            pltpu.VMEM((len(OFFSETS) + 1, size, size), jnp.float32),
             pltpu.SemaphoreType.DMA((len(OFFSETS),)),
         ],
         compiler_params=pltpu.CompilerParams(vmem_limit_bytes=44 * 1024 * 1024),

time: 47.9 us -> 46.9 us (0.979)
  other arithmetic: 3.96 us -> 0.01 us
  local copies, waits for them, and re-layouts: 0.73 us -> 2.78 us
  starting transfers between devices: 7.98 us -> 9.33 us
    unnamed x1 -> x7, local copies, waits for them, and re-layouts: 0.71 us -> 2.77 us
    mul x4 -> x0, other arithmetic: 1.82 us -> none  [the longest x2 1.79 us: place(): jnp.cos(latitude) * jnp.cos(longitude)]
    concatenate x2 -> x0, other arithmetic: 1.39 us -> none  [the longest x1 0.71 us: shards(): package = jnp.concatenate([observed, dipoles], 1)]
    ppermute x7, starting transfers between devices: 7.98 us -> 9.33 us  [cycled(): lax.ppermute(value, axis, [(i, (i + steps) % count) for i in range(count)])]
    cos x1 -> x0, other arithmetic: 0.73 us -> none  [place(): jnp.cos(latitude) * jnp.cos(longitude)]
  transfers between devices with their start and end apart: 7 -> 7, of which waited for: 4 -> 3; matrix products, arithmetic and copies ran while one was open for 1% -> 0% of each run, Pallas kernels for 0% -> 0%
where the time goes in v5:
time: 46.9 us; the launch traced here: 46.5 us
  Pallas kernels  25.1 us (54%)
  starting transfers between devices  9.33 us (20%)
  waiting for transfers between devices  7.98 us (17%)
  local copies, waits for them, and re-layouts  2.78 us (6%)
  between operations  1.35 us (3%)
    pallas_call x1, Pallas kernels, shards(): pl.pallas_call(functools.partial(row_kernel, lat_tiles=lat_tiles), out_sh...  24.8 us
    ppermute x7, starting transfers between devices, cycled(): lax.ppermute(value, axis, [(i, (i + steps) % count) for i in range(count)])  9.33 us
    ppermute x7, waiting for transfers between devices, cycled(): lax.ppermute(value, axis, [(i, (i + steps) % count) for i in range(count)])  7.98 us
    unnamed x7, local copies, waits for them, and re-layouts  2.77 us
  transfers between devices with their start and end apart: 7, of which 3 were waited for; matrix products, arithmetic and copies ran while one was open for 0% of the time, Pallas kernels for 0%

profile of v5, /device:TPU:0, one launch (start us, length us, event | category | flops | bytes accessed | tf_op | source)
XLA Modules:
  0.0 46.5 jit_solution(15791256509084652702)
XLA Ops:
  1.3 0.7 %copy.9 = f32[1,1,3,1024]{3,2,1,0:T(4,128)S(1)} copy(f32[1,1,3,1024]{3,1,2,0:T(1,128)} %param.6) | data formatting | bytes 24576
  2.0 0.0 copy-start
  2.0 0.7 %copy-done = f32[1,1,2,1024]{3,2,1,0:T(2,128)S(1)} copy-done((f32[1,1,2,1024]{3,2,1,0:T(2,128)S(1)}, f32[1,1,2,1024]{3,2,1,0:T(2,128)}, u32[]{:S(2)}) %copy-start) | copy-done | bytes 8216
  2.7 0.0 copy-start.1
  2.7 0.7 %copy-done.1 = f32[1,1,2,256]{3,2,1,0:T(2,128)S(1)} copy-done((f32[1,1,2,256]{3,2,1,0:T(2,128)S(1)}, f32[1,1,2,256]{3,2,1,0:T(2,128)}, u32[]{:S(2)}) %copy-start.1) | copy-done | bytes 2072
  3.4 0.0 copy-start.2
  3.4 0.7 %copy-done.2 = f32[1,1,256]{2,1,0:T(1,128)S(1)} copy-done((f32[1,1,256]{2,1,0:T(1,128)S(1)}, f32[1,1,256]{2,1,0:T(1,128)}, u32[]{:S(2)}) %copy-start.2) | copy-done | bytes 1048
  4.0 0.3 pack_tile.1
  4.3 5.1 %collective-permute-start.4 = (f32[8,1280]{1,0:T(8,128)S(1)}, f32[8,1280]{1,0:T(8,128)S(1)}, u32[]{:S(2)}, u32[]{:S(2)}) collective-permute-start(f32[8,1280]{1,0:T(8,128)S(1)} %get-tuple-element.12.own_ref), channel_id=1, source_target_pairs={{0,3},{1,0},{2,1},{3,2},{4,7},{5,4},{6,5},{7,6},{8,11},{9,8},{10,9... | collective-permute-start | bytes 122888 | tf_op jit(solution)/shard_map/ppermute | solution.py:41
  9.4 0.0 collective-permute-start.3
  9.4 1.6 %collective-permute-start.1 = (f32[8,1280]{1,0:T(8,128)S(1)}, f32[8,1280]{1,0:T(8,128)S(1)}, u32[]{:S(2)}, u32[]{:S(2)}) collective-permute-start(f32[8,1280]{1,0:T(8,128)S(1)} %get-tuple-element.12.own_ref), channel_id=1, source_target_pairs={{0,28},{4,0},{8,4},{12,8},{16,12},{20,16},{24,20},{28,24},{1,29},{... | collective-permute-start | bytes 122888 | tf_op jit(solution)/shard_map/ppermute | solution.py:41
  11.1 0.0 collective-permute-start
  11.1 0.7 %collective-permute-start.2 = (f32[8,256]{1,0:T(8,128)S(1)}, f32[8,256]{1,0:T(8,128)S(1)}, u32[]{:S(2)}, u32[]{:S(2)}) collective-permute-start(f32[8,256]{1,0:T(8,128)S(1)} %get-tuple-element.13), channel_id=1, source_target_pairs={{0,2},{1,3},{2,0},{3,1},{4,6},{5,7},{6,4},{7,5},{8,10},{9,11},{10,... | collective-permute-start | bytes 24584 | tf_op jit(solution)/shard_map/ppermute | solution.py:41
  11.8 3.8 %collective-permute-done.2.far_west_ref.far_east_ref = f32[8,256]{1,0:T(8,128)S(1)} collective-permute-done((f32[8,256]{1,0:T(8,128)S(1)}, f32[8,256]{1,0:T(8,128)S(1)}, u32[]{:S(2)}, u32[]{:S(2)}) %collective-permute-start.2) | collective-permute-done | bytes 8224 | tf_op jit(solution)/shard_map/ppermute | solution.py:41
  15.6 0.0 collective-permute-done.4.east_ref
  15.6 0.0 collective-permute-done.3.west_ref
  15.6 0.0 collective-permute-done.1.south_ref
  15.6 0.0 collective-permute-done.north_ref
  15.7 1.9 %collective-permute-start.6 = (f32[8,768]{1,0:T(8,128)S(1)}, f32[8,768]{1,0:T(8,128)S(1)}, u32[]{:S(2)}, u32[]{:S(2)}) collective-permute-start(f32[8,768]{1,0:T(8,128)S(1)} %get-tuple-element.22), channel_id=1, source_target_pairs={{0,28},{4,0},{8,4},{12,8},{16,12},{20,16},{24,20},{28,24},{1,29},{... | collective-permute-start | bytes 73736 | tf_op jit(solution)/shard_map/ppermute | solution.py:41
  17.5 0.0 collective-permute-start.5
  17.5 1.5 %collective-permute-done.6.far_south_ref = f32[8,768]{1,0:T(8,128)S(1)} collective-permute-done((f32[8,768]{1,0:T(8,128)S(1)}, f32[8,768]{1,0:T(8,128)S(1)}, u32[]{:S(2)}, u32[]{:S(2)}) %collective-permute-start.6) | collective-permute-done | bytes 24608 | tf_op jit(solution)/shard_map/ppermute | solution.py:41
  19.1 2.6 %collective-permute-done.5.far_north_ref = f32[8,768]{1,0:T(8,128)S(1)} collective-permute-done((f32[8,768]{1,0:T(8,128)S(1)}, f32[8,768]{1,0:T(8,128)S(1)}, u32[]{:S(2)}, u32[]{:S(2)}) %collective-permute-start.5) | collective-permute-done | bytes 24608 | tf_op jit(solution)/shard_map/ppermute | solution.py:41
  21.7 24.8 %row_blocks.1 = (f32[13,256,256]{2,1,0:T(8,128)}, f32[1,256]{1,0:T(1,128)}) custom-call(f32[8,1280]{1,0:T(8,128)S(1)} %get-tuple-element.12.own_ref, f32[8,1280]{1,0:T(8,128)S(1)} %collective-permute-done.north_ref, f32[8,1280]{1,0:T(8,128)S(1)} %collective-permute-done.1.south_ref, f32[8,1280]{1,0:T(8,128)S(1)} %collective-permute-done.3.west_ref, ...), custom_call_target="tpu_custom_call" | custom-call | tf_op jit(solution)/shard_map/row_blocks/pallas_call | solution.py:387
  (5 shorter events, 0.0 us)
Async XLA Ops:
  2.0 0.7 %copy-start = (f32[1,1,2,1024]{3,2,1,0:T(2,128)S(1)}, f32[1,1,2,1024]{3,2,1,0:T(2,128)}, u32[]{:S(2)}) copy-start(f32[1,1,2,1024]{3,2,1,0:T(2,128)} %param.5) | copy-start | bytes 24580
  2.7 0.7 %copy-start.1 = (f32[1,1,2,256]{3,2,1,0:T(2,128)S(1)}, f32[1,1,2,256]{3,2,1,0:T(2,128)}, u32[]{:S(2)}) copy-start(f32[1,1,2,256]{3,2,1,0:T(2,128)} %param.7) | copy-start | bytes 6148
  3.4 0.7 %copy-start.2 = (f32[1,1,256]{2,1,0:T(1,128)S(1)}, f32[1,1,256]{2,1,0:T(1,128)}, u32[]{:S(2)}) copy-start(f32[1,1,256]{2,1,0:T(1,128)} %param.8) | copy-start | bytes 3076
  4.3 11.3 %collective-permute-start.4 = (f32[8,1280]{1,0:T(8,128)S(1)}, f32[8,1280]{1,0:T(8,128)S(1)}, u32[]{:S(2)}, u32[]{:S(2)}) collective-permute-start(f32[8,1280]{1,0:T(8,128)S(1)} %get-tuple-element.12.own_ref), channel_id=1, source_target_pairs={{0,3},{1,0},{2,1},{3,2},{4,7},{5,4},{6,5},{7,6},{8,11},{9,8},{10,9... | collective-permute-start | bytes 122888 | tf_op jit(solution)/shard_map/ppermute | solution.py:41
  9.4 6.2 %collective-permute-start.3 = (f32[8,1280]{1,0:T(8,128)S(1)}, f32[8,1280]{1,0:T(8,128)S(1)}, u32[]{:S(2)}, u32[]{:S(2)}) collective-permute-start(f32[8,1280]{1,0:T(8,128)S(1)} %get-tuple-element.12.own_ref), channel_id=1, source_target_pairs={{0,1},{1,2},{2,3},{3,0},{4,5},{5,6},{6,7},{7,4},{8,9},{9,10},{10,1... | collective-permute-start | bytes 122888 | tf_op jit(solution)/shard_map/ppermute | solution.py:41
  9.4 6.2 %collective-permute-start.1 = (f32[8,1280]{1,0:T(8,128)S(1)}, f32[8,1280]{1,0:T(8,128)S(1)}, u32[]{:S(2)}, u32[]{:S(2)}) collective-permute-start(f32[8,1280]{1,0:T(8,128)S(1)} %get-tuple-element.12.own_ref), channel_id=1, source_target_pairs={{0,28},{4,0},{8,4},{12,8},{16,12},{20,16},{24,20},{28,24},{1,29},{... | collective-permute-start | bytes 122888 | tf_op jit(solution)/shard_map/ppermute | solution.py:41
  11.1 4.6 %collective-permute-start = (f32[8,1280]{1,0:T(8,128)S(1)}, f32[8,1280]{1,0:T(8,128)S(1)}, u32[]{:S(2)}, u32[]{:S(2)}) collective-permute-start(f32[8,1280]{1,0:T(8,128)S(1)} %get-tuple-element.12.own_ref), channel_id=1, source_target_pairs={{0,4},{4,8},{8,12},{12,16},{16,20},{20,24},{24,28},{28,0},{1,5},{5... | collective-permute-start | bytes 122888 | tf_op jit(solution)/shard_map/ppermute | solution.py:41
  11.1 4.5 %collective-permute-start.2 = (f32[8,256]{1,0:T(8,128)S(1)}, f32[8,256]{1,0:T(8,128)S(1)}, u32[]{:S(2)}, u32[]{:S(2)}) collective-permute-start(f32[8,256]{1,0:T(8,128)S(1)} %get-tuple-element.13), channel_id=1, source_target_pairs={{0,2},{1,3},{2,0},{3,1},{4,6},{5,7},{6,4},{7,5},{8,10},{9,11},{10,... | collective-permute-start | bytes 24584 | tf_op jit(solution)/shard_map/ppermute | solution.py:41
  15.7 3.4 %collective-permute-start.6 = (f32[8,768]{1,0:T(8,128)S(1)}, f32[8,768]{1,0:T(8,128)S(1)}, u32[]{:S(2)}, u32[]{:S(2)}) collective-permute-start(f32[8,768]{1,0:T(8,128)S(1)} %get-tuple-element.22), channel_id=1, source_target_pairs={{0,28},{4,0},{8,4},{12,8},{16,12},{20,16},{24,20},{28,24},{1,29},{... | collective-permute-start | bytes 73736 | tf_op jit(solution)/shard_map/ppermute | solution.py:41
  17.5 4.2 %collective-permute-start.5 = (f32[8,768]{1,0:T(8,128)S(1)}, f32[8,768]{1,0:T(8,128)S(1)}, u32[]{:S(2)}, u32[]{:S(2)}) collective-permute-start(f32[8,768]{1,0:T(8,128)S(1)} %get-tuple-element.23), channel_id=1, source_target_pairs={{0,4},{4,8},{8,12},{12,16},{16,20},{20,24},{24,28},{28,0},{1,5},{5... | collective-permute-start | bytes 73736 | tf_op jit(solution)/shard_map/ppermute | solution.py:41

commit v6 on v5

--- a/solution.py
+++ b/solution.py
@@ -90,57 +90,54 @@
     return high, middle, rest - middle
 
 
-def row_kernel(
-    own_ref,
-    north_ref,
-    south_ref,
-    west_ref,
-    east_ref,
-    far_north_ref,
-    far_south_ref,
-    far_west_ref,
-    far_east_ref,
-    gram_ref,
-    rhs_ref,
-    obs,
-    column,
-    tall,
-    flat,
-    held_even,
-    held_odd,
-    weighted_even,
-    weighted_odd,
-    apart_even,
-    apart_odd,
-    kept,
-    predicted,
-    right,
-    table,
-    items,
-    members,
-    counts,
-    waits,
-    gram,
-    sent,
-    *,
-    lat_tiles,
-):
-    size = rhs_ref.shape[1]
+def row_kernel(*refs, lat_tiles, opening):
+    refs = list(refs)
+    own_ref, north_ref, south_ref, west_ref, east_ref = refs[:5]
+    if opening:
+        gram, right = refs[5:7]
+        rest = refs[7:]
+        tiles, targets = (0,), range(len(CROSS))
+    else:
+        far_north_ref, far_south_ref, far_west_ref, far_east_ref, gram_in, right_in, gram_ref, rhs_ref = refs[5:13]
+        rest = refs[13:]
+        tiles, targets = (3, 4, 1, 2), range(len(OFFSETS))
+    (
+        obs,
+        column,
+        tall,
+        flat,
+        held_even,
+        held_odd,
+        weighted_even,
+        weighted_odd,
+        apart_even,
+        apart_odd,
+        kept,
+        predicted,
+        table,
+        items,
+        members,
+        counts,
+    ) = rest[:16]
+    if not opening:
+        right, waits, gram, sent = rest[16:]
+    size = right.shape[0]
     chunks = obs.shape[0] // len(CROSS)
     slots = chunks * CHUNK
     lat = lax.axis_index("lat")
 
-    for tile, ref in enumerate((own_ref, north_ref, south_ref, west_ref, east_ref)):
+    arrived = (own_ref, north_ref, south_ref, west_ref, east_ref)
+    for tile in tiles:
         for chunk in range(chunks):
-            obs[tile * chunks + chunk] = ref[:, chunk * CHUNK : (chunk + 1) * CHUNK]
-    sources = {(0, 0): own_ref, (-1, 0): north_ref, (1, 0): south_ref, (0, -1): west_ref, (0, 1): east_ref}
-    sources = {offset: (ref, slots) for offset, ref in sources.items()}
-    for at, offset in enumerate(((-2, 0), (-1, -1), (-1, 1))):
-        sources[offset] = (far_north_ref, at * size)
-    for at, offset in enumerate(((2, 0), (1, -1), (1, 1))):
-        sources[offset] = (far_south_ref, at * size)
-    sources[(0, -2)] = (far_west_ref, 0)
-    sources[(0, 2)] = (far_east_ref, 0)
+            obs[tile * chunks + chunk] = arrived[tile][:, chunk * CHUNK : (chunk + 1) * CHUNK]
+    sources = {offset: (ref, slots) for offset, ref in zip(CROSS, arrived)}
+    if not opening:
+        for at, offset in enumerate(((-2, 0), (-1, -1), (-1, 1))):
+            sources[offset] = (far_north_ref, at * size)
+        for at, offset in enumerate(((2, 0), (1, -1), (1, 1))):
+            sources[offset] = (far_south_ref, at * size)
+        sources[(0, -2)] = (far_west_ref, 0)
+        sources[(0, 2)] = (far_east_ref, 0)
 
     def inside(step):
         return (lat + step >= 0) & (lat + step < lat_tiles)
@@ -149,8 +146,9 @@
     parts = lax.broadcasted_iota(jnp.int32, (DEPTH, 4 * LANES), 1) // LANES
     picks = ((picks == parts) | (picks == parts + 16) | (picks == parts + 32)).astype(jnp.bfloat16)
     row_of = lax.broadcasted_iota(jnp.int32, (8, size), 0)
-    right[...] = jnp.zeros_like(right)
-    for target, offset in enumerate(OFFSETS):
+    right[...] = jnp.zeros_like(right) if opening else right_in[...]
+    for target in targets:
+        offset = OFFSETS[target]
         ref, start = sources[offset]
         values = ref[:, start : start + size]
         if offset[0] != 0:
@@ -159,7 +157,8 @@
         ones = jnp.ones_like(values)
         stacked = jnp.concatenate([high, high, middle, high, low, middle, ones, jnp.zeros_like(values)], 0)
         upright = stacked.T.astype(jnp.bfloat16)
-        gram[target] = jnp.zeros((size, size), jnp.float32)
+        fresh = opening or target >= len(CROSS)
+        gram[target] = jnp.zeros((size, size), jnp.float32) if fresh else gram_in[target]
         tall[target] = upright
         wide = lax.dot_general(upright, picks, (((1,), (0,)), ((), ())), preferred_element_type=jnp.float32)
         for part in range(4):
@@ -167,14 +166,14 @@
 
     row_of = lax.broadcasted_iota(jnp.int32, (8, CHUNK), 0)
     base = STRETCH * (OBS_RADIUS * OBS_RADIUS + SOURCE_RADIUS * SOURCE_RADIUS)
-    for at in range(obs.shape[0]):
+    for at in [tile * chunks + chunk for tile in tiles for chunk in range(chunks)]:
         high, middle, low = split(jnp.where(row_of < 3, obs[at] * (-2.0 * STRETCH), 0.0))
         first, second, third = split(jnp.full((8, CHUNK), base, jnp.float32))
         constant = jnp.where(row_of == 0, first, jnp.where(row_of == 1, second, jnp.where(row_of == 2, third, 0.0)))
         stacked = jnp.concatenate([high, middle, high, low, high, middle, constant, jnp.zeros_like(high)], 0)
         flat[at] = stacked.astype(jnp.bfloat16)
 
-    for tile in range(len(CROSS)):
+    for tile in tiles:
         step = CROSS[tile]
         row = lat + step[0]
         first_row, last_row = row == 0, row == lat_tiles - 1
@@ -193,7 +192,7 @@
 
     total = jnp.int32(0)
     for full in (5, 4):
-        for tile in (0, 3, 4, 1, 2):
+        for tile in tiles:
 
             def note(chunk, at, tile=tile):
                 items[0, at] = tile
@@ -265,17 +264,19 @@
     last = items[0, total - 1]
     twice = items[0, jnp.maximum(total - 2, 0)] == last
 
-    def clear(target, carry):
-        waits[target] = 0
-        return carry
-
-    lax.fori_loop(0, len(OFFSETS), clear, 0)
-
-    def mark(at, carry):
-        waits[table[last, at]] = 1
-        return carry
-
-    lax.fori_loop(0, members[last], mark, 0)
+    if not opening:
+
+        def clear(target, carry):
+            waits[target] = 0
+            return carry
+
+        lax.fori_loop(0, len(OFFSETS), clear, 0)
+
+        def mark(at, carry):
+            waits[table[last, at]] = 1
+            return carry
+
+        lax.fori_loop(0, members[last], mark, 0)
 
     def early(target, carry):
         @pl.when(waits[target] == 0)
@@ -291,13 +292,15 @@
         later, later_chunk = items[0, after], items[1, after]
         predicted[...] = jnp.zeros_like(predicted)
 
-        @pl.when((item == total - 1) & twice)
-        def _():
-            lax.fori_loop(0, len(OFFSETS), early, 0)
+        if not opening:
+
+            @pl.when((item == total - 1) & twice)
+            def _():
+                lax.fori_loop(0, len(OFFSETS), early, 0)
 
         def block(at, carry):
             separate(later, later_chunk, at, apart_later)
-            target = jnp.where(item == 0, len(OFFSETS), table[before, at])
+            target = jnp.where(item == 0, len(targets), table[before, at])
             multiply(target, at, held_before, weighted_before)
             evaluate(tile, chunk, at, held, apart)
             return carry
@@ -322,14 +325,17 @@
     def _():
         advance(total - 1, held_even, weighted_even, apart_even, held_odd, weighted_odd, apart_odd)
 
-    @pl.when(jnp.logical_not(twice))
-    def _():
-        lax.fori_loop(0, len(OFFSETS), early, 0)
+    if not opening:
+
+        @pl.when(jnp.logical_not(twice))
+        def _():
+            lax.fori_loop(0, len(OFFSETS), early, 0)
 
     def drain(held, weighted):
         def block(at, carry):
             multiply(table[last, at], at, held, weighted)
-            flush(table[last, at])
+            if not opening:
+                flush(table[last, at])
             return carry
 
         lax.fori_loop(0, members[last], block, 0)
@@ -342,13 +348,14 @@
     def _():
         drain(held_odd, weighted_odd)
 
-    rhs_ref[...] = jnp.sum(right[...].T, axis=0, keepdims=True)
-
-    def close(target, carry):
-        pltpu.make_async_copy(gram.at[target], gram_ref.at[target], sent.at[target]).wait()
-        return carry
-
-    lax.fori_loop(0, len(OFFSETS), close, 0)
+    if not opening:
+        rhs_ref[...] = jnp.sum(right[...].T, axis=0, keepdims=True)
+
+        def close(target, carry):
+            pltpu.make_async_copy(gram.at[target], gram_ref.at[target], sent.at[target]).wait()
+            return carry
+
+        lax.fori_loop(0, len(OFFSETS), close, 0)
 
 
 def shards(obs_frac, obs_field, dipole_frac, dipole_moment, obs_count):
@@ -384,18 +391,13 @@
     far_north = cycled(jnp.concatenate([north[:, slots:], west[:, slots:], east[:, slots:]], 1), "lat", 1)
     far_south = cycled(jnp.concatenate([south[:, slots:], west[:, slots:], east[:, slots:]], 1), "lat", -1)
     chunks = slots // CHUNK
-    gram, rhs = pl.pallas_call(
-        functools.partial(row_kernel, lat_tiles=lat_tiles),
-        out_shape=(
-            jax.ShapeDtypeStruct((len(OFFSETS), size, size), jnp.float32),
-            jax.ShapeDtypeStruct((1, size), jnp.float32),
-        ),
-        in_specs=[pl.BlockSpec(memory_space=pltpu.VMEM)] * 9,
-        out_specs=(pl.BlockSpec(memory_space=pl.ANY), pl.BlockSpec(memory_space=pltpu.VMEM)),
-        scratch_shapes=[
+    vmem = pl.BlockSpec(memory_space=pltpu.VMEM)
+
+    def working(targets):
+        return [
             pltpu.VMEM((5 * chunks, 8, CHUNK), jnp.float32),
-            pltpu.VMEM((len(OFFSETS), 4, size, LANES), jnp.float32),
-            pltpu.VMEM((len(OFFSETS), size, DEPTH), jnp.bfloat16),
+            pltpu.VMEM((targets, 4, size, LANES), jnp.float32),
+            pltpu.VMEM((targets, size, DEPTH), jnp.bfloat16),
             pltpu.VMEM((5 * chunks, DEPTH, CHUNK), jnp.bfloat16),
             pltpu.VMEM((5, size, 3 * CHUNK), jnp.bfloat16),
             pltpu.VMEM((5, size, 3 * CHUNK), jnp.bfloat16),
@@ -405,18 +407,45 @@
             pltpu.VMEM((5, size, CHUNK), jnp.float32),
             pltpu.VMEM((2, 3, size, CHUNK), jnp.float32),
             pltpu.VMEM((3, 8, CHUNK), jnp.float32),
-            pltpu.VMEM((size, LANES), jnp.float32),
             pltpu.SMEM((5, 5), jnp.int32),
             pltpu.SMEM((2, 5 * chunks), jnp.int32),
             pltpu.SMEM((5,), jnp.int32),
             pltpu.SMEM((5,), jnp.int32),
+        ]
+
+    products = 2 * 3 * slots * size * size
+    own_gram, own_right = pl.pallas_call(
+        functools.partial(row_kernel, lat_tiles=lat_tiles, opening=True),
+        out_shape=(
+            jax.ShapeDtypeStruct((len(CROSS) + 1, size, size), jnp.float32),
+            jax.ShapeDtypeStruct((size, LANES), jnp.float32),
+        ),
+        in_specs=[vmem] * 5,
+        out_specs=(vmem, vmem),
+        scratch_shapes=working(len(CROSS)),
+        compiler_params=pltpu.CompilerParams(vmem_limit_bytes=26 * 1024 * 1024),
+        cost_estimate=pl.CostEstimate(flops=5 * products, bytes_accessed=8 * size * size * 4, transcendentals=0),
+        name="own_rows",
+    )(package, north, south, west, east)
+    gram, rhs = pl.pallas_call(
+        functools.partial(row_kernel, lat_tiles=lat_tiles, opening=False),
+        out_shape=(
+            jax.ShapeDtypeStruct((len(OFFSETS), size, size), jnp.float32),
+            jax.ShapeDtypeStruct((1, size), jnp.float32),
+        ),
+        in_specs=[vmem] * 11,
+        out_specs=(pl.BlockSpec(memory_space=pl.ANY), vmem),
+        scratch_shapes=working(len(OFFSETS))
+        + [
+            pltpu.VMEM((size, LANES), jnp.float32),
             pltpu.SMEM((len(OFFSETS),), jnp.int32),
             pltpu.VMEM((len(OFFSETS) + 1, size, size), jnp.float32),
             pltpu.SemaphoreType.DMA((len(OFFSETS),)),
         ],
         compiler_params=pltpu.CompilerParams(vmem_limit_bytes=44 * 1024 * 1024),
+        cost_estimate=pl.CostEstimate(flops=20 * products, bytes_accessed=16 * size * size * 4, transcendentals=0),
         name="row_blocks",
-    )(package, north, south, west, east, far_north, far_south, far_west, far_east)
+    )(package, north, south, west, east, far_north, far_south, far_west, far_east, own_gram, own_right)
     return (gram[None, None], rhs[None])
 
 

time: 46.9 us -> 45.7 us (0.974)
  waiting for transfers between devices: 7.98 us -> 3.83 us
  Pallas kernels: 25.1 us -> 28 us
    ppermute x7, waiting for transfers between devices: 7.98 us -> 3.83 us  [cycled(): lax.ppermute(value, axis, [(i, (i + steps) % count) for i in range(count)])]
    pallas_call x1 -> x2, Pallas kernels: 24.8 us -> 27.8 us  [shards(): pl.pallas_call(functools.partial(row_kernel, lat_tiles=lat_tiles, opening...]
  transfers between devices with their start and end apart: 7 -> 7, of which waited for: 3 -> 1; matrix products, arithmetic and copies ran while one was open for 0% -> 0% of each run, Pallas kernels for 0% -> 17%
where the time goes in v6:
time: 45.7 us; the launch traced here: 45.3 us
  Pallas kernels  28 us (61%)
  starting transfers between devices  9.33 us (20%)
  waiting for transfers between devices  3.83 us (8%)
  local copies, waits for them, and re-layouts  2.78 us (6%)
  between operations  1.37 us (3%)
    pallas_call x2, Pallas kernels, shards(): pl.pallas_call(functools.partial(row_kernel, lat_tiles=lat_tiles, opening...  27.8 us
    ppermute x7, starting transfers between devices, cycled(): lax.ppermute(value, axis, [(i, (i + steps) % count) for i in range(count)])  9.33 us
    ppermute x7, waiting for transfers between devices, cycled(): lax.ppermute(value, axis, [(i, (i + steps) % count) for i in range(count)])  3.83 us
    unnamed x7, local copies, waits for them, and re-layouts  2.77 us
  transfers between devices with their start and end apart: 7, of which 1 were waited for; matrix products, arithmetic and copies ran while one was open for 0% of the time, Pallas kernels for 17%

profile of v6, /device:TPU:0, one launch (start us, length us, event | category | flops | bytes accessed | tf_op | source)
XLA Modules:
  0.0 45.3 jit_solution(2262359648696068675)
XLA Ops:
  1.3 0.7 %copy.9 = f32[1,1,3,1024]{3,2,1,0:T(4,128)S(1)} copy(f32[1,1,3,1024]{3,1,2,0:T(1,128)} %param.6) | data formatting | bytes 24576
  2.0 0.0 copy-start
  2.0 0.7 %copy-done = f32[1,1,2,1024]{3,2,1,0:T(2,128)S(1)} copy-done((f32[1,1,2,1024]{3,2,1,0:T(2,128)S(1)}, f32[1,1,2,1024]{3,2,1,0:T(2,128)}, u32[]{:S(2)}) %copy-start) | copy-done | bytes 8216
  2.7 0.0 copy-start.1
  2.7 0.7 %copy-done.1 = f32[1,1,2,256]{3,2,1,0:T(2,128)S(1)} copy-done((f32[1,1,2,256]{3,2,1,0:T(2,128)S(1)}, f32[1,1,2,256]{3,2,1,0:T(2,128)}, u32[]{:S(2)}) %copy-start.1) | copy-done | bytes 2072
  3.4 0.0 copy-start.2
  3.4 0.7 %copy-done.2 = f32[1,1,256]{2,1,0:T(1,128)S(1)} copy-done((f32[1,1,256]{2,1,0:T(1,128)S(1)}, f32[1,1,256]{2,1,0:T(1,128)}, u32[]{:S(2)}) %copy-start.2) | copy-done | bytes 1048
  4.0 0.3 pack_tile.1
  4.3 5.1 %collective-permute-start.4 = (f32[8,1280]{1,0:T(8,128)S(1)}, f32[8,1280]{1,0:T(8,128)S(1)}, u32[]{:S(2)}, u32[]{:S(2)}) collective-permute-start(f32[8,1280]{1,0:T(8,128)S(1)} %get-tuple-element.14.refs_0_), channel_id=1, source_target_pairs={{0,3},{1,0},{2,1},{3,2},{4,7},{5,4},{6,5},{7,6},{8,11},{9,8},{10,9... | collective-permute-start | bytes 122888 | tf_op jit(solution)/shard_map/ppermute | solution.py:41
  9.4 0.0 collective-permute-start.3
  9.4 1.6 %collective-permute-start.1 = (f32[8,1280]{1,0:T(8,128)S(1)}, f32[8,1280]{1,0:T(8,128)S(1)}, u32[]{:S(2)}, u32[]{:S(2)}) collective-permute-start(f32[8,1280]{1,0:T(8,128)S(1)} %get-tuple-element.14.refs_0_), channel_id=1, source_target_pairs={{0,28},{4,0},{8,4},{12,8},{16,12},{20,16},{24,20},{28,24},{1,29},{... | collective-permute-start | bytes 122888 | tf_op jit(solution)/shard_map/ppermute | solution.py:41
  11.1 0.0 collective-permute-start
  11.1 0.7 %collective-permute-start.2 = (f32[8,256]{1,0:T(8,128)S(1)}, f32[8,256]{1,0:T(8,128)S(1)}, u32[]{:S(2)}, u32[]{:S(2)}) collective-permute-start(f32[8,256]{1,0:T(8,128)S(1)} %get-tuple-element.15), channel_id=1, source_target_pairs={{0,2},{1,3},{2,0},{3,1},{4,6},{5,7},{6,4},{7,5},{8,10},{9,11},{10,... | collective-permute-start | bytes 24584 | tf_op jit(solution)/shard_map/ppermute | solution.py:41
  11.8 3.8 %collective-permute-done.2.refs_7_.refs_8_ = f32[8,256]{1,0:T(8,128)S(1)} collective-permute-done((f32[8,256]{1,0:T(8,128)S(1)}, f32[8,256]{1,0:T(8,128)S(1)}, u32[]{:S(2)}, u32[]{:S(2)}) %collective-permute-start.2) | collective-permute-done | bytes 8224 | tf_op jit(solution)/shard_map/ppermute | solution.py:41
  15.6 0.0 collective-permute-done.4.refs_4_
  15.6 0.0 collective-permute-done.3.refs_3_
  15.6 0.0 collective-permute-done.1.refs_2_
  15.6 0.0 collective-permute-done.refs_1_
  15.7 1.9 %collective-permute-start.6 = (f32[8,768]{1,0:T(8,128)S(1)}, f32[8,768]{1,0:T(8,128)S(1)}, u32[]{:S(2)}, u32[]{:S(2)}) collective-permute-start(f32[8,768]{1,0:T(8,128)S(1)} %get-tuple-element.26), channel_id=1, source_target_pairs={{0,28},{4,0},{8,4},{12,8},{16,12},{20,16},{24,20},{28,24},{1,29},{... | collective-permute-start | bytes 73736 | tf_op jit(solution)/shard_map/ppermute | solution.py:41
  17.5 0.0 collective-permute-start.5
  17.5 7.7 %own_rows.1 = (f32[6,256,256]{2,1,0:T(8,128)S(1)}, f32[256,128]{1,0:T(8,128)S(1)}) custom-call(f32[8,1280]{1,0:T(8,128)S(1)} %get-tuple-element.14.refs_0_, f32[8,1280]{1,0:T(8,128)S(1)} %collective-permute-done.refs_1_, f32[8,1280]{1,0:T(8,128)S(1)} %collective-permute-done.1.refs_2_, f32[8,1280]{1,0:T(8,128)S(1)} %collective-permute-done.3.refs_3_, ...), custom_call_target="tpu_custom_call" | custom-call | flops 2013265920 | bytes 2097152 | tf_op jit(solution)/shard_map/own_rows/pallas_call | solution.py:417
  25.3 0.0 collective-permute-done.6.refs_6_
  25.3 0.0 collective-permute-done.5.refs_5_
  25.3 20.0 %row_blocks.1 = (f32[13,256,256]{2,1,0:T(8,128)}, f32[1,256]{1,0:T(1,128)}) custom-call(f32[8,1280]{1,0:T(8,128)S(1)} %get-tuple-element.14.refs_0_, f32[8,1280]{1,0:T(8,128)S(1)} %collective-permute-done.refs_1_, f32[8,1280]{1,0:T(8,128)S(1)} %collective-permute-done.1.refs_2_, f32[8,1280]{1,0:T(8,128)S(1)} %collective-permute-done.3.refs_3_, ...), custom_call_target="tpu_custom_call" | custom-call | flops 8053063680 | bytes 4194304 | tf_op jit(solution)/shard_map/row_blocks/pallas_call | solution.py:430
  (5 shorter events, 0.0 us)
Async XLA Ops:
  2.0 0.7 %copy-start = (f32[1,1,2,1024]{3,2,1,0:T(2,128)S(1)}, f32[1,1,2,1024]{3,2,1,0:T(2,128)}, u32[]{:S(2)}) copy-start(f32[1,1,2,1024]{3,2,1,0:T(2,128)} %param.5) | copy-start | bytes 24580
  2.7 0.7 %copy-start.1 = (f32[1,1,2,256]{3,2,1,0:T(2,128)S(1)}, f32[1,1,2,256]{3,2,1,0:T(2,128)}, u32[]{:S(2)}) copy-start(f32[1,1,2,256]{3,2,1,0:T(2,128)} %param.7) | copy-start | bytes 6148
  3.4 0.7 %copy-start.2 = (f32[1,1,256]{2,1,0:T(1,128)S(1)}, f32[1,1,256]{2,1,0:T(1,128)}, u32[]{:S(2)}) copy-start(f32[1,1,256]{2,1,0:T(1,128)} %param.8) | copy-start | bytes 3076
  4.3 11.3 %collective-permute-start.4 = (f32[8,1280]{1,0:T(8,128)S(1)}, f32[8,1280]{1,0:T(8,128)S(1)}, u32[]{:S(2)}, u32[]{:S(2)}) collective-permute-start(f32[8,1280]{1,0:T(8,128)S(1)} %get-tuple-element.14.refs_0_), channel_id=1, source_target_pairs={{0,3},{1,0},{2,1},{3,2},{4,7},{5,4},{6,5},{7,6},{8,11},{9,8},{10,9... | collective-permute-start | bytes 122888 | tf_op jit(solution)/shard_map/ppermute | solution.py:41
  9.4 6.2 %collective-permute-start.3 = (f32[8,1280]{1,0:T(8,128)S(1)}, f32[8,1280]{1,0:T(8,128)S(1)}, u32[]{:S(2)}, u32[]{:S(2)}) collective-permute-start(f32[8,1280]{1,0:T(8,128)S(1)} %get-tuple-element.14.refs_0_), channel_id=1, source_target_pairs={{0,1},{1,2},{2,3},{3,0},{4,5},{5,6},{6,7},{7,4},{8,9},{9,10},{10,1... | collective-permute-start | bytes 122888 | tf_op jit(solution)/shard_map/ppermute | solution.py:41
  9.4 6.2 %collective-permute-start.1 = (f32[8,1280]{1,0:T(8,128)S(1)}, f32[8,1280]{1,0:T(8,128)S(1)}, u32[]{:S(2)}, u32[]{:S(2)}) collective-permute-start(f32[8,1280]{1,0:T(8,128)S(1)} %get-tuple-element.14.refs_0_), channel_id=1, source_target_pairs={{0,28},{4,0},{8,4},{12,8},{16,12},{20,16},{24,20},{28,24},{1,29},{... | collective-permute-start | bytes 122888 | tf_op jit(solution)/shard_map/ppermute | solution.py:41
  11.1 4.6 %collective-permute-start = (f32[8,1280]{1,0:T(8,128)S(1)}, f32[8,1280]{1,0:T(8,128)S(1)}, u32[]{:S(2)}, u32[]{:S(2)}) collective-permute-start(f32[8,1280]{1,0:T(8,128)S(1)} %get-tuple-element.14.refs_0_), channel_id=1, source_target_pairs={{0,4},{4,8},{8,12},{12,16},{16,20},{20,24},{24,28},{28,0},{1,5},{5... | collective-permute-start | bytes 122888 | tf_op jit(solution)/shard_map/ppermute | solution.py:41
  11.1 4.5 %collective-permute-start.2 = (f32[8,256]{1,0:T(8,128)S(1)}, f32[8,256]{1,0:T(8,128)S(1)}, u32[]{:S(2)}, u32[]{:S(2)}) collective-permute-start(f32[8,256]{1,0:T(8,128)S(1)} %get-tuple-element.15), channel_id=1, source_target_pairs={{0,2},{1,3},{2,0},{3,1},{4,6},{5,7},{6,4},{7,5},{8,10},{9,11},{10,... | collective-permute-start | bytes 24584 | tf_op jit(solution)/shard_map/ppermute | solution.py:41
  15.7 9.6 %collective-permute-start.6 = (f32[8,768]{1,0:T(8,128)S(1)}, f32[8,768]{1,0:T(8,128)S(1)}, u32[]{:S(2)}, u32[]{:S(2)}) collective-permute-start(f32[8,768]{1,0:T(8,128)S(1)} %get-tuple-element.26), channel_id=1, source_target_pairs={{0,28},{4,0},{8,4},{12,8},{16,12},{20,16},{24,20},{28,24},{1,29},{... | collective-permute-start | bytes 73736 | tf_op jit(solution)/shard_map/ppermute | solution.py:41
  17.5 7.8 %collective-permute-start.5 = (f32[8,768]{1,0:T(8,128)S(1)}, f32[8,768]{1,0:T(8,128)S(1)}, u32[]{:S(2)}, u32[]{:S(2)}) collective-permute-start(f32[8,768]{1,0:T(8,128)S(1)} %get-tuple-element.27), channel_id=1, source_target_pairs={{0,4},{4,8},{8,12},{12,16},{16,20},{20,24},{24,28},{28,0},{1,5},{5... | collective-permute-start | bytes 73736 | tf_op jit(solution)/shard_map/ppermute | solution.py:41

commit v7 on v6

--- a/solution.py
+++ b/solution.py
@@ -41,20 +41,11 @@
     return lax.ppermute(value, axis, [(i, (i + steps) % count) for i in range(count)])
 
 
-def pack_kernel(
-    obs_frac_ref, obs_field_ref, dipole_frac_ref, moment_ref, obs_count, package, dipoles,
-    obs_frac, obs_field, dipole_frac, moment, landed, *, lat_tiles, lon_tiles,
-):
-    loads = [
-        pltpu.make_async_copy(source, target, landed.at[at])
-        for at, (source, target) in enumerate(
-            ((obs_frac_ref, obs_frac), (obs_field_ref, obs_field), (dipole_frac_ref, dipole_frac), (moment_ref, moment))
-        )
-    ]
-    for load in loads:
-        load.start()
-    for load in loads:
-        load.wait()
+def pack_kernel(raw, obs_count, package, dipoles, *, lat_tiles, lon_tiles):
+    size = dipoles.shape[1]
+    slots = raw.shape[1] - size
+    obs_frac, obs_field = raw[0:2, :slots], raw[2:5, :slots]
+    dipole_frac, moment = raw[0:2, slots:], raw[2:3, slots:]
     lat_index = lax.axis_index("lat").astype(jnp.float32)
     lon_index = lax.axis_index("lon").astype(jnp.float32)
     lat_span = 160.0 * DEGREE / lat_tiles
@@ -70,14 +61,13 @@
             radius * sine[0:1],
         ]
 
-    slots, size = obs_frac.shape[1], dipole_frac.shape[1]
-    for row, value in enumerate(place(obs_frac[...], OBS_RADIUS)):
+    for row, value in enumerate(place(obs_frac, OBS_RADIUS)):
         package[row : row + 1, :slots] = value
-    package[3:6, :slots] = obs_field[...]
+    package[3:6, :slots] = obs_field
     index = lax.broadcasted_iota(jnp.int32, (1, slots), 1)
     package[6:7, :slots] = (index < obs_count[0, 0]).astype(jnp.float32)
     package[7:8, :slots] = jnp.zeros((1, slots), jnp.float32)
-    rows = place(dipole_frac[...], SOURCE_RADIUS) + [moment[...], jnp.zeros((4, size), jnp.float32)]
+    rows = place(dipole_frac, SOURCE_RADIUS) + [moment, jnp.zeros((4, size), jnp.float32)]
     filled = jnp.concatenate(rows, 0)
     package[:, slots:] = filled
     dipoles[...] = filled
@@ -256,9 +246,9 @@
                 pull = right[span, :]
                 for c in range(3):
                     value = kept[0, c, span, over]
-                    scaled = (jnp.broadcast_to(scale[c][:1, over], (LANES, LANES)) * value).astype(jnp.bfloat16)
+                    scaled = (jnp.concatenate([scale[c][:, over]] * (LANES // ROWS), axis=0) * value).astype(jnp.bfloat16)
                     weighted[c * CHUNK + lane : c * CHUNK + lane + LANES, span] = scaled.T
-                    pull = pull + jnp.broadcast_to(force[c][:1, over], (LANES, LANES)) * value
+                    pull = pull + jnp.concatenate([force[c][:, over]] * (LANES // ROWS), axis=0) * value
                 right[span, :] = pull
 
     last = items[0, total - 1]
@@ -363,24 +353,20 @@
     lon_tiles = lax.axis_size("lon")
     size = dipole_frac.shape[3]
     slots = obs_frac.shape[3]
+    observed = jnp.concatenate([obs_frac[0, 0], obs_field[0, 0], jnp.zeros((3, slots), jnp.float32)], 0)
+    drawn = jnp.concatenate([dipole_frac[0, 0], dipole_moment[0], jnp.zeros((5, size), jnp.float32)], 0)
+    raw = jnp.concatenate([observed, drawn], 1)
     package, dipoles = pl.pallas_call(
         functools.partial(pack_kernel, lat_tiles=lat_tiles, lon_tiles=lon_tiles),
         out_shape=(
             jax.ShapeDtypeStruct((8, slots + size), jnp.float32),
             jax.ShapeDtypeStruct((8, size), jnp.float32),
         ),
-        in_specs=[pl.BlockSpec(memory_space=pltpu.HBM)] * 4 + [pl.BlockSpec(memory_space=pltpu.SMEM)],
+        in_specs=[pl.BlockSpec(memory_space=pltpu.VMEM), pl.BlockSpec(memory_space=pltpu.SMEM)],
         out_specs=(pl.BlockSpec(memory_space=pltpu.VMEM), pl.BlockSpec(memory_space=pltpu.VMEM)),
-        scratch_shapes=[
-            pltpu.VMEM((2, slots), jnp.float32),
-            pltpu.VMEM((3, slots), jnp.float32),
-            pltpu.VMEM((2, size), jnp.float32),
-            pltpu.VMEM((1, size), jnp.float32),
-            pltpu.SemaphoreType.DMA((4,)),
-        ],
         compiler_params=pltpu.CompilerParams(vmem_limit_bytes=4 * 1024 * 1024),
         name="pack_tile",
-    )(obs_frac[0, 0], obs_field[0, 0], dipole_frac[0, 0], dipole_moment[0], obs_count)
+    )(raw, obs_count)
     north = cycled(package, "lat", 1)
     south = cycled(package, "lat", -1)
     far_west = cycled(dipoles, "lon", 2)

time: 45.7 us -> 44.2 us (0.967)
  local copies, waits for them, and re-layouts: 2.78 us -> 0.73 us
  other arithmetic: 0.01 us -> 0.76 us
    unnamed x7 -> x1, local copies, waits for them, and re-layouts: 2.77 us -> 0.71 us
    concatenate x0 -> x1, other arithmetic: none -> 0.75 us  [shards(): raw = jnp.concatenate([observed, drawn], 1)]
  transfers between devices with their start and end apart: 7 -> 7, of which waited for: 1 -> 1; matrix products, arithmetic and copies ran while one was open for 0% -> 0% of each run, Pallas kernels for 17% -> 18%
where the time goes in v7:
time: 44.2 us; the launch traced here: 44 us
  Pallas kernels  28 us (63%)
  starting transfers between devices  9.33 us (21%)
  waiting for transfers between devices  3.83 us (9%)
  between operations  1.37 us (3%)
  other arithmetic  0.76 us (2%)
  local copies, waits for them, and re-layouts  0.73 us (2%)
    pallas_call x2, Pallas kernels, shards(): pl.pallas_call(functools.partial(row_kernel, lat_tiles=lat_tiles, opening...  27.7 us
    ppermute x7, starting transfers between devices, cycled(): lax.ppermute(value, axis, [(i, (i + steps) % count) for i in range(count)])  9.33 us
    ppermute x7, waiting for transfers between devices, cycled(): lax.ppermute(value, axis, [(i, (i + steps) % count) for i in range(count)])  3.83 us
  transfers between devices with their start and end apart: 7, of which 1 were waited for; matrix products, arithmetic and copies ran while one was open for 0% of the time, Pallas kernels for 18%

profile of v7, /device:TPU:0, one launch (start us, length us, event | category | flops | bytes accessed | tf_op | source)
XLA Modules:
  0.0 44.0 jit_solution(8264614811087958440)
XLA Ops:
  1.3 0.7 %copy.9 = f32[1,1,3,1024]{3,2,1,0:T(4,128)S(1)} copy(f32[1,1,3,1024]{3,1,2,0:T(1,128)} %param.6) | data formatting | bytes 24576
  2.0 0.8 %maximum_maximum_fusion.raw = f32[8,1280]{1,0:T(8,128)S(1)} fusion(f32[5,256]{1,0:T(8,128)S(1)} %broadcast_in_dim.13, f32[1,256]{1,0:T(1,128)} %bitcast.11, f32[2,256]{1,0:T(2,128)} %bitcast.10, f32[3,1024]{1,0:T(4,128)S(1)} %broadcast_in_dim.12, f32[3,1024]{1,0:T(4,128)S(1)} %bitcast.8, f32[2,1024]{1,0:T(2,128)} %bitcast.9), kind=kLoop, calls=%fused_computation | loop fusion | flops 51200 | bytes 81920 | tf_op jit(solution)/shard_map/concatenate | solution.py:358
  2.8 0.2 pack_tile.1
  3.0 5.1 %collective-permute-start.4 = (f32[8,1280]{1,0:T(8,128)S(1)}, f32[8,1280]{1,0:T(8,128)S(1)}, u32[]{:S(2)}, u32[]{:S(2)}) collective-permute-start(f32[8,1280]{1,0:T(8,128)S(1)} %get-tuple-element.14.refs_0_), channel_id=1, source_target_pairs={{0,3},{1,0},{2,1},{3,2},{4,7},{5,4},{6,5},{7,6},{8,11},{9,8},{10,9... | collective-permute-start | bytes 122888 | tf_op jit(solution)/shard_map/ppermute | solution.py:41
  8.1 0.0 collective-permute-start.3
  8.1 1.6 %collective-permute-start.1 = (f32[8,1280]{1,0:T(8,128)S(1)}, f32[8,1280]{1,0:T(8,128)S(1)}, u32[]{:S(2)}, u32[]{:S(2)}) collective-permute-start(f32[8,1280]{1,0:T(8,128)S(1)} %get-tuple-element.14.refs_0_), channel_id=1, source_target_pairs={{0,28},{4,0},{8,4},{12,8},{16,12},{20,16},{24,20},{28,24},{1,29},{... | collective-permute-start | bytes 122888 | tf_op jit(solution)/shard_map/ppermute | solution.py:41
  9.7 0.0 collective-permute-start
  9.7 0.7 %collective-permute-start.2 = (f32[8,256]{1,0:T(8,128)S(1)}, f32[8,256]{1,0:T(8,128)S(1)}, u32[]{:S(2)}, u32[]{:S(2)}) collective-permute-start(f32[8,256]{1,0:T(8,128)S(1)} %get-tuple-element.15), channel_id=1, source_target_pairs={{0,2},{1,3},{2,0},{3,1},{4,6},{5,7},{6,4},{7,5},{8,10},{9,11},{10,... | collective-permute-start | bytes 24584 | tf_op jit(solution)/shard_map/ppermute | solution.py:41
  10.4 3.8 %collective-permute-done.2.refs_7_.refs_8_ = f32[8,256]{1,0:T(8,128)S(1)} collective-permute-done((f32[8,256]{1,0:T(8,128)S(1)}, f32[8,256]{1,0:T(8,128)S(1)}, u32[]{:S(2)}, u32[]{:S(2)}) %collective-permute-start.2) | collective-permute-done | bytes 8224 | tf_op jit(solution)/shard_map/ppermute | solution.py:41
  14.3 0.0 collective-permute-done.4.refs_4_
  14.3 0.0 collective-permute-done.3.refs_3_
  14.3 0.0 collective-permute-done.1.refs_2_
  14.3 0.0 collective-permute-done.refs_1_
  14.3 1.9 %collective-permute-start.6 = (f32[8,768]{1,0:T(8,128)S(1)}, f32[8,768]{1,0:T(8,128)S(1)}, u32[]{:S(2)}, u32[]{:S(2)}) collective-permute-start(f32[8,768]{1,0:T(8,128)S(1)} %get-tuple-element.26), channel_id=1, source_target_pairs={{0,28},{4,0},{8,4},{12,8},{16,12},{20,16},{24,20},{28,24},{1,29},{... | collective-permute-start | bytes 73736 | tf_op jit(solution)/shard_map/ppermute | solution.py:41
  16.2 0.0 collective-permute-start.5
  16.2 7.7 %own_rows.1 = (f32[6,256,256]{2,1,0:T(8,128)S(1)}, f32[256,128]{1,0:T(8,128)S(1)}) custom-call(f32[8,1280]{1,0:T(8,128)S(1)} %get-tuple-element.14.refs_0_, f32[8,1280]{1,0:T(8,128)S(1)} %collective-permute-done.refs_1_, f32[8,1280]{1,0:T(8,128)S(1)} %collective-permute-done.1.refs_2_, f32[8,1280]{1,0:T(8,128)S(1)} %collective-permute-done.3.refs_3_, ...), custom_call_target="tpu_custom_call" | custom-call | flops 2013265920 | bytes 2097152 | tf_op jit(solution)/shard_map/own_rows/pallas_call | solution.py:403
  23.9 0.0 collective-permute-done.6.refs_6_
  24.0 0.0 collective-permute-done.5.refs_5_
  24.0 20.0 %row_blocks.1 = (f32[13,256,256]{2,1,0:T(8,128)}, f32[1,256]{1,0:T(1,128)}) custom-call(f32[8,1280]{1,0:T(8,128)S(1)} %get-tuple-element.14.refs_0_, f32[8,1280]{1,0:T(8,128)S(1)} %collective-permute-done.refs_1_, f32[8,1280]{1,0:T(8,128)S(1)} %collective-permute-done.1.refs_2_, f32[8,1280]{1,0:T(8,128)S(1)} %collective-permute-done.3.refs_3_, ...), custom_call_target="tpu_custom_call" | custom-call | flops 8053063680 | bytes 4194304 | tf_op jit(solution)/shard_map/row_blocks/pallas_call | solution.py:416
  (7 shorter events, 0.0 us)
Async XLA Ops:
  3.0 11.3 %collective-permute-start.4 = (f32[8,1280]{1,0:T(8,128)S(1)}, f32[8,1280]{1,0:T(8,128)S(1)}, u32[]{:S(2)}, u32[]{:S(2)}) collective-permute-start(f32[8,1280]{1,0:T(8,128)S(1)} %get-tuple-element.14.refs_0_), channel_id=1, source_target_pairs={{0,3},{1,0},{2,1},{3,2},{4,7},{5,4},{6,5},{7,6},{8,11},{9,8},{10,9... | collective-permute-start | bytes 122888 | tf_op jit(solution)/shard_map/ppermute | solution.py:41
  8.1 6.2 %collective-permute-start.3 = (f32[8,1280]{1,0:T(8,128)S(1)}, f32[8,1280]{1,0:T(8,128)S(1)}, u32[]{:S(2)}, u32[]{:S(2)}) collective-permute-start(f32[8,1280]{1,0:T(8,128)S(1)} %get-tuple-element.14.refs_0_), channel_id=1, source_target_pairs={{0,1},{1,2},{2,3},{3,0},{4,5},{5,6},{6,7},{7,4},{8,9},{9,10},{10,1... | collective-permute-start | bytes 122888 | tf_op jit(solution)/shard_map/ppermute | solution.py:41
  8.1 6.2 %collective-permute-start.1 = (f32[8,1280]{1,0:T(8,128)S(1)}, f32[8,1280]{1,0:T(8,128)S(1)}, u32[]{:S(2)}, u32[]{:S(2)}) collective-permute-start(f32[8,1280]{1,0:T(8,128)S(1)} %get-tuple-element.14.refs_0_), channel_id=1, source_target_pairs={{0,28},{4,0},{8,4},{12,8},{16,12},{20,16},{24,20},{28,24},{1,29},{... | collective-permute-start | bytes 122888 | tf_op jit(solution)/shard_map/ppermute | solution.py:41
  9.7 4.6 %collective-permute-start = (f32[8,1280]{1,0:T(8,128)S(1)}, f32[8,1280]{1,0:T(8,128)S(1)}, u32[]{:S(2)}, u32[]{:S(2)}) collective-permute-start(f32[8,1280]{1,0:T(8,128)S(1)} %get-tuple-element.14.refs_0_), channel_id=1, source_target_pairs={{0,4},{4,8},{8,12},{12,16},{16,20},{20,24},{24,28},{28,0},{1,5},{5... | collective-permute-start | bytes 122888 | tf_op jit(solution)/shard_map/ppermute | solution.py:41
  9.7 4.5 %collective-permute-start.2 = (f32[8,256]{1,0:T(8,128)S(1)}, f32[8,256]{1,0:T(8,128)S(1)}, u32[]{:S(2)}, u32[]{:S(2)}) collective-permute-start(f32[8,256]{1,0:T(8,128)S(1)} %get-tuple-element.15), channel_id=1, source_target_pairs={{0,2},{1,3},{2,0},{3,1},{4,6},{5,7},{6,4},{7,5},{8,10},{9,11},{10,... | collective-permute-start | bytes 24584 | tf_op jit(solution)/shard_map/ppermute | solution.py:41
  14.3 9.6 %collective-permute-start.6 = (f32[8,768]{1,0:T(8,128)S(1)}, f32[8,768]{1,0:T(8,128)S(1)}, u32[]{:S(2)}, u32[]{:S(2)}) collective-permute-start(f32[8,768]{1,0:T(8,128)S(1)} %get-tuple-element.26), channel_id=1, source_target_pairs={{0,28},{4,0},{8,4},{12,8},{16,12},{20,16},{24,20},{28,24},{1,29},{... | collective-permute-start | bytes 73736 | tf_op jit(solution)/shard_map/ppermute | solution.py:41
  16.2 7.8 %collective-permute-start.5 = (f32[8,768]{1,0:T(8,128)S(1)}, f32[8,768]{1,0:T(8,128)S(1)}, u32[]{:S(2)}, u32[]{:S(2)}) collective-permute-start(f32[8,768]{1,0:T(8,128)S(1)} %get-tuple-element.27), channel_id=1, source_target_pairs={{0,4},{4,8},{8,12},{12,16},{16,20},{20,24},{24,28},{28,0},{1,5},{5... | collective-permute-start | bytes 73736 | tf_op jit(solution)/shard_map/ppermute | solution.py:41

commit v8 on v7

--- a/solution.py
+++ b/solution.py
@@ -31,6 +31,7 @@
 DEGREE = math.pi / 180.0
 CHUNK = 512
 ROWS = 16
+WIDTH = 256
 LANES = 128
 DEPTH = 64
 STRETCH = KERNEL_SCALE ** (-2.0 / 3.0)
@@ -84,12 +85,13 @@
     refs = list(refs)
     own_ref, north_ref, south_ref, west_ref, east_ref = refs[:5]
     if opening:
-        gram, right = refs[5:7]
-        rest = refs[7:]
+        gram, right, column, tall = refs[5:9]
+        rest = refs[9:10] + [column, tall] + refs[10:]
         tiles, targets = (0,), range(len(CROSS))
     else:
-        far_north_ref, far_south_ref, far_west_ref, far_east_ref, gram_in, right_in, gram_ref, rhs_ref = refs[5:13]
-        rest = refs[13:]
+        far_north_ref, far_south_ref, far_west_ref, far_east_ref = refs[5:9]
+        gram_in, right_in, column_in, tall_in, gram_ref, rhs_ref = refs[9:15]
+        rest = refs[15:]
         tiles, targets = (3, 4, 1, 2), range(len(OFFSETS))
     (
         obs,
@@ -138,6 +140,11 @@
     row_of = lax.broadcasted_iota(jnp.int32, (8, size), 0)
     right[...] = jnp.zeros_like(right) if opening else right_in[...]
     for target in targets:
+        if not opening and target < len(CROSS):
+            gram[target] = gram_in[target]
+            column[target] = column_in[target]
+            tall[target] = tall_in[target]
+            continue
         offset = OFFSETS[target]
         ref, start = sources[offset]
         values = ref[:, start : start + size]
@@ -147,8 +154,7 @@
         ones = jnp.ones_like(values)
         stacked = jnp.concatenate([high, high, middle, high, low, middle, ones, jnp.zeros_like(values)], 0)
         upright = stacked.T.astype(jnp.bfloat16)
-        fresh = opening or target >= len(CROSS)
-        gram[target] = jnp.zeros((size, size), jnp.float32) if fresh else gram_in[target]
+        gram[target] = jnp.zeros((size, size), jnp.float32)
         tall[target] = upright
         wide = lax.dot_general(upright, picks, (((1,), (0,)), ((), ())), preferred_element_type=jnp.float32)
         for part in range(4):
@@ -200,26 +206,28 @@
     def evaluate(tile, chunk, at, held, apart):
         target = table[tile, at]
         spare = (at != 0).astype(jnp.int32)
-        point = [jnp.broadcast_to(obs[chunk, c : c + 1, :], (ROWS, CHUNK)) for c in range(3)]
-        sums = [predicted[c] for c in range(3)]
         near = 1.5 * (OBS_RADIUS * OBS_RADIUS - SOURCE_RADIUS * SOURCE_RADIUS) * STRETCH
-        for start in range(0, size, ROWS):
-            span = slice(start, start + ROWS)
-            wide = [jnp.concatenate([column[target, part, span, :]] * (CHUNK // LANES), axis=1) for part in range(4)]
-            inverse = lax.rsqrt(apart[at, span, :])
-            inverse_square = inverse * inverse
-            cube = inverse_square * inverse
-            along = cube * (near * inverse_square - 1.5)
-            across = along + cube
+        for left in range(0, CHUNK, WIDTH):
+            over = slice(left, left + WIDTH)
+            point = [jnp.broadcast_to(obs[chunk, c : c + 1, over], (ROWS, WIDTH)) for c in range(3)]
+            sums = [predicted[c, :, over] for c in range(3)]
+            for start in range(0, size, ROWS):
+                span = slice(start, start + ROWS)
+                wide = [jnp.concatenate([column[target, part, span, :]] * (WIDTH // LANES), axis=1) for part in range(4)]
+                inverse = lax.rsqrt(apart[at, span, over])
+                inverse_square = inverse * inverse
+                cube = inverse_square * inverse
+                along = cube * (near * inverse_square - 1.5)
+                across = along + cube
+                for c in range(3):
+                    value = along * point[c] - across * wide[c]
+                    held[at, span, c * CHUNK + left : c * CHUNK + left + WIDTH] = value.astype(jnp.bfloat16)
+                    kept[spare, c, span, over] = value
+                    part = value * wide[3]
+                    for sub in range(0, ROWS, 8):
+                        sums[c] = sums[c] + part[sub : sub + 8]
             for c in range(3):
-                value = along * point[c] - across * wide[c]
-                held[at, span, c * CHUNK : (c + 1) * CHUNK] = value.astype(jnp.bfloat16)
-                kept[spare, c, span, :] = value
-                part = value * wide[3]
-                for sub in range(0, ROWS, 8):
-                    sums[c] = sums[c] + part[sub : sub + 8]
-        for c in range(3):
-            predicted[c] = sums[c]
+                predicted[c, :, over] = sums[c]
 
     def multiply(target, at, held, weighted):
         for half in (slice(0, size // 2), slice(size // 2, size)):
@@ -323,12 +331,15 @@
 
     def drain(held, weighted):
         def block(at, carry):
+            if not opening:
+                flush(table[last, at - 1])
             multiply(table[last, at], at, held, weighted)
-            if not opening:
-                flush(table[last, at])
             return carry
 
-        lax.fori_loop(0, members[last], block, 0)
+        multiply(table[last, 0], 0, held, weighted)
+        lax.fori_loop(1, members[last], block, 0)
+        if not opening:
+            flush(table[last, members[last] - 1])
 
     @pl.when(odd)
     def _():
@@ -379,11 +390,10 @@
     chunks = slots // CHUNK
     vmem = pl.BlockSpec(memory_space=pltpu.VMEM)
 
-    def working(targets):
+    def working(*dipole_room):
         return [
             pltpu.VMEM((5 * chunks, 8, CHUNK), jnp.float32),
-            pltpu.VMEM((targets, 4, size, LANES), jnp.float32),
-            pltpu.VMEM((targets, size, DEPTH), jnp.bfloat16),
+            *dipole_room,
             pltpu.VMEM((5 * chunks, DEPTH, CHUNK), jnp.bfloat16),
             pltpu.VMEM((5, size, 3 * CHUNK), jnp.bfloat16),
             pltpu.VMEM((5, size, 3 * CHUNK), jnp.bfloat16),
@@ -400,15 +410,17 @@
         ]
 
     products = 2 * 3 * slots * size * size
-    own_gram, own_right = pl.pallas_call(
+    handed = pl.pallas_call(
         functools.partial(row_kernel, lat_tiles=lat_tiles, opening=True),
         out_shape=(
             jax.ShapeDtypeStruct((len(CROSS) + 1, size, size), jnp.float32),
             jax.ShapeDtypeStruct((size, LANES), jnp.float32),
+            jax.ShapeDtypeStruct((len(CROSS), 4, size, LANES), jnp.float32),
+            jax.ShapeDtypeStruct((len(CROSS), size, DEPTH), jnp.bfloat16),
         ),
         in_specs=[vmem] * 5,
-        out_specs=(vmem, vmem),
-        scratch_shapes=working(len(CROSS)),
+        out_specs=(vmem,) * 4,
+        scratch_shapes=working(),
         compiler_params=pltpu.CompilerParams(vmem_limit_bytes=26 * 1024 * 1024),
         cost_estimate=pl.CostEstimate(flops=5 * products, bytes_accessed=8 * size * size * 4, transcendentals=0),
         name="own_rows",
@@ -419,9 +431,12 @@
             jax.ShapeDtypeStruct((len(OFFSETS), size, size), jnp.float32),
             jax.ShapeDtypeStruct((1, size), jnp.float32),
         ),
-        in_specs=[vmem] * 11,
+        in_specs=[vmem] * 13,
         out_specs=(pl.BlockSpec(memory_space=pl.ANY), vmem),
-        scratch_shapes=working(len(OFFSETS))
+        scratch_shapes=working(
+            pltpu.VMEM((len(OFFSETS), 4, size, LANES), jnp.float32),
+            pltpu.VMEM((len(OFFSETS), size, DEPTH), jnp.bfloat16),
+        )
         + [
             pltpu.VMEM((size, LANES), jnp.float32),
             pltpu.SMEM((len(OFFSETS),), jnp.int32),
@@ -431,7 +446,7 @@
         compiler_params=pltpu.CompilerParams(vmem_limit_bytes=44 * 1024 * 1024),
         cost_estimate=pl.CostEstimate(flops=20 * products, bytes_accessed=16 * size * size * 4, transcendentals=0),
         name="row_blocks",
-    )(package, north, south, west, east, far_north, far_south, far_west, far_east, own_gram, own_right)
+    )(package, north, south, west, east, far_north, far_south, far_west, far_east, *handed)
     return (gram[None, None], rhs[None])
 
 

time: 44.2 us -> 43.3 us (0.980)
  Pallas kernels: 28 us -> 27.1 us
    pallas_call x2, Pallas kernels: 27.7 us -> 26.8 us  [shards(): pl.pallas_call(functools.partial(row_kernel, lat_tiles=lat_tiles, opening...]
where the time goes in v8:
time: 43.3 us; the launch traced here: 43.1 us
  Pallas kernels  27.1 us (63%)
  starting transfers between devices  9.33 us (22%)
  waiting for transfers between devices  3.83 us (9%)
  between operations  1.37 us (3%)
  other arithmetic  0.76 us (2%)
  local copies, waits for them, and re-layouts  0.73 us (2%)
    pallas_call x2, Pallas kernels, shards(): pl.pallas_call(functools.partial(row_kernel, lat_tiles=lat_tiles, opening...  26.8 us
    ppermute x7, starting transfers between devices, cycled(): lax.ppermute(value, axis, [(i, (i + steps) % count) for i in range(count)])  9.33 us
    ppermute x7, waiting for transfers between devices, cycled(): lax.ppermute(value, axis, [(i, (i + steps) % count) for i in range(count)])  3.83 us
  transfers between devices with their start and end apart: 7, of which 1 were waited for; matrix products, arithmetic and copies ran while one was open for 0% of the time, Pallas kernels for 18%

profile of v8, /device:TPU:0, one launch (start us, length us, event | category | flops | bytes accessed | tf_op | source)
XLA Modules:
  0.0 43.1 jit_solution(5107802016851513818)
XLA Ops:
  1.3 0.7 %copy.9 = f32[1,1,3,1024]{3,2,1,0:T(4,128)S(1)} copy(f32[1,1,3,1024]{3,1,2,0:T(1,128)} %param.6) | data formatting | bytes 24576
  2.0 0.8 %maximum_maximum_fusion.raw = f32[8,1280]{1,0:T(8,128)S(1)} fusion(f32[5,256]{1,0:T(8,128)S(1)} %broadcast_in_dim.13, f32[1,256]{1,0:T(1,128)} %bitcast.11, f32[2,256]{1,0:T(2,128)} %bitcast.10, f32[3,1024]{1,0:T(4,128)S(1)} %broadcast_in_dim.12, f32[3,1024]{1,0:T(4,128)S(1)} %bitcast.8, f32[2,1024]{1,0:T(2,128)} %bitcast.9), kind=kLoop, calls=%fused_computation | loop fusion | flops 51200 | bytes 81920 | tf_op jit(solution)/shard_map/concatenate | solution.py:369
  2.8 0.2 pack_tile.1
  3.0 5.1 %collective-permute-start.4 = (f32[8,1280]{1,0:T(8,128)S(1)}, f32[8,1280]{1,0:T(8,128)S(1)}, u32[]{:S(2)}, u32[]{:S(2)}) collective-permute-start(f32[8,1280]{1,0:T(8,128)S(1)} %get-tuple-element.16.refs_0_), channel_id=1, source_target_pairs={{0,3},{1,0},{2,1},{3,2},{4,7},{5,4},{6,5},{7,6},{8,11},{9,8},{10,9... | collective-permute-start | bytes 122888 | tf_op jit(solution)/shard_map/ppermute | solution.py:42
  8.1 0.0 collective-permute-start.3
  8.1 1.6 %collective-permute-start.1 = (f32[8,1280]{1,0:T(8,128)S(1)}, f32[8,1280]{1,0:T(8,128)S(1)}, u32[]{:S(2)}, u32[]{:S(2)}) collective-permute-start(f32[8,1280]{1,0:T(8,128)S(1)} %get-tuple-element.16.refs_0_), channel_id=1, source_target_pairs={{0,28},{4,0},{8,4},{12,8},{16,12},{20,16},{24,20},{28,24},{1,29},{... | collective-permute-start | bytes 122888 | tf_op jit(solution)/shard_map/ppermute | solution.py:42
  9.7 0.0 collective-permute-start
  9.7 0.7 %collective-permute-start.2 = (f32[8,256]{1,0:T(8,128)S(1)}, f32[8,256]{1,0:T(8,128)S(1)}, u32[]{:S(2)}, u32[]{:S(2)}) collective-permute-start(f32[8,256]{1,0:T(8,128)S(1)} %get-tuple-element.17), channel_id=1, source_target_pairs={{0,2},{1,3},{2,0},{3,1},{4,6},{5,7},{6,4},{7,5},{8,10},{9,11},{10,... | collective-permute-start | bytes 24584 | tf_op jit(solution)/shard_map/ppermute | solution.py:42
  10.4 3.8 %collective-permute-done.2.refs_7_.refs_8_ = f32[8,256]{1,0:T(8,128)S(1)} collective-permute-done((f32[8,256]{1,0:T(8,128)S(1)}, f32[8,256]{1,0:T(8,128)S(1)}, u32[]{:S(2)}, u32[]{:S(2)}) %collective-permute-start.2) | collective-permute-done | bytes 8224 | tf_op jit(solution)/shard_map/ppermute | solution.py:42
  14.3 0.0 collective-permute-done.4.refs_4_
  14.3 0.0 collective-permute-done.3.refs_3_
  14.3 0.0 collective-permute-done.1.refs_2_
  14.3 0.0 collective-permute-done.refs_1_
  14.3 1.9 %collective-permute-start.6 = (f32[8,768]{1,0:T(8,128)S(1)}, f32[8,768]{1,0:T(8,128)S(1)}, u32[]{:S(2)}, u32[]{:S(2)}) collective-permute-start(f32[8,768]{1,0:T(8,128)S(1)} %get-tuple-element.30), channel_id=1, source_target_pairs={{0,28},{4,0},{8,4},{12,8},{16,12},{20,16},{24,20},{28,24},{1,29},{... | collective-permute-start | bytes 73736 | tf_op jit(solution)/shard_map/ppermute | solution.py:42
  16.2 0.0 collective-permute-start.5
  16.2 7.6 %own_rows.1 = (f32[6,256,256]{2,1,0:T(8,128)S(1)}, f32[256,128]{1,0:T(8,128)S(1)}, f32[5,4,256,128]{3,2,1,0:T(8,128)S(1)}, bf16[5,256,64]{2,1,0:T(8,128)(2,1)S(1)}) custom-call(f32[8,1280]{1,0:T(8,128)S(1)} %get-tuple-element.16.refs_0_, f32[8,1280]{1,0:T(8,128)S(1)} %collective-permute-done.refs_1_, f32[8,1280]{1,0:T(8,128)S(1)} %collective-permute-done.1.refs_2_, ...), custom_call_target="tpu_custom_call" | custom-call | flops 2013265920 | bytes 2097152 | tf_op jit(solution)/shard_map/own_rows/pallas_call | solution.py:413
  23.9 0.0 collective-permute-done.6.refs_6_
  23.9 0.0 collective-permute-done.5.refs_5_
  23.9 19.2 %row_blocks.1 = (f32[13,256,256]{2,1,0:T(8,128)}, f32[1,256]{1,0:T(1,128)}) custom-call(f32[8,1280]{1,0:T(8,128)S(1)} %get-tuple-element.16.refs_0_, f32[8,1280]{1,0:T(8,128)S(1)} %collective-permute-done.refs_1_, f32[8,1280]{1,0:T(8,128)S(1)} %collective-permute-done.1.refs_2_, f32[8,1280]{1,0:T(8,128)S(1)} %collective-permute-done.3.refs_3_, ...), custom_call_target="tpu_custom_call" | custom-call | flops 8053063680 | bytes 4194304 | tf_op jit(solution)/shard_map/row_blocks/pallas_call | solution.py:428
  (7 shorter events, 0.0 us)
Async XLA Ops:
  3.0 11.3 %collective-permute-start.4 = (f32[8,1280]{1,0:T(8,128)S(1)}, f32[8,1280]{1,0:T(8,128)S(1)}, u32[]{:S(2)}, u32[]{:S(2)}) collective-permute-start(f32[8,1280]{1,0:T(8,128)S(1)} %get-tuple-element.16.refs_0_), channel_id=1, source_target_pairs={{0,3},{1,0},{2,1},{3,2},{4,7},{5,4},{6,5},{7,6},{8,11},{9,8},{10,9... | collective-permute-start | bytes 122888 | tf_op jit(solution)/shard_map/ppermute | solution.py:42
  8.1 6.2 %collective-permute-start.3 = (f32[8,1280]{1,0:T(8,128)S(1)}, f32[8,1280]{1,0:T(8,128)S(1)}, u32[]{:S(2)}, u32[]{:S(2)}) collective-permute-start(f32[8,1280]{1,0:T(8,128)S(1)} %get-tuple-element.16.refs_0_), channel_id=1, source_target_pairs={{0,1},{1,2},{2,3},{3,0},{4,5},{5,6},{6,7},{7,4},{8,9},{9,10},{10,1... | collective-permute-start | bytes 122888 | tf_op jit(solution)/shard_map/ppermute | solution.py:42
  8.1 6.2 %collective-permute-start.1 = (f32[8,1280]{1,0:T(8,128)S(1)}, f32[8,1280]{1,0:T(8,128)S(1)}, u32[]{:S(2)}, u32[]{:S(2)}) collective-permute-start(f32[8,1280]{1,0:T(8,128)S(1)} %get-tuple-element.16.refs_0_), channel_id=1, source_target_pairs={{0,28},{4,0},{8,4},{12,8},{16,12},{20,16},{24,20},{28,24},{1,29},{... | collective-permute-start | bytes 122888 | tf_op jit(solution)/shard_map/ppermute | solution.py:42
  9.7 4.6 %collective-permute-start = (f32[8,1280]{1,0:T(8,128)S(1)}, f32[8,1280]{1,0:T(8,128)S(1)}, u32[]{:S(2)}, u32[]{:S(2)}) collective-permute-start(f32[8,1280]{1,0:T(8,128)S(1)} %get-tuple-element.16.refs_0_), channel_id=1, source_target_pairs={{0,4},{4,8},{8,12},{12,16},{16,20},{20,24},{24,28},{28,0},{1,5},{5... | collective-permute-start | bytes 122888 | tf_op jit(solution)/shard_map/ppermute | solution.py:42
  9.7 4.5 %collective-permute-start.2 = (f32[8,256]{1,0:T(8,128)S(1)}, f32[8,256]{1,0:T(8,128)S(1)}, u32[]{:S(2)}, u32[]{:S(2)}) collective-permute-start(f32[8,256]{1,0:T(8,128)S(1)} %get-tuple-element.17), channel_id=1, source_target_pairs={{0,2},{1,3},{2,0},{3,1},{4,6},{5,7},{6,4},{7,5},{8,10},{9,11},{10,... | collective-permute-start | bytes 24584 | tf_op jit(solution)/shard_map/ppermute | solution.py:42
  14.3 9.5 %collective-permute-start.6 = (f32[8,768]{1,0:T(8,128)S(1)}, f32[8,768]{1,0:T(8,128)S(1)}, u32[]{:S(2)}, u32[]{:S(2)}) collective-permute-start(f32[8,768]{1,0:T(8,128)S(1)} %get-tuple-element.30), channel_id=1, source_target_pairs={{0,28},{4,0},{8,4},{12,8},{16,12},{20,16},{24,20},{28,24},{1,29},{... | collective-permute-start | bytes 73736 | tf_op jit(solution)/shard_map/ppermute | solution.py:42
  16.2 7.7 %collective-permute-start.5 = (f32[8,768]{1,0:T(8,128)S(1)}, f32[8,768]{1,0:T(8,128)S(1)}, u32[]{:S(2)}, u32[]{:S(2)}) collective-permute-start(f32[8,768]{1,0:T(8,128)S(1)} %get-tuple-element.31), channel_id=1, source_target_pairs={{0,4},{4,8},{8,12},{12,16},{16,20},{20,24},{24,28},{28,0},{1,5},{5... | collective-permute-start | bytes 73736 | tf_op jit(solution)/shard_map/ppermute | solution.py:42

commit v9 on v8

--- a/solution.py
+++ b/solution.py
@@ -34,7 +34,8 @@
 WIDTH = 256
 LANES = 128
 DEPTH = 64
-STRETCH = KERNEL_SCALE ** (-2.0 / 3.0)
+STRETCH = 1.0 / (1.5 * (OBS_RADIUS * OBS_RADIUS - SOURCE_RADIUS * SOURCE_RADIUS))
+SHRINK = KERNEL_SCALE * STRETCH**1.5
 
 
 def cycled(value, axis, steps):
@@ -121,7 +122,9 @@
     arrived = (own_ref, north_ref, south_ref, west_ref, east_ref)
     for tile in tiles:
         for chunk in range(chunks):
-            obs[tile * chunks + chunk] = arrived[tile][:, chunk * CHUNK : (chunk + 1) * CHUNK]
+            seen = arrived[tile][:, chunk * CHUNK : (chunk + 1) * CHUNK]
+            place = lax.broadcasted_iota(jnp.int32, seen.shape, 0)
+            obs[tile * chunks + chunk] = jnp.where(place < 3, seen * SHRINK, seen)
     sources = {offset: (ref, slots) for offset, ref in zip(CROSS, arrived)}
     if not opening:
         for at, offset in enumerate(((-2, 0), (-1, -1), (-1, 1))):
@@ -148,6 +151,7 @@
         offset = OFFSETS[target]
         ref, start = sources[offset]
         values = ref[:, start : start + size]
+        values = jnp.where(row_of < 3, values * SHRINK, values)
         if offset[0] != 0:
             values = jnp.where((row_of < 3) | inside(offset[0]), values, 0.0)
         high, middle, low = split(values)
@@ -162,8 +166,10 @@
 
     row_of = lax.broadcasted_iota(jnp.int32, (8, CHUNK), 0)
     base = STRETCH * (OBS_RADIUS * OBS_RADIUS + SOURCE_RADIUS * SOURCE_RADIUS)
-    for at in [tile * chunks + chunk for tile in tiles for chunk in range(chunks)]:
-        high, middle, low = split(jnp.where(row_of < 3, obs[at] * (-2.0 * STRETCH), 0.0))
+    for tile, chunk in [(tile, chunk) for tile in tiles for chunk in range(chunks)]:
+        at = tile * chunks + chunk
+        seen = arrived[tile][:, chunk * CHUNK : (chunk + 1) * CHUNK]
+        high, middle, low = split(jnp.where(row_of < 3, seen * (-2.0 * STRETCH / SHRINK), 0.0))
         first, second, third = split(jnp.full((8, CHUNK), base, jnp.float32))
         constant = jnp.where(row_of == 0, first, jnp.where(row_of == 1, second, jnp.where(row_of == 2, third, 0.0)))
         stacked = jnp.concatenate([high, middle, high, low, high, middle, constant, jnp.zeros_like(high)], 0)
@@ -206,7 +212,6 @@
     def evaluate(tile, chunk, at, held, apart):
         target = table[tile, at]
         spare = (at != 0).astype(jnp.int32)
-        near = 1.5 * (OBS_RADIUS * OBS_RADIUS - SOURCE_RADIUS * SOURCE_RADIUS) * STRETCH
         for left in range(0, CHUNK, WIDTH):
             over = slice(left, left + WIDTH)
             point = [jnp.broadcast_to(obs[chunk, c : c + 1, over], (ROWS, WIDTH)) for c in range(3)]
@@ -217,7 +222,7 @@
                 inverse = lax.rsqrt(apart[at, span, over])
                 inverse_square = inverse * inverse
                 cube = inverse_square * inverse
-                along = cube * (near * inverse_square - 1.5)
+                along = cube * (inverse_square - 1.5)
                 across = along + cube
                 for c in range(3):
                     value = along * point[c] - across * wide[c]

time: 43.3 us -> 43 us (level)
  no operation moved by 1% of the time
where the time goes in v9:
time: 43 us; the launch traced here: 42.8 us
  Pallas kernels  26.7 us (62%)
  starting transfers between devices  9.33 us (22%)
  waiting for transfers between devices  3.83 us (9%)
  between operations  1.37 us (3%)
  other arithmetic  0.76 us (2%)
  local copies, waits for them, and re-layouts  0.73 us (2%)
    pallas_call x2, Pallas kernels, shards(): pl.pallas_call(functools.partial(row_kernel, lat_tiles=lat_tiles, opening...  26.5 us
    ppermute x7, starting transfers between devices, cycled(): lax.ppermute(value, axis, [(i, (i + steps) % count) for i in range(count)])  9.33 us
    ppermute x7, waiting for transfers between devices, cycled(): lax.ppermute(value, axis, [(i, (i + steps) % count) for i in range(count)])  3.83 us
  transfers between devices with their start and end apart: 7, of which 1 were waited for; matrix products, arithmetic and copies ran while one was open for 0% of the time, Pallas kernels for 18%

profile of v9, /device:TPU:0, one launch (start us, length us, event | category | flops | bytes accessed | tf_op | source)
XLA Modules:
  0.0 42.8 jit_solution(15625441629457257454)
XLA Ops:
  1.3 0.7 %copy.9 = f32[1,1,3,1024]{3,2,1,0:T(4,128)S(1)} copy(f32[1,1,3,1024]{3,1,2,0:T(1,128)} %param.6) | data formatting | bytes 24576
  2.0 0.8 %maximum_maximum_fusion.raw = f32[8,1280]{1,0:T(8,128)S(1)} fusion(f32[5,256]{1,0:T(8,128)S(1)} %broadcast_in_dim.13, f32[1,256]{1,0:T(1,128)} %bitcast.11, f32[2,256]{1,0:T(2,128)} %bitcast.10, f32[3,1024]{1,0:T(4,128)S(1)} %broadcast_in_dim.12, f32[3,1024]{1,0:T(4,128)S(1)} %bitcast.8, f32[2,1024]{1,0:T(2,128)} %bitcast.9), kind=kLoop, calls=%fused_computation | loop fusion | flops 51200 | bytes 81920 | tf_op jit(solution)/shard_map/concatenate | solution.py:374
  2.8 0.2 pack_tile.1
  3.0 5.1 %collective-permute-start.4 = (f32[8,1280]{1,0:T(8,128)S(1)}, f32[8,1280]{1,0:T(8,128)S(1)}, u32[]{:S(2)}, u32[]{:S(2)}) collective-permute-start(f32[8,1280]{1,0:T(8,128)S(1)} %get-tuple-element.16.refs_0_), channel_id=1, source_target_pairs={{0,3},{1,0},{2,1},{3,2},{4,7},{5,4},{6,5},{7,6},{8,11},{9,8},{10,9... | collective-permute-start | bytes 122888 | tf_op jit(solution)/shard_map/ppermute | solution.py:43
  8.1 0.0 collective-permute-start.3
  8.1 1.6 %collective-permute-start.1 = (f32[8,1280]{1,0:T(8,128)S(1)}, f32[8,1280]{1,0:T(8,128)S(1)}, u32[]{:S(2)}, u32[]{:S(2)}) collective-permute-start(f32[8,1280]{1,0:T(8,128)S(1)} %get-tuple-element.16.refs_0_), channel_id=1, source_target_pairs={{0,28},{4,0},{8,4},{12,8},{16,12},{20,16},{24,20},{28,24},{1,29},{... | collective-permute-start | bytes 122888 | tf_op jit(solution)/shard_map/ppermute | solution.py:43
  9.7 0.0 collective-permute-start
  9.7 0.7 %collective-permute-start.2 = (f32[8,256]{1,0:T(8,128)S(1)}, f32[8,256]{1,0:T(8,128)S(1)}, u32[]{:S(2)}, u32[]{:S(2)}) collective-permute-start(f32[8,256]{1,0:T(8,128)S(1)} %get-tuple-element.17), channel_id=1, source_target_pairs={{0,2},{1,3},{2,0},{3,1},{4,6},{5,7},{6,4},{7,5},{8,10},{9,11},{10,... | collective-permute-start | bytes 24584 | tf_op jit(solution)/shard_map/ppermute | solution.py:43
  10.4 3.8 %collective-permute-done.2.refs_7_.refs_8_ = f32[8,256]{1,0:T(8,128)S(1)} collective-permute-done((f32[8,256]{1,0:T(8,128)S(1)}, f32[8,256]{1,0:T(8,128)S(1)}, u32[]{:S(2)}, u32[]{:S(2)}) %collective-permute-start.2) | collective-permute-done | bytes 8224 | tf_op jit(solution)/shard_map/ppermute | solution.py:43
  14.3 0.0 collective-permute-done.4.refs_4_
  14.3 0.0 collective-permute-done.3.refs_3_
  14.3 0.0 collective-permute-done.1.refs_2_
  14.3 0.0 collective-permute-done.refs_1_
  14.3 1.9 %collective-permute-start.6 = (f32[8,768]{1,0:T(8,128)S(1)}, f32[8,768]{1,0:T(8,128)S(1)}, u32[]{:S(2)}, u32[]{:S(2)}) collective-permute-start(f32[8,768]{1,0:T(8,128)S(1)} %get-tuple-element.30), channel_id=1, source_target_pairs={{0,28},{4,0},{8,4},{12,8},{16,12},{20,16},{24,20},{28,24},{1,29},{... | collective-permute-start | bytes 73736 | tf_op jit(solution)/shard_map/ppermute | solution.py:43
  16.2 0.0 collective-permute-start.5
  16.2 7.7 %own_rows.1 = (f32[6,256,256]{2,1,0:T(8,128)S(1)}, f32[256,128]{1,0:T(8,128)S(1)}, f32[5,4,256,128]{3,2,1,0:T(8,128)S(1)}, bf16[5,256,64]{2,1,0:T(8,128)(2,1)S(1)}) custom-call(f32[8,1280]{1,0:T(8,128)S(1)} %get-tuple-element.16.refs_0_, f32[8,1280]{1,0:T(8,128)S(1)} %collective-permute-done.refs_1_, f32[8,1280]{1,0:T(8,128)S(1)} %collective-permute-done.1.refs_2_, ...), custom_call_target="tpu_custom_call" | custom-call | flops 2013265920 | bytes 2097152 | tf_op jit(solution)/shard_map/own_rows/pallas_call | solution.py:418
  23.9 0.0 collective-permute-done.6.refs_6_
  23.9 0.0 collective-permute-done.5.refs_5_
  23.9 18.9 %row_blocks.1 = (f32[13,256,256]{2,1,0:T(8,128)}, f32[1,256]{1,0:T(1,128)}) custom-call(f32[8,1280]{1,0:T(8,128)S(1)} %get-tuple-element.16.refs_0_, f32[8,1280]{1,0:T(8,128)S(1)} %collective-permute-done.refs_1_, f32[8,1280]{1,0:T(8,128)S(1)} %collective-permute-done.1.refs_2_, f32[8,1280]{1,0:T(8,128)S(1)} %collective-permute-done.3.refs_3_, ...), custom_call_target="tpu_custom_call" | custom-call | flops 8053063680 | bytes 4194304 | tf_op jit(solution)/shard_map/row_blocks/pallas_call | solution.py:433
  (7 shorter events, 0.0 us)
Async XLA Ops:
  3.0 11.3 %collective-permute-start.4 = (f32[8,1280]{1,0:T(8,128)S(1)}, f32[8,1280]{1,0:T(8,128)S(1)}, u32[]{:S(2)}, u32[]{:S(2)}) collective-permute-start(f32[8,1280]{1,0:T(8,128)S(1)} %get-tuple-element.16.refs_0_), channel_id=1, source_target_pairs={{0,3},{1,0},{2,1},{3,2},{4,7},{5,4},{6,5},{7,6},{8,11},{9,8},{10,9... | collective-permute-start | bytes 122888 | tf_op jit(solution)/shard_map/ppermute | solution.py:43
  8.1 6.2 %collective-permute-start.3 = (f32[8,1280]{1,0:T(8,128)S(1)}, f32[8,1280]{1,0:T(8,128)S(1)}, u32[]{:S(2)}, u32[]{:S(2)}) collective-permute-start(f32[8,1280]{1,0:T(8,128)S(1)} %get-tuple-element.16.refs_0_), channel_id=1, source_target_pairs={{0,1},{1,2},{2,3},{3,0},{4,5},{5,6},{6,7},{7,4},{8,9},{9,10},{10,1... | collective-permute-start | bytes 122888 | tf_op jit(solution)/shard_map/ppermute | solution.py:43
  8.1 6.2 %collective-permute-start.1 = (f32[8,1280]{1,0:T(8,128)S(1)}, f32[8,1280]{1,0:T(8,128)S(1)}, u32[]{:S(2)}, u32[]{:S(2)}) collective-permute-start(f32[8,1280]{1,0:T(8,128)S(1)} %get-tuple-element.16.refs_0_), channel_id=1, source_target_pairs={{0,28},{4,0},{8,4},{12,8},{16,12},{20,16},{24,20},{28,24},{1,29},{... | collective-permute-start | bytes 122888 | tf_op jit(solution)/shard_map/ppermute | solution.py:43
  9.7 4.6 %collective-permute-start = (f32[8,1280]{1,0:T(8,128)S(1)}, f32[8,1280]{1,0:T(8,128)S(1)}, u32[]{:S(2)}, u32[]{:S(2)}) collective-permute-start(f32[8,1280]{1,0:T(8,128)S(1)} %get-tuple-element.16.refs_0_), channel_id=1, source_target_pairs={{0,4},{4,8},{8,12},{12,16},{16,20},{20,24},{24,28},{28,0},{1,5},{5... | collective-permute-start | bytes 122888 | tf_op jit(solution)/shard_map/ppermute | solution.py:43
  9.7 4.5 %collective-permute-start.2 = (f32[8,256]{1,0:T(8,128)S(1)}, f32[8,256]{1,0:T(8,128)S(1)}, u32[]{:S(2)}, u32[]{:S(2)}) collective-permute-start(f32[8,256]{1,0:T(8,128)S(1)} %get-tuple-element.17), channel_id=1, source_target_pairs={{0,2},{1,3},{2,0},{3,1},{4,6},{5,7},{6,4},{7,5},{8,10},{9,11},{10,... | collective-permute-start | bytes 24584 | tf_op jit(solution)/shard_map/ppermute | solution.py:43
  14.3 9.5 %collective-permute-start.6 = (f32[8,768]{1,0:T(8,128)S(1)}, f32[8,768]{1,0:T(8,128)S(1)}, u32[]{:S(2)}, u32[]{:S(2)}) collective-permute-start(f32[8,768]{1,0:T(8,128)S(1)} %get-tuple-element.30), channel_id=1, source_target_pairs={{0,28},{4,0},{8,4},{12,8},{16,12},{20,16},{24,20},{28,24},{1,29},{... | collective-permute-start | bytes 73736 | tf_op jit(solution)/shard_map/ppermute | solution.py:43
  16.2 7.7 %collective-permute-start.5 = (f32[8,768]{1,0:T(8,128)S(1)}, f32[8,768]{1,0:T(8,128)S(1)}, u32[]{:S(2)}, u32[]{:S(2)}) collective-permute-start(f32[8,768]{1,0:T(8,128)S(1)} %get-tuple-element.31), channel_id=1, source_target_pairs={{0,4},{4,8},{8,12},{12,16},{16,20},{20,24},{24,28},{28,0},{1,5},{5... | collective-permute-start | bytes 73736 | tf_op jit(solution)/shard_map/ppermute | solution.py:43
